TPU v7x, 32 devices: a whole 2x2x4 slice. The times are simulated.
32 devices in a mesh: dp: 8 (over y, x, core), fsdp: 4 (over z).
Axes of the slice: x: 2, y: 2, z: 4, core: 2. Of those that a mesh axis runs over, the one named last changes fastest.
Arguments:
- layer_input: bfloat16 [64, 1024, 768], P(('dp', 'fsdp')), may hold values from -8 to 8
- cotangent: bfloat16 [64, 1024, 768], P(('dp', 'fsdp')), may hold values from -6 to 6
- doc_lengths: int32 [64, 8], P(('dp', 'fsdp')), may hold values from 1 to 512, 1024 in all within a row
- pad_tail: int32 [64], P(('dp', 'fsdp')), may hold values from 0 to 256
- query_weight: bfloat16 [768, 768], P(('dp', 'fsdp')), may hold values from -0.25 to 0.25
- query_bias: bfloat16 [768], P(('dp', 'fsdp')), may hold values from -3 to 3
- key_weight: bfloat16 [768, 768], P(('dp', 'fsdp')), may hold values from -0.25 to 0.25
- value_weight: bfloat16 [768, 768], P(('dp', 'fsdp')), may hold values from -0.21875 to 0.21875
- value_bias: bfloat16 [768], P(('dp', 'fsdp')), may hold values from -3 to 3
- merge_weight: bfloat16 [768, 768], P(('dp', 'fsdp')), may hold values from -0.875 to 0.875
- merge_bias: bfloat16 [768], P(('dp', 'fsdp')), may hold values from -1.75 to 1.75
- first_gain: bfloat16 [768], P(('dp', 'fsdp')), may hold values from 0.099609375 to 1.8984375
- first_shift: bfloat16 [768], P(('dp', 'fsdp')), may hold values from -1.75 to 1.75
- inner_weight: bfloat16 [768, 3072], P(('dp', 'fsdp')), may hold values from -0.21875 to 0.21875
- inner_bias: bfloat16 [3072], P(('dp', 'fsdp')), may hold values from -3 to 3
- outer_weight: bfloat16 [3072, 768], P(('dp', 'fsdp')), may hold values from -0.109375 to 0.109375
- outer_bias: bfloat16 [768], P(('dp', 'fsdp')), may hold values from -1.75 to 1.75
- second_gain: bfloat16 [768], P(('dp', 'fsdp')), may hold values from 0.099609375 to 1.8984375
- second_shift: bfloat16 [768], P(('dp', 'fsdp')), may hold values from -1.75 to 1.75
Outputs:
- layer_output: bfloat16 [64, 1024, 768], P(('dp', 'fsdp'))
- input_gradient: float32 [64, 1024, 768], P(('dp', 'fsdp'))
- query_weight_gradient: float32 [768, 768], P(('dp', 'fsdp'))
- query_bias_gradient: float32 [768], P(('dp', 'fsdp'))
- key_weight_gradient: float32 [768, 768], P(('dp', 'fsdp'))
- value_weight_gradient: float32 [768, 768], P(('dp', 'fsdp'))
- value_bias_gradient: float32 [768], P(('dp', 'fsdp'))
- merge_weight_gradient: float32 [768, 768], P(('dp', 'fsdp'))
- merge_bias_gradient: float32 [768], P(('dp', 'fsdp'))
- first_gain_gradient: float32 [768], P(('dp', 'fsdp'))
- first_shift_gradient: float32 [768], P(('dp', 'fsdp'))
- inner_weight_gradient: float32 [768, 3072], P(('dp', 'fsdp'))
- inner_bias_gradient: float32 [3072], P(('dp', 'fsdp'))
- outer_weight_gradient: float32 [3072, 768], P(('dp', 'fsdp'))
- outer_bias_gradient: float32 [768], P(('dp', 'fsdp'))
- second_gain_gradient: float32 [768], P(('dp', 'fsdp'))
- second_shift_gradient: float32 [768], P(('dp', 'fsdp'))
- layer_stats: float32 [5], replicated
Inputs may be any that keep to these rules, and one draw needn't show every extreme that they name: `doc_lengths`: each row sums to 1024.
All inputs are finite; a program needn't handle non-finite values.
Results may differ from a plain program's by a relative error of at most 0.014.
Values may be sent and summed in bfloat16 or wider, within the bound.
No kernel may reach another device: no remote copies, remote signals or barrier semaphores. Data moves between devices by JAX's collectives and lax.ppermute only.
A program may use at most 256 MiB of HBM per device.

v0:
```python
import jax
import jax.numpy as jnp
from jax import lax
from jax.sharding import PartitionSpec as P

HEADS = 12
HEAD_DIM = 64
LEN = 1024
DOCS = 8
MICRO = 2


EPSILON = 1e-12
NEGATIVE = -1e30
ROOT_HALF = 0.7071067811865476
INV_ROOT_TWO_PI = 0.3989422804014327
block_limit = 512


def positions(lengths_row, pad_count):
    doc_ends = jnp.cumsum(lengths_row)
    places = jnp.arange(LEN, dtype=jnp.int32)
    segment = jnp.sum((places[:, None] >= doc_ends[None, :]).astype(jnp.int32), axis=1)
    is_valid = places < LEN - pad_count
    return (jnp.where(is_valid, segment, DOCS), is_valid)


def matmul(left, right):
    return jnp.dot(left, right, preferred_element_type=jnp.float32)


def transposed_times(left, right):
    return lax.dot_general(
        left, right, (((0,), (0,)), ((), ())), preferred_element_type=jnp.float32
    )


def times_transposed(left, right):
    return lax.dot_general(
        left, right, (((1,), (1,)), ((), ())), preferred_element_type=jnp.float32
    )


def gelu_value(inner):
    return 0.5 * inner * (1.0 + lax.erf(inner * ROOT_HALF))


def gelu_slope(inner):
    return (
        0.5 * (1.0 + lax.erf(inner * ROOT_HALF))
        + inner * jnp.exp(-0.5 * inner * inner) * INV_ROOT_TWO_PI
    )


def norm_forward(values, gain, shift):
    center = jnp.mean(values, axis=-1, keepdims=True)
    centred = values - center
    inverse = lax.rsqrt(jnp.mean(centred * centred, axis=-1, keepdims=True) + EPSILON)
    normed = centred * inverse
    return (normed * gain + shift, normed, inverse)


def norm_backward(upstream, normed, inverse, gain):
    scaled = upstream * gain
    return inverse * (
        scaled
        - jnp.mean(scaled, axis=-1, keepdims=True)
        - normed * jnp.mean(scaled * normed, axis=-1, keepdims=True)
    )


def block_scores(queries, own_segment, key_rows, segment):
    scores = jnp.einsum(
        "qhd,khd->hqk", queries, key_rows, preferred_element_type=jnp.float32
    ) * HEAD_DIM ** (-0.5)
    allowed = own_segment[:, None] == segment[None, :]
    return jnp.where(allowed[None], scores, NEGATIVE)


def attend_forward(item):
    query_rows, key_rows, value_rows, segment = item
    length = query_rows.shape[0]
    block = min(block_limit, length)

    def one_block(index):
        start = index * block
        queries = lax.dynamic_slice_in_dim(query_rows, start, block, 0)
        own_segment = lax.dynamic_slice_in_dim(segment, start, block, 0)
        masked = block_scores(queries, own_segment, key_rows, segment)
        top = jnp.max(masked, axis=-1, keepdims=True)
        expo = jnp.exp(masked - top)
        total = jnp.sum(expo, axis=-1, keepdims=True)
        probs_low = (expo / total).astype(jnp.bfloat16)
        mixed = jnp.einsum(
            "hqk,khd->qhd", probs_low, value_rows, preferred_element_type=jnp.float32
        )
        return (mixed.astype(jnp.bfloat16), (top + jnp.log(total))[..., 0])

    mixed, logsum = lax.map(one_block, jnp.arange(length // block))
    return (mixed.reshape(length, -1), logsum)


def attend_backward(item):
    query_rows, key_rows, value_rows, segment, logsum, mixed_grad = item
    length = query_rows.shape[0]
    block = min(block_limit, length)
    scale = HEAD_DIM ** (-0.5)

    def one_block(carry, index):
        key_grad, value_grad = carry
        start = index * block
        queries = lax.dynamic_slice_in_dim(query_rows, start, block, 0)
        own_segment = lax.dynamic_slice_in_dim(segment, start, block, 0)
        grad_block = lax.dynamic_slice_in_dim(mixed_grad, start, block, 0)
        block_logsum = lax.dynamic_index_in_dim(logsum, index, 0, keepdims=False)
        masked = block_scores(queries, own_segment, key_rows, segment)
        probs = jnp.exp(masked - block_logsum[..., None])
        prob_grad = jnp.einsum(
            "qhd,khd->hqk", grad_block, value_rows, preferred_element_type=jnp.float32
        )
        inner_sum = jnp.sum(prob_grad * probs, axis=-1, keepdims=True)
        score_low = (probs * (prob_grad - inner_sum)).astype(jnp.bfloat16)
        query_grad = (
            jnp.einsum("hqk,khd->qhd", score_low, key_rows, preferred_element_type=jnp.float32)
            * scale
        )
        key_grad = (
            key_grad
            + jnp.einsum("hqk,qhd->khd", score_low, queries, preferred_element_type=jnp.float32)
            * scale
        )
        value_grad = value_grad + jnp.einsum(
            "hqk,qhd->khd",
            probs.astype(jnp.bfloat16),
            grad_block,
            preferred_element_type=jnp.float32,
        )
        return ((key_grad, value_grad), query_grad)

    zeros = jnp.zeros(key_rows.shape, jnp.float32)
    (key_grad, value_grad), query_grad = lax.scan(
        one_block, (zeros, zeros), jnp.arange(length // block)
    )
    return (query_grad.reshape(key_rows.shape), key_grad, value_grad)


def heads_view(values, count_seq):
    return values.reshape(count_seq, LEN, HEADS, HEAD_DIM)


def forward_pass(whole, rows, segment, is_valid):
    (
        query_mat,
        query_add,
        key_mat,
        value_mat,
        value_add,
        merge_mat,
        merge_add,
        first_scale,
        first_offset,
        inner_mat,
        inner_add,
        outer_mat,
        outer_add,
        second_scale,
        second_offset,
    ) = whole
    count_seq = rows.shape[0]
    width = rows.shape[2]
    flat = rows.reshape(-1, width)
    query_rows = (matmul(flat, query_mat) + query_add.astype(jnp.float32)).astype(jnp.bfloat16)
    key_rows = matmul(flat, key_mat).astype(jnp.bfloat16)
    value_rows = (matmul(flat, value_mat) + value_add.astype(jnp.float32)).astype(jnp.bfloat16)
    mixed, logsum = lax.map(
        attend_forward,
        (
            heads_view(query_rows, count_seq),
            heads_view(key_rows, count_seq),
            heads_view(value_rows, count_seq),
            segment,
        ),
    )
    mixed = mixed.reshape(-1, width)
    branch = matmul(mixed, merge_mat) + merge_add.astype(jnp.float32)
    flat_value = flat.astype(jnp.float32)
    first, first_normed, first_inverse = norm_forward(
        flat_value + branch, first_scale.astype(jnp.float32), first_offset.astype(jnp.float32)
    )
    first_low = first.astype(jnp.bfloat16)
    inner = matmul(first_low, inner_mat) + inner_add.astype(jnp.float32)
    hidden = gelu_value(inner).astype(jnp.bfloat16)
    second = matmul(hidden, outer_mat) + outer_add.astype(jnp.float32)
    result, second_normed, second_inverse = norm_forward(
        first + second, second_scale.astype(jnp.float32), second_offset.astype(jnp.float32)
    )
    weight = is_valid.reshape(-1, 1).astype(jnp.float32)
    sums = jnp.stack(
        [
            jnp.sum(weight * flat_value * flat_value),
            jnp.sum(weight * branch * branch),
            jnp.sum(weight * second * second),
            jnp.sum(weight * result * result),
        ]
    )
    kept = (
        query_rows,
        key_rows,
        value_rows,
        logsum,
        mixed,
        first_normed,
        first_inverse,
        first_low,
        inner,
        hidden,
        second_normed,
        second_inverse,
    )
    return (result.astype(jnp.bfloat16).reshape(rows.shape), kept, sums)


def backward_pass(whole, rows, grad_rows, segment, is_valid, kept):
    (
        query_mat,
        query_add,
        key_mat,
        value_mat,
        value_add,
        merge_mat,
        merge_add,
        first_scale,
        first_offset,
        inner_mat,
        inner_add,
        outer_mat,
        outer_add,
        second_scale,
        second_offset,
    ) = whole
    (
        query_rows,
        key_rows,
        value_rows,
        logsum,
        mixed,
        first_normed,
        first_inverse,
        first_low,
        inner,
        hidden,
        second_normed,
        second_inverse,
    ) = kept
    count_seq = rows.shape[0]
    width = rows.shape[2]
    flat = rows.reshape(-1, width)
    weight = is_valid.reshape(-1, 1).astype(jnp.float32)
    upstream = grad_rows.reshape(-1, width).astype(jnp.float32) * weight
    second_scale_grad = jnp.sum(upstream * second_normed, axis=0)
    second_offset_grad = jnp.sum(upstream, axis=0)
    upper_grad = norm_backward(
        upstream, second_normed, second_inverse, second_scale.astype(jnp.float32)
    )
    upper_low = upper_grad.astype(jnp.bfloat16)
    outer_mat_grad = transposed_times(hidden, upper_low)
    outer_add_grad = jnp.sum(upper_low.astype(jnp.float32), axis=0)
    hidden_grad = times_transposed(upper_low, outer_mat)
    inner_low = (hidden_grad * gelu_slope(inner)).astype(jnp.bfloat16)
    inner_mat_grad = transposed_times(first_low, inner_low)
    inner_add_grad = jnp.sum(inner_low.astype(jnp.float32), axis=0)
    first_grad = upper_grad + times_transposed(inner_low, inner_mat)
    first_scale_grad = jnp.sum(first_grad * first_normed, axis=0)
    first_offset_grad = jnp.sum(first_grad, axis=0)
    residual_grad = norm_backward(
        first_grad, first_normed, first_inverse, first_scale.astype(jnp.float32)
    )
    branch_low = residual_grad.astype(jnp.bfloat16)
    merge_mat_grad = transposed_times(mixed, branch_low)
    merge_add_grad = jnp.sum(branch_low.astype(jnp.float32), axis=0)
    mixed_grad = times_transposed(branch_low, merge_mat).astype(jnp.bfloat16)
    query_grad, key_grad, value_grad = lax.map(
        attend_backward,
        (
            heads_view(query_rows, count_seq),
            heads_view(key_rows, count_seq),
            heads_view(value_rows, count_seq),
            segment,
            logsum,
            heads_view(mixed_grad, count_seq),
        ),
    )
    query_low = query_grad.reshape(-1, width).astype(jnp.bfloat16)
    key_low = key_grad.reshape(-1, width).astype(jnp.bfloat16)
    value_low = value_grad.reshape(-1, width).astype(jnp.bfloat16)
    query_mat_grad = transposed_times(flat, query_low)
    query_add_grad = jnp.sum(query_low.astype(jnp.float32), axis=0)
    key_mat_grad = transposed_times(flat, key_low)
    value_mat_grad = transposed_times(flat, value_low)
    value_add_grad = jnp.sum(value_low.astype(jnp.float32), axis=0)
    input_grad = (
        residual_grad
        + times_transposed(query_low, query_mat)
        + times_transposed(key_low, key_mat)
        + times_transposed(value_low, value_mat)
    )
    grads = (
        query_mat_grad,
        query_add_grad,
        key_mat_grad,
        value_mat_grad,
        value_add_grad,
        merge_mat_grad,
        merge_add_grad,
        first_scale_grad,
        first_offset_grad,
        inner_mat_grad,
        inner_add_grad,
        outer_mat_grad,
        outer_add_grad,
        second_scale_grad,
        second_offset_grad,
    )
    return (input_grad.reshape(rows.shape), grads)


def collect(shards):
    return (
        lax.all_gather(shards[0], ("dp", "fsdp"), axis=0, tiled=True),
        lax.all_gather(shards[1], ("dp", "fsdp"), axis=0, tiled=True),
        lax.all_gather(shards[2], ("dp", "fsdp"), axis=0, tiled=True),
        lax.all_gather(shards[3], ("dp", "fsdp"), axis=0, tiled=True),
        lax.all_gather(shards[4], ("dp", "fsdp"), axis=0, tiled=True),
        lax.all_gather(shards[5], ("dp", "fsdp"), axis=0, tiled=True),
        lax.all_gather(shards[6], ("dp", "fsdp"), axis=0, tiled=True),
        lax.all_gather(shards[7], ("dp", "fsdp"), axis=0, tiled=True),
        lax.all_gather(shards[8], ("dp", "fsdp"), axis=0, tiled=True),
        lax.all_gather(shards[9], ("dp", "fsdp"), axis=0, tiled=True),
        lax.all_gather(shards[10], ("dp", "fsdp"), axis=0, tiled=True),
        lax.all_gather(shards[11], ("dp", "fsdp"), axis=0, tiled=True),
        lax.all_gather(shards[12], ("dp", "fsdp"), axis=0, tiled=True),
        lax.all_gather(shards[13], ("dp", "fsdp"), axis=0, tiled=True),
        lax.all_gather(shards[14], ("dp", "fsdp"), axis=0, tiled=True),
    )


def per_device(
    layer_input,
    cotangent,
    doc_lengths,
    pad_tail,
    query_weight,
    query_bias,
    key_weight,
    value_weight,
    value_bias,
    merge_weight,
    merge_bias,
    first_gain,
    first_shift,
    inner_weight,
    inner_bias,
    outer_weight,
    outer_bias,
    second_gain,
    second_shift,
):
    shards = (
        query_weight,
        query_bias,
        key_weight,
        value_weight,
        value_bias,
        merge_weight,
        merge_bias,
        first_gain,
        first_shift,
        inner_weight,
        inner_bias,
        outer_weight,
        outer_bias,
        second_gain,
        second_shift,
    )
    segments, validity = jax.vmap(positions)(doc_lengths, pad_tail)
    per_micro = layer_input.shape[0] // MICRO
    output_blocks = []
    grad_blocks = []
    totals = None
    stat_sums = jnp.zeros((4,), jnp.float32)
    for micro_step in range(MICRO):
        lower = micro_step * per_micro
        rows = layer_input[lower : lower + per_micro]
        grad_rows = cotangent[lower : lower + per_micro]
        segment = segments[lower : lower + per_micro]
        is_valid = validity[lower : lower + per_micro]
        forward_weights = collect(shards)
        result, kept, sums = forward_pass(forward_weights, rows, segment, is_valid)
        backward_weights = (
            lax.all_gather(query_weight, ("dp", "fsdp"), axis=0, tiled=True),
            lax.all_gather(query_bias, ("dp", "fsdp"), axis=0, tiled=True),
            lax.all_gather(key_weight, ("dp", "fsdp"), axis=0, tiled=True),
            lax.all_gather(value_weight, ("dp", "fsdp"), axis=0, tiled=True),
            lax.all_gather(value_bias, ("dp", "fsdp"), axis=0, tiled=True),
            lax.all_gather(merge_weight, ("dp", "fsdp"), axis=0, tiled=True),
            lax.all_gather(merge_bias, ("dp", "fsdp"), axis=0, tiled=True),
            lax.all_gather(first_gain, ("dp", "fsdp"), axis=0, tiled=True),
            lax.all_gather(first_shift, ("dp", "fsdp"), axis=0, tiled=True),
            lax.all_gather(inner_weight, ("dp", "fsdp"), axis=0, tiled=True),
            lax.all_gather(inner_bias, ("dp", "fsdp"), axis=0, tiled=True),
            lax.all_gather(outer_weight, ("dp", "fsdp"), axis=0, tiled=True),
            lax.all_gather(outer_bias, ("dp", "fsdp"), axis=0, tiled=True),
            lax.all_gather(second_gain, ("dp", "fsdp"), axis=0, tiled=True),
            lax.all_gather(second_shift, ("dp", "fsdp"), axis=0, tiled=True),
        )
        input_grad, micro_grads = backward_pass(
            backward_weights, rows, grad_rows, segment, is_valid, kept
        )
        output_blocks.append(result)
        grad_blocks.append(input_grad)
        stat_sums = stat_sums + sums
        totals = micro_grads if totals is None else jax.tree.map(jnp.add, totals, micro_grads)
    totals = (
        lax.psum_scatter(totals[0], ("dp", "fsdp"), scatter_dimension=0, tiled=True),
        lax.psum_scatter(totals[1], ("dp", "fsdp"), scatter_dimension=0, tiled=True),
        lax.psum_scatter(totals[2], ("dp", "fsdp"), scatter_dimension=0, tiled=True),
        lax.psum_scatter(totals[3], ("dp", "fsdp"), scatter_dimension=0, tiled=True),
        lax.psum_scatter(totals[4], ("dp", "fsdp"), scatter_dimension=0, tiled=True),
        lax.psum_scatter(totals[5], ("dp", "fsdp"), scatter_dimension=0, tiled=True),
        lax.psum_scatter(totals[6], ("dp", "fsdp"), scatter_dimension=0, tiled=True),
        lax.psum_scatter(totals[7], ("dp", "fsdp"), scatter_dimension=0, tiled=True),
        lax.psum_scatter(totals[8], ("dp", "fsdp"), scatter_dimension=0, tiled=True),
        lax.psum_scatter(totals[9], ("dp", "fsdp"), scatter_dimension=0, tiled=True),
        lax.psum_scatter(totals[10], ("dp", "fsdp"), scatter_dimension=0, tiled=True),
        lax.psum_scatter(totals[11], ("dp", "fsdp"), scatter_dimension=0, tiled=True),
        lax.psum_scatter(totals[12], ("dp", "fsdp"), scatter_dimension=0, tiled=True),
        lax.psum_scatter(totals[13], ("dp", "fsdp"), scatter_dimension=0, tiled=True),
        lax.psum_scatter(totals[14], ("dp", "fsdp"), scatter_dimension=0, tiled=True),
    )
    local_count = jnp.sum(validity.astype(jnp.float32))
    count, global_sums = lax.psum((local_count, stat_sums), ("dp", "fsdp"))
    all_tokens = layer_input.shape[0] * LEN * lax.axis_size(("dp", "fsdp"))
    width = layer_input.shape[2]
    stats = jnp.concatenate(
        [jnp.reshape(count / all_tokens, (1,)), jnp.sqrt(global_sums / (count * width))]
    )
    layer_output = jnp.concatenate(output_blocks, axis=0)
    input_gradient = jnp.concatenate(grad_blocks, axis=0)
    return (
        layer_output,
        input_gradient,
        totals[0],
        totals[1],
        totals[2],
        totals[3],
        totals[4],
        totals[5],
        totals[6],
        totals[7],
        totals[8],
        totals[9],
        totals[10],
        totals[11],
        totals[12],
        totals[13],
        totals[14],
        stats,
    )


def solution(mesh):
    in_specs = (
        P(("dp", "fsdp"), None, None),
        P(("dp", "fsdp"), None, None),
        P(("dp", "fsdp"), None),
        P(("dp", "fsdp")),
        P(("dp", "fsdp"), None),
        P(("dp", "fsdp")),
        P(("dp", "fsdp"), None),
        P(("dp", "fsdp"), None),
        P(("dp", "fsdp")),
        P(("dp", "fsdp"), None),
        P(("dp", "fsdp")),
        P(("dp", "fsdp")),
        P(("dp", "fsdp")),
        P(("dp", "fsdp"), None),
        P(("dp", "fsdp")),
        P(("dp", "fsdp"), None),
        P(("dp", "fsdp")),
        P(("dp", "fsdp")),
        P(("dp", "fsdp")),
    )
    out_specs = (
        P(("dp", "fsdp"), None, None),
        P(("dp", "fsdp"), None, None),
        P(("dp", "fsdp"), None),
        P(("dp", "fsdp")),
        P(("dp", "fsdp"), None),
        P(("dp", "fsdp"), None),
        P(("dp", "fsdp")),
        P(("dp", "fsdp"), None),
        P(("dp", "fsdp")),
        P(("dp", "fsdp")),
        P(("dp", "fsdp")),
        P(("dp", "fsdp"), None),
        P(("dp", "fsdp")),
        P(("dp", "fsdp"), None),
        P(("dp", "fsdp")),
        P(("dp", "fsdp")),
        P(("dp", "fsdp")),
        P(),
    )
    return jax.shard_map(
        per_device, mesh=mesh, in_specs=in_specs, out_specs=out_specs, check_vma=False
    )
```

profile of v0, /device:TPU:0, one launch (start us, length us, event | category | flops | bytes accessed | tf_op | source)
XLA Modules:
  0.0 1471.9 jit_solution(1130040377138631337)
XLA Ops:
  21.0 42.5 %all-reduce.19 = (bf16[768]{0:T(1024)(128)(2,1)S(1)}, bf16[768]{0:T(1024)(128)(2,1)S(1)}, bf16[768]{0:T(1024)(128)(2,1)S(1)}, bf16[768]{0:T(1024)(128)(2,1)S(1)}...) all-reduce(bf16[768]{0:T(1024)(128)(2,1)S(1)} %dynamic-update-slice, ...), channel_id=1, replica_groups=mesh['dp'=8,'fsdp'=4] {'dp','fsdp'}, use_global_device_ids=true, to_apply=%add | all-reduce | flops 9216 | bytes 36864
  82.3 41.3 %all-gather.11.cloned.1.call-done = bf16[768,768]{1,0:T(8,128)(2,1)} async-done(((bf16[24,768]{1,0:T(8,128)(2,1)}), bf16[768,768]{1,0:T(8,128)(2,1)}) %all-gather.11.cloned.1.call-update) | async-done | bytes 1179664 | tf_op jit(solution)/shard_map/all_gather | solution.py:332
  128.0 51.5 %all-gather.7.cloned.1.call-done = bf16[768,768]{1,0:T(8,128)(2,1)} async-done(((bf16[24,768]{1,0:T(8,128)(2,1)}), bf16[768,768]{1,0:T(8,128)(2,1)}) %all-gather.7.cloned.1.call-update) | async-done | bytes 1179664 | tf_op jit(solution)/shard_map/all_gather | solution.py:329
  184.0 73.0 %while.95 = (s32[]{:T(128)}, bf16[2,512,12,64]{1,3,2,0:T(8,128)(2,1)}, f32[2,12,512]{2,1,0:T(8,128)S(1)}, s32[2]{0:T(128)S(1)}, s32[1024]{0:T(1024)S(1)}, /*inde...) while((s32[]{:T(128)}, ...), condition=%wide.region_13.14_spmd, body=%wide.region_10.13_spmd.sunk | while | flops 1687021568 | bytes 189499632 | solution.py:99
  186.0 10.6 fusion.273
  196.6 12.3 fusion.274
  212.0 8.5 fusion.275
  222.2 10.7 fusion.273
  232.9 12.4 fusion.274
  248.5 8.5 fusion.275
  267.5 81.8 %while.94 = (s32[]{:T(128)}, bf16[2,512,12,64]{1,3,2,0:T(8,128)(2,1)}, f32[2,12,512]{2,1,0:T(8,128)S(1)}, s32[2]{0:T(128)S(1)}, s32[1024]{0:T(1024)S(1)}, /*inde...) while((s32[]{:T(128)}, ...), condition=%wide.region_5.6_spmd, body=%wide.region_2.5_spmd.sunk | while | flops 1687021568 | bytes 189499632 | solution.py:99
  269.2 10.6 fusion.268
  279.8 13.0 fusion.269
  296.1 8.5 fusion.270
  306.3 10.6 fusion.268
  317.0 12.4 fusion.269
  332.5 8.5 fusion.270
  367.0 7.9 fusion.148
  379.4 13.6 multiply_convert_fusion.3
  393.0 9.9 fusion.164
  402.9 12.9 fusion.156
  418.7 11.3 fusion.74
  430.0 5.1 convert_reduce_fusion.3
  435.1 15.0 %convert_reduce_fusion.1 = (f32[3072]{0:T(1024)}, bf16[1024,3072]{1,0:T(8,128)(2,1)}) fusion(f32[1024,3072]{1,0:T(8,128)} %get-tuple-element.658, f32[3072]{0:T(1024)S(1)} %copy-done.97, bf16[1024,768]{0,1:T(8,128)(2,1)S(1)} %get-tuple-element.606, bf16[3072,768]{1,0:T(8,128)(2,1)} %all-gather.17.cloned.1.call-done), kind=kOutput, calls=%fused_computation.93 | convolution fusion | flops 4872729600 | bytes 25190400 | tf_op jit(solution)/shard_map/dot_general | solution.py:39
  450.1 10.7 multiply_reduce_fusion.3
  462.8 14.9 %convert_reduce_fusion = (f32[3072]{0:T(1024)}, bf16[1024,3072]{1,0:T(8,128)(2,1)}) fusion(f32[1024,3072]{1,0:T(8,128)} %copy-done.31, f32[3072]{0:T(1024)S(1)} %copy-done.97, bf16[1024,768]{0,1:T(8,128)(2,1)S(1)} %get-tuple-element.604, bf16[3072,768]{1,0:T(8,128)(2,1)} %all-gather.17.cloned.1.call-done), kind=kOutput, calls=%fused_computation.92 | convolution fusion | flops 4872729600 | bytes 25190400 | tf_op jit(solution)/shard_map/dot_general | solution.py:39
  477.7 13.0 convert_reduce_fusion.5
  506.4 175.1 %while.97 = (s32[]{:T(128)}, f32[1024,12,64]{0,2,1:T(8,128)}, f32[1024,12,64]{0,2,1:T(8,128)}, bf16[2,512,12,64]{1,3,2,0:T(8,128)(2,1)}, s32[2]{0:T(128)S(1)}, /...) while((s32[]{:T(128)}, f32[1024,12,64]{0,2,1:T(8,128)}, ...), condition=%wide.region_31.32_spmd.clone, body=%wide.region_29.31_spmd.clone.sunk | while | flops 4125747200 | bytes 225634640 | solution.py:141
  510.5 11.6 fusion.295
  522.1 13.7 bitcast_add_fusion.11
  535.8 18.2 %multiply_reduce_fusion.15 = (f32[12,512]{1,0:T(8,128)S(1)}, f32[12,512,1024]{2,1,0:T(8,128)}) fusion(f32[12,512,1024]{2,1,0:T(8,128)} %fusion.295, f32[12,512]{1,0:T(8,128)S(1)} %dynamic-slice_bitcast_fusion.5, pred[512,1024]{1,0:T(8,128)(4,1)S(1)} %broadcast_compare_fusion.11, bf16[1024,12,64]{0,2,1:T(8,128)(2,1)} %get-tuple-element.1030, ...), kind=kOutput, calls=%fused_computation.56.clone.1 | convolution fusion | flops 836757504 | bytes 53264388 | tf_op jit(solution)/shard_map/while/body/eval_jaxpr/while/body/eval_jaxpr/qhd,khd->hqk/dot_general | solution.py:118
  553.9 21.9 %multiply_convert_fusion.7 = bf16[12,512,1024]{2,1,0:T(8,128)(2,1)} fusion(f32[12,512,1024]{2,1,0:T(8,128)} %get-tuple-element.914, f32[12,512,1024]{2,1,0:T(8,128)} %fusion.295, f32[12,512]{1,0:T(8,128)S(1)} %get-tuple-element.915, f32[12,512]{1,0:T(8,128)S(1)} %dynamic-slice_bitcast_fusion.5, pred[512,1024]{1,0:T(8,128)(4,1)S(1)} %broadcast_compare_fusion.11), kind=kLoop, calls=%fused_computation.55.clone.1 | loop fusion | flops 37748736 | bytes 63488000 | tf_op jit(solution)/shard_map/while/body/eval_jaxpr/while/body/eval_jaxpr/convert_element_type | solution.py:122
  575.8 9.6 bitcast_dynamic-update-slice_fusion.11
  585.4 8.5 bitcast_add_fusion.10
  597.6 11.4 fusion.295
  609.0 14.2 bitcast_add_fusion.11
  623.2 18.1 %multiply_reduce_fusion.15 = (f32[12,512]{1,0:T(8,128)S(1)}, f32[12,512,1024]{2,1,0:T(8,128)}) fusion(f32[12,512,1024]{2,1,0:T(8,128)} %fusion.295, f32[12,512]{1,0:T(8,128)S(1)} %dynamic-slice_bitcast_fusion.5, pred[512,1024]{1,0:T(8,128)(4,1)S(1)} %broadcast_compare_fusion.11, bf16[1024,12,64]{0,2,1:T(8,128)(2,1)} %get-tuple-element.1030, ...), kind=kOutput, calls=%fused_computation.56.clone.1 | convolution fusion | flops 836757504 | bytes 53264388 | tf_op jit(solution)/shard_map/while/body/eval_jaxpr/while/body/eval_jaxpr/qhd,khd->hqk/dot_general | solution.py:118
  641.2 21.2 %multiply_convert_fusion.7 = bf16[12,512,1024]{2,1,0:T(8,128)(2,1)} fusion(f32[12,512,1024]{2,1,0:T(8,128)} %get-tuple-element.914, f32[12,512,1024]{2,1,0:T(8,128)} %fusion.295, f32[12,512]{1,0:T(8,128)S(1)} %get-tuple-element.915, f32[12,512]{1,0:T(8,128)S(1)} %dynamic-slice_bitcast_fusion.5, pred[512,1024]{1,0:T(8,128)(4,1)S(1)} %broadcast_compare_fusion.11), kind=kLoop, calls=%fused_computation.55.clone.1 | loop fusion | flops 37748736 | bytes 63488000 | tf_op jit(solution)/shard_map/while/body/eval_jaxpr/while/body/eval_jaxpr/convert_element_type | solution.py:122
  662.4 9.5 bitcast_dynamic-update-slice_fusion.11
  671.9 9.4 bitcast_add_fusion.10
  687.8 173.7 %while.96 = (s32[]{:T(128)}, f32[1024,12,64]{0,2,1:T(8,128)}, f32[1024,12,64]{0,2,1:T(8,128)}, bf16[2,512,12,64]{1,3,2,0:T(8,128)(2,1)}, s32[2]{0:T(128)S(1)}, /...) while((s32[]{:T(128)}, f32[1024,12,64]{0,2,1:T(8,128)}, ...), condition=%wide.region_24.25_spmd.clone, body=%wide.region_22.24_spmd.clone.sunk | while | flops 4125747200 | bytes 225634640 | solution.py:141
  691.5 11.4 fusion.285
  702.9 13.3 bitcast_add_fusion.9
  716.2 18.1 %multiply_reduce_fusion.14 = (f32[12,512]{1,0:T(8,128)S(1)}, f32[12,512,1024]{2,1,0:T(8,128)}) fusion(f32[12,512,1024]{2,1,0:T(8,128)} %fusion.285, f32[12,512]{1,0:T(8,128)S(1)} %dynamic-slice_bitcast_fusion.4, pred[512,1024]{1,0:T(8,128)(4,1)S(1)} %broadcast_compare_fusion.10, bf16[1024,12,64]{0,2,1:T(8,128)(2,1)} %get-tuple-element.1078, ...), kind=kOutput, calls=%fused_computation.33.clone.1 | convolution fusion | flops 836757504 | bytes 53264388 | tf_op jit(solution)/shard_map/while/body/eval_jaxpr/while/body/eval_jaxpr/qhd,khd->hqk/dot_general | solution.py:118
  734.2 21.2 %multiply_convert_fusion.6 = bf16[12,512,1024]{2,1,0:T(8,128)(2,1)} fusion(f32[12,512,1024]{2,1,0:T(8,128)} %get-tuple-element.901, f32[12,512,1024]{2,1,0:T(8,128)} %fusion.285, f32[12,512]{1,0:T(8,128)S(1)} %get-tuple-element.902, f32[12,512]{1,0:T(8,128)S(1)} %dynamic-slice_bitcast_fusion.4, pred[512,1024]{1,0:T(8,128)(4,1)S(1)} %broadcast_compare_fusion.10), kind=kLoop, calls=%fused_computation.32.clone.1 | loop fusion | flops 37748736 | bytes 63488000 | tf_op jit(solution)/shard_map/while/body/eval_jaxpr/while/body/eval_jaxpr/convert_element_type | solution.py:122
  755.4 9.5 bitcast_dynamic-update-slice_fusion.10
  764.9 8.7 bitcast_add_fusion.8
  777.3 11.4 fusion.285
  788.6 14.2 bitcast_add_fusion.9
  802.8 18.1 %multiply_reduce_fusion.14 = (f32[12,512]{1,0:T(8,128)S(1)}, f32[12,512,1024]{2,1,0:T(8,128)}) fusion(f32[12,512,1024]{2,1,0:T(8,128)} %fusion.285, f32[12,512]{1,0:T(8,128)S(1)} %dynamic-slice_bitcast_fusion.4, pred[512,1024]{1,0:T(8,128)(4,1)S(1)} %broadcast_compare_fusion.10, bf16[1024,12,64]{0,2,1:T(8,128)(2,1)} %get-tuple-element.1078, ...), kind=kOutput, calls=%fused_computation.33.clone.1 | convolution fusion | flops 836757504 | bytes 53264388 | tf_op jit(solution)/shard_map/while/body/eval_jaxpr/while/body/eval_jaxpr/qhd,khd->hqk/dot_general | solution.py:118
  820.9 21.2 %multiply_convert_fusion.6 = bf16[12,512,1024]{2,1,0:T(8,128)(2,1)} fusion(f32[12,512,1024]{2,1,0:T(8,128)} %get-tuple-element.901, f32[12,512,1024]{2,1,0:T(8,128)} %fusion.285, f32[12,512]{1,0:T(8,128)S(1)} %get-tuple-element.902, f32[12,512]{1,0:T(8,128)S(1)} %dynamic-slice_bitcast_fusion.4, pred[512,1024]{1,0:T(8,128)(4,1)S(1)} %broadcast_compare_fusion.10), kind=kLoop, calls=%fused_computation.32.clone.1 | loop fusion | flops 37748736 | bytes 63488000 | tf_op jit(solution)/shard_map/while/body/eval_jaxpr/while/body/eval_jaxpr/convert_element_type | solution.py:122
  842.1 9.6 bitcast_dynamic-update-slice_fusion.10
  851.7 9.6 bitcast_add_fusion.8
  894.9 8.6 fusion.150
  903.5 10.6 convolution_add_fusion.1
  915.6 7.3 fusion.165
  922.8 10.5 convolution_add_fusion
  943.1 5.3 maximum_add_fusion
  948.3 41.2 %all-reduce.18 = (f32[768]{0:T(1024)S(1)}, f32[768]{0:T(1024)S(1)}, f32[768]{0:T(1024)S(1)}, f32[768]{0:T(1024)S(1)}, f32[768]{0:T(1024)S(1)}, /*index=5*/f32[30...) all-reduce(f32[768]{0:T(1024)S(1)} %add.408, ...), channel_id=3, replica_groups=mesh['dp'=8,'fsdp'=4] {'dp','fsdp'}, use_global_device_ids=true, to_apply=%region_35.36.clone | all-reduce | flops 9221 | bytes 73768
  1012.1 6.6 copy.121
  1019.9 57.2 %reduce-scatter.19.cloned.1.call-done = f32[24,768]{1,0:T(8,128)} async-done(((f32[768,768]{1,0:T(8,128)}), f32[24,768]{1,0:T(8,128)}) %reduce-scatter.19.cloned.1.call-update) | async-done | bytes 73744
  1077.1 104.5 %reduce-scatter.21.cloned.1.call-done = f32[24,768]{1,0:T(8,128)} async-done(((f32[768,768]{1,0:T(8,128)}), f32[24,768]{1,0:T(8,128)}) %reduce-scatter.21.cloned.1.call-update) | async-done | bytes 73744
  1181.7 141.2 %reduce-scatter.15.cloned.1.call-done = f32[24,3072]{1,0:T(8,128)} async-done(((f32[768,3072]{1,0:T(8,128)}), f32[24,3072]{1,0:T(8,128)}) %reduce-scatter.15.cloned.1.call-update) | async-done | bytes 294928 | tf_op jit(solution)/shard_map/reduce_scatter | solution.py:433
  1322.9 142.0 %reduce-scatter.17.cloned.1.call-done = f32[96,768]{1,0:T(8,128)} async-done(((f32[3072,768]{1,0:T(8,128)}), f32[96,768]{1,0:T(8,128)}) %reduce-scatter.17.cloned.1.call-update) | async-done | bytes 294928 | tf_op jit(solution)/shard_map/reduce_scatter | solution.py:435
  (459 shorter events, 187.5 us)
Async XLA Ops:
  7.2 72.0 %all-gather.9.cloned.1.call-start = ((), (), s32[]{:S(2)}) async-start(), calls=%async_computation.7 | async-start | bytes 1216512 | tf_op jit(solution)/shard_map/all_gather | solution.py:331
  7.9 115.7 %all-gather.11.cloned.1.call-start = ((), (), s32[]{:S(2)}) async-start(), calls=%async_computation.8 | async-start | bytes 1216512 | tf_op jit(solution)/shard_map/all_gather | solution.py:332
  8.7 170.8 %all-gather.7.cloned.1.call-start = ((), (), s32[]{:S(2)}) async-start(), calls=%async_computation.6 | async-start | bytes 1216512 | tf_op jit(solution)/shard_map/all_gather | solution.py:329
  9.4 349.0 %all-gather.13.cloned.1.call-start = ((), (), s32[]{:S(2)}) async-start(), calls=%async_computation.9 | async-start | bytes 1216512 | tf_op jit(solution)/shard_map/all_gather | solution.py:334
  10.0 357.0 %all-gather.15.cloned.1.call-start = ((), (), s32[]{:S(2)}) async-start(), calls=%async_computation.10 | async-start | bytes 4866048 | tf_op jit(solution)/shard_map/all_gather | solution.py:338
  10.6 382.5 %all-gather.17.cloned.1.call-start = ((), (), s32[]{:S(2)}) async-start(), calls=%async_computation.11 | async-start | bytes 4866048 | tf_op jit(solution)/shard_map/all_gather | solution.py:340
  11.1 1008.7 %reduce-scatter.13.cloned.1.call-start = ((), (), s32[]{:S(2)}) async-start(), calls=%async_computation.12 | async-start | bytes 2433024 | tf_op jit(solution)/shard_map/reduce_scatter | solution.py:429
  11.9 55.9 %copy-start.111 = (s32[2]{0:T(128)}, s32[2]{0:T(128)S(1)}, u32[]{:S(2)}) copy-start(s32[2]{0:T(128)S(1)} %broadcast_subtract_fusion) | copy-start | bytes 28
  63.5 116.0 %copy-start.105 = (f32[768]{0:T(1024)}, f32[768]{0:T(1024)S(1)}, u32[]{:S(2)}) copy-start(f32[768]{0:T(1024)S(1)} %convert_element_type.260) | copy-start | bytes 9220
  65.3 58.4 %copy-start.107 = (f32[768]{0:T(1024)}, f32[768]{0:T(1024)S(1)}, u32[]{:S(2)}) copy-start(f32[768]{0:T(1024)S(1)} %convert_element_type.263) | copy-start | bytes 9220
  184.0 74.2 %copy-start.108 = (f32[768]{0:T(1024)S(1)}, f32[768]{0:T(1024)}, u32[]{:S(2)}) copy-start(f32[768]{0:T(1024)} %copy-done.107) | copy-start | bytes 9220
  185.9 23.0 %copy-start.14 = (bf16[1024,12,64]{0,2,1:T(8,128)(2,1)S(1)}, bf16[1024,12,64]{0,2,1:T(8,128)(2,1)}, u32[]{:S(2)}) copy-start(bf16[1024,12,64]{0,2,1:T(8,128)(2,1)} %get-tuple-element.947) | copy-start | bytes 4718596 | tf_op jit(solution)/shard_map/while/body/eval_jaxpr/while
  196.6 15.4 %copy-start = (f32[12,512,1024]{2,1,0:T(8,128)S(1)}, f32[12,512,1024]{2,1,0:T(8,128)}, u32[]{:S(2)}) copy-start(f32[12,512,1024]{2,1,0:T(8,128)} %get-tuple-element.888) | copy-start | bytes 75497472 | tf_op jit(solution)/shard_map/while/body/eval_jaxpr/while
  222.2 23.0 %copy-start.14 = (bf16[1024,12,64]{0,2,1:T(8,128)(2,1)S(1)}, bf16[1024,12,64]{0,2,1:T(8,128)(2,1)}, u32[]{:S(2)}) copy-start(bf16[1024,12,64]{0,2,1:T(8,128)(2,1)} %get-tuple-element.947) | copy-start | bytes 4718596 | tf_op jit(solution)/shard_map/while/body/eval_jaxpr/while
  232.9 15.6 %copy-start = (f32[12,512,1024]{2,1,0:T(8,128)S(1)}, f32[12,512,1024]{2,1,0:T(8,128)}, u32[]{:S(2)}) copy-start(f32[12,512,1024]{2,1,0:T(8,128)} %get-tuple-element.888) | copy-start | bytes 75497472 | tf_op jit(solution)/shard_map/while/body/eval_jaxpr/while
  269.2 23.6 %copy-start.13 = (bf16[1024,12,64]{0,2,1:T(8,128)(2,1)S(1)}, bf16[1024,12,64]{0,2,1:T(8,128)(2,1)}, u32[]{:S(2)}) copy-start(bf16[1024,12,64]{0,2,1:T(8,128)(2,1)} %get-tuple-element.983) | copy-start | bytes 4718596 | tf_op jit(solution)/shard_map/while/body/eval_jaxpr/while
  279.8 16.3 %copy-start.1 = (f32[12,512,1024]{2,1,0:T(8,128)S(1)}, f32[12,512,1024]{2,1,0:T(8,128)}, u32[]{:S(2)}) copy-start(f32[12,512,1024]{2,1,0:T(8,128)} %get-tuple-element.878) | copy-start | bytes 75497472 | tf_op jit(solution)/shard_map/while/body/eval_jaxpr/while
  306.3 23.1 %copy-start.13 = (bf16[1024,12,64]{0,2,1:T(8,128)(2,1)S(1)}, bf16[1024,12,64]{0,2,1:T(8,128)(2,1)}, u32[]{:S(2)}) copy-start(bf16[1024,12,64]{0,2,1:T(8,128)(2,1)} %get-tuple-element.983) | copy-start | bytes 4718596 | tf_op jit(solution)/shard_map/while/body/eval_jaxpr/while
  317.0 15.5 %copy-start.1 = (f32[12,512,1024]{2,1,0:T(8,128)S(1)}, f32[12,512,1024]{2,1,0:T(8,128)}, u32[]{:S(2)}) copy-start(f32[12,512,1024]{2,1,0:T(8,128)} %get-tuple-element.878) | copy-start | bytes 75497472 | tf_op jit(solution)/shard_map/while/body/eval_jaxpr/while
  349.3 5.8 copy-start.2
  349.3 5.8 copy-start.7
  349.3 5.8 copy-start.70
  349.3 5.8 copy-start.44
  365.2 128.8 %copy-start.11 = (f32[1024,768]{0,1:T(8,128)}, f32[1024,768]{0,1:T(8,128)S(1)}, u32[]{:S(2)}) copy-start(f32[1024,768]{0,1:T(8,128)S(1)} %get-tuple-element.656) | copy-start | bytes 9437188
  365.3 112.5 %copy-start.93 = (f32[1024]{0:T(1024)}, f32[1024]{0:T(1024)S(1)}, u32[]{:S(2)}) copy-start(f32[1024]{0:T(1024)S(1)} %broadcast_multiply_fusion.11) | copy-start | bytes 12292
  365.3 128.8 %copy-start.74 = (f32[1024]{0:T(1024)}, f32[1024]{0:T(1024)S(1)}, u32[]{:S(2)}) copy-start(f32[1024]{0:T(1024)S(1)} %broadcast_multiply_fusion.9) | copy-start | bytes 12292
  366.9 127.2 %copy-start.78 = (f32[1024]{0:T(1024)}, f32[1024]{0:T(1024)S(1)}, u32[]{:S(2)}) copy-start(f32[1024]{0:T(1024)S(1)} %add_rsqrt_fusion.1) | copy-start | bytes 12292
  366.9 110.8 %copy-start.109 = (f32[1024]{0:T(1024)}, f32[1024]{0:T(1024)S(1)}, u32[]{:S(2)}) copy-start(f32[1024]{0:T(1024)S(1)} %add_rsqrt_fusion.3) | copy-start | bytes 12292
  367.0 12.5 copy-start.97
  367.0 12.4 copy-start.29
  367.0 12.4 copy-start.46
  393.0 9.9 copy-start.95
  418.7 11.3 copy-start.26
  418.7 11.3 copy-start.27
  430.0 20.1 %slice-start = ((s8[4718592]{0:T(1024)(128)(4,1)}), s8[4194304]{0:T(1024)(128)(4,1)S(1)}, s32[]{:S(2)}) async-start(s8[4718592]{0:T(1024)(128)(4,1)} %bitcast.322), calls=%async_computation.18 | async-start | bytes 8388608
  435.1 15.0 %copy-start.62 = (bf16[1024,768]{0,1:T(8,128)(2,1)}, bf16[1024,768]{0,1:T(8,128)(2,1)S(1)}, u32[]{:S(2)}) copy-start(bf16[1024,768]{0,1:T(8,128)(2,1)S(1)} %get-tuple-element.606) | copy-start | bytes 4718596
  435.1 15.0 %copy-start.30 = (f32[1024,768]{0,1:T(8,128)S(1)}, f32[1024,768]{0,1:T(8,128)}, u32[]{:S(2)}) copy-start(f32[1024,768]{0,1:T(8,128)} %copy-done.28) | copy-start | bytes 9437188
  435.1 15.0 %slice-start.1 = ((s8[4718592]{0:T(1024)(128)(4,1)}), s8[524288]{0:T(1024)(128)(4,1)S(1)}, s32[]{:S(2)}) async-start(s8[4718592]{0:T(1024)(128)(4,1)} %bitcast.322), calls=%async_computation.19 | async-start | bytes 1048576
  462.8 14.9 %copy-start.56 = (bf16[1024,768]{0,1:T(8,128)(2,1)}, bf16[1024,768]{0,1:T(8,128)(2,1)S(1)}, u32[]{:S(2)}) copy-start(bf16[1024,768]{0,1:T(8,128)(2,1)S(1)} %get-tuple-element.604) | copy-start | bytes 4718596
  477.7 13.0 copy-start.43
  500.5 5.9 copy-start.5
  500.5 5.9 copy-start.69
  500.5 5.9 copy-start.73
  500.5 519.4 %reduce-scatter.23.cloned.1.call-start = ((), (), s32[]{:S(2)}) async-start(), calls=%async_computation.17 | async-start | bytes 2433024
  510.5 11.7 copy-start.34
  575.8 9.6 copy-start.10
  597.6 11.4 copy-start.34
  662.4 9.5 copy-start.10
  681.6 6.3 copy-start.3
  681.6 6.3 copy-start.67
  681.6 6.3 copy-start.71
  691.5 11.4 copy-start.33
  755.4 9.5 copy-start.8
  777.2 11.4 copy-start.33
  842.1 9.6 copy-start.8
  874.5 202.6 %reduce-scatter.19.cloned.1.call-start = ((), (), s32[]{:S(2)}) async-start(), calls=%async_computation.15 | async-start | bytes 2433024
  883.9 297.8 %reduce-scatter.21.cloned.1.call-start = ((), (), s32[]{:S(2)}) async-start(), calls=%async_computation.16 | async-start | bytes 2433024
  894.8 8.7 copy-start.12
  894.8 8.7 copy-start.75
  894.8 8.7 copy-start.79
  894.8 428.1 %reduce-scatter.15.cloned.1.call-start = ((), (), s32[]{:S(2)}) async-start(), calls=%async_computation.13 | async-start | bytes 9732096 | tf_op jit(solution)/shard_map/reduce_scatter | solution.py:433
  914.2 8.7 copy-start.57
  914.2 550.7 %reduce-scatter.17.cloned.1.call-start = ((), (), s32[]{:S(2)}) async-start(), calls=%async_computation.14 | async-start | bytes 9732096 | tf_op jit(solution)/shard_map/reduce_scatter | solution.py:435
  937.2 5.2 copy-start.23
  (75 other events, 182.9 us)
Sparse Core Ops, SparseCore 0:
  10.8 56.9 all-gather.8
  70.7 52.9 all-gather.10
  126.4 53.0 all-gather.6
  182.1 53.0 all-gather.12
  237.9 62.5 all-gather.14
  303.1 62.3 all-gather.16
  500.6 98.1 reduce-scatter.12
  874.6 98.4 reduce-scatter.22
  979.0 98.0 reduce-scatter.18
  1083.7 97.9 reduce-scatter.20
  1188.1 134.6 reduce-scatter.14
  1330.2 134.5 reduce-scatter.16
where the time goes:
time: 1480 us; the launch traced here: 1470 us
  waiting for transfers between devices  542 us (37%)
  matrix products  521 us (35%)
  other arithmetic  187 us (13%)
  local copies, waits for them, and re-layouts  98.8 us (7%)
  blocking collectives  83.7 us (6%)
  loops' own time  22.6 us (2%)
  between operations  17.2 us (1%)
    unnamed x15, waiting for transfers between devices  166 us
    reduce_scatter x1, waiting for transfers between devices, per_device(): lax.psum_scatter(totals[11], ('dp', 'fsdp'), scatter_dimension=0, tiled=T...  142 us
    reduce_scatter x1, waiting for transfers between devices, per_device(): lax.psum_scatter(totals[9], ('dp', 'fsdp'), scatter_dimension=0, tiled=True)  141 us
    dot_general x8, matrix products, block_scores(): jnp.einsum('qhd,khd->hqk', queries, key_rows, preferred_element_type=jnp....  88.3 us
    convert_element_type x4, other arithmetic, one_block(): score_low = (probs * (prob_grad - inner_sum)).astype(jnp.bfloat16)  85.4 us
    unnamed x2, blocking collectives  83.7 us
    dot_general x12, matrix products, times_transposed(): lax.dot_general(left, right, (((1,), (1,)), ((), ())), preferred_element_...  73.6 us
    dot_general x4, matrix products, one_block(): jnp.einsum('qhd,khd->hqk', grad_block, value_rows, preferred_element_type...  72.3 us
  transfers between devices with their start and end apart: 12, of which 6 were waited for; matrix products, arithmetic and copies ran while one was open for 46% of the time, Pallas kernels for 0%

commit v1 on v0

v1 whole, which is shorter than its diff:
```python
import functools

import jax
import jax.numpy as jnp
from jax import lax
from jax.experimental import pallas as pl
from jax.experimental.pallas import tpu as pltpu
from jax.sharding import PartitionSpec as P

HEAD_DIM = 64
LEN = 1024
DOCS = 8
EPSILON = 1e-12
NEGATIVE = -1e30
ROOT_HALF = 0.7071067811865476
INV_ROOT_TWO_PI = 0.3989422804014327
AXES = ("dp", "fsdp")
F32 = jnp.float32
BF16 = jnp.bfloat16

GROUP = 256
HEADS_IN = GROUP // HEAD_DIM
TRIPLE = 3 * GROUP
QB = 256
CHUNK = 256
VEC = 128


def dot(left, right, left_dim=1, right_dim=0):
    return lax.dot_general(
        left, right, (((left_dim,), (right_dim,)), ((), ())), preferred_element_type=F32
    )


def head_masks():
    lane = lax.broadcasted_iota(jnp.int32, (1, GROUP), 1) // HEAD_DIM
    return [lane == h for h in range(HEADS_IN)]


def segments(doc_lengths, pad_tail):
    ends = jnp.cumsum(doc_lengths, axis=1)
    limit = (LEN - pad_tail)[:, None]
    places = jnp.arange(LEN, dtype=jnp.int32)
    segment = jnp.sum((places[None, :, None] >= ends[:, None, :]).astype(jnp.int32), axis=2)
    segment = jnp.where(places[None] < limit, segment, DOCS)
    borders = jnp.concatenate(
        [jnp.zeros_like(limit), jnp.minimum(ends, limit), limit, jnp.full_like(limit, LEN)], axis=1
    )[:, None, :]
    first = (jnp.arange(LEN // QB, dtype=jnp.int32) * QB)[None, :, None]
    low = jnp.max(jnp.where(borders <= first, borders, 0), axis=2)
    high = jnp.min(jnp.where(borders > first + QB - 1, borders, LEN), axis=2)
    low = (low // 128) * 128
    count = (high - low + CHUNK - 1) // CHUNK
    low = jnp.minimum(low, LEN - CHUNK * count)
    return segment, low.astype(jnp.int32), count.astype(jnp.int32)


def forward_kernel(
    low_ref, count_ref, rows_ref, w_ref, bias_ref, segc_ref, segr_ref,
    qkv_ref, mixed_ref, lse_ref, keyt_ref,
):
    s = pl.program_id(0)
    qkv_ref[...] = (dot(rows_ref[...], w_ref[...]) + bias_ref[0:1, :]).astype(BF16)
    keyt_ref[...] = qkv_ref[:, GROUP : 2 * GROUP].T
    masks = head_masks()

    def block(i, carry):
        start = pl.multiple_of(i * QB, QB)
        queries = qkv_ref[pl.ds(start, QB), :GROUP] * BF16(HEAD_DIM**-0.5)
        zero = jnp.zeros_like(queries)
        own = segc_ref[pl.ds(start, QB), :][:, :1]
        low = pl.multiple_of(low_ref[s, i], 128)
        count = count_ref[s, i]
        for c in range(1, LEN // CHUNK + 1):

            @pl.when(count == c)
            def _():
                span = pl.ds(low, CHUNK * c)
                keys = keyt_ref[:, span]
                values = qkv_ref[span, 2 * GROUP :]
                allowed = own == segr_ref[0:1, span]
                lane = lax.broadcasted_iota(jnp.int32, (QB, 128), 1)
                mixed = None
                for h in range(HEADS_IN):
                    scores = dot(jnp.where(masks[h], queries, zero), keys)
                    scores = jnp.where(allowed, scores, NEGATIVE)
                    top = jnp.max(scores, axis=1, keepdims=True)
                    expo = jnp.exp(scores - top)
                    total = jnp.sum(expo, axis=1, keepdims=True)
                    part = dot(expo.astype(BF16), values) * (1.0 / total)
                    logsum = top + jnp.log(total)
                    if h == 0:
                        mixed, sums = part, jnp.broadcast_to(logsum, (QB, 128))
                    else:
                        mixed, sums = jnp.where(masks[h], part, mixed), jnp.where(lane == h, logsum, sums)
                mixed_ref[pl.ds(start, QB), :] = mixed.astype(BF16)
                lse_ref[:, pl.ds(start, QB)] = sums.T[:8]

        return carry

    lax.fori_loop(0, LEN // QB, block, 0)


def attention_forward(rows, w, bias, segc, segr, low, count):
    seqs, _, width = rows.shape
    groups = width // GROUP
    return pl.pallas_call(
        forward_kernel,
        grid_spec=pltpu.PrefetchScalarGridSpec(
            num_scalar_prefetch=2,
            grid=(seqs, groups),
            in_specs=[
                pl.BlockSpec((None, LEN, width), lambda s, g, *_: (s, 0, 0)),
                pl.BlockSpec((width, TRIPLE), lambda s, g, *_: (0, g)),
                pl.BlockSpec((8, TRIPLE), lambda s, g, *_: (0, g)),
                pl.BlockSpec((None, LEN, 128), lambda s, g, *_: (s, 0, 0)),
                pl.BlockSpec((None, 8, LEN), lambda s, g, *_: (s, 0, 0)),
            ],
            out_specs=[
                pl.BlockSpec((None, LEN, TRIPLE), lambda s, g, *_: (s, 0, g)),
                pl.BlockSpec((None, LEN, GROUP), lambda s, g, *_: (s, 0, g)),
                pl.BlockSpec((None, None, 8, LEN), lambda s, g, *_: (s, g, 0, 0)),
            ],
            scratch_shapes=[pltpu.VMEM((GROUP, LEN), BF16)],
        ),
        out_shape=[
            jax.ShapeDtypeStruct((seqs, LEN, 3 * width), BF16),
            jax.ShapeDtypeStruct((seqs, LEN, width), BF16),
            jax.ShapeDtypeStruct((seqs, groups, 8, LEN), F32),
        ],
        compiler_params=pltpu.CompilerParams(vmem_limit_bytes=48 * 2**20),
        name="attention_forward",
    )(low, count, rows, w, bias, segc, segr)


def backward_kernel(
    low_ref, count_ref, qkv_ref, mixed_ref, grad_ref, rowst_ref, lse_ref, segc_ref, segr_ref,
    dqkv_ref, dw_ref, sums_ref,
    q_ref, qt_ref, gt_ref, kt_ref, dqt_ref, acc_ref, delta_ref,
):
    s = pl.program_id(1)
    masks = head_masks()
    grad = grad_ref[...]
    prod = grad.astype(F32) * mixed_ref[...].astype(F32)
    coarse = prod.astype(BF16)
    fine = (prod - coarse.astype(F32)).astype(BF16)
    pick = lax.broadcasted_iota(jnp.int32, (8, GROUP), 1) // HEAD_DIM
    pick = (pick == lax.broadcasted_iota(jnp.int32, (8, GROUP), 0)).astype(F32).astype(BF16)
    delta_ref[...] = dot(pick, coarse, 1, 1) + dot(pick, fine, 1, 1)
    queries = qkv_ref[:, :GROUP] * BF16(HEAD_DIM**-0.5)
    q_ref[...] = queries
    qt_ref[...] = queries.T
    gt_ref[...] = grad.T
    kt_ref[...] = qkv_ref[:, GROUP : 2 * GROUP].T
    dqt_ref[...] = jnp.zeros_like(dqt_ref)

    def block(i, carry):
        start = pl.multiple_of(i * QB, QB)
        mine = pl.ds(start, QB)
        keys = qkv_ref[mine, GROUP : 2 * GROUP]
        values = qkv_ref[mine, 2 * GROUP :]
        zero = jnp.zeros_like(keys)
        own = segc_ref[mine, :][:, :1]
        low = pl.multiple_of(low_ref[s, i], 128)
        count = count_ref[s, i]
        for c in range(1, LEN // CHUNK + 1):

            @pl.when(count == c)
            def _():
                span = pl.ds(low, CHUNK * c)
                allowed = own == segr_ref[0:1, span]
                dkey = dvalue = None
                for h in range(HEADS_IN):
                    scores = dot(jnp.where(masks[h], keys, zero), qt_ref[:, span])
                    probs = jnp.exp(jnp.where(allowed, scores, NEGATIVE) - lse_ref[h : h + 1, span])
                    pgrad = dot(jnp.where(masks[h], values, zero), gt_ref[:, span])
                    low_score = (probs * (pgrad - delta_ref[h : h + 1, span])).astype(BF16)
                    v_part = dot(probs.astype(BF16), grad_ref[span, :])
                    k_part = dot(low_score, q_ref[span, :])
                    head = slice(h * HEAD_DIM, (h + 1) * HEAD_DIM)
                    dqt_ref[head, span] += dot(kt_ref[head, mine], low_score)
                    if h == 0:
                        dkey, dvalue = k_part, v_part
                    else:
                        dkey, dvalue = jnp.where(masks[h], k_part, dkey), jnp.where(masks[h], v_part, dvalue)
                dqkv_ref[mine, GROUP : 2 * GROUP] = dkey.astype(BF16)
                dqkv_ref[mine, 2 * GROUP :] = dvalue.astype(BF16)

        return carry

    lax.fori_loop(0, LEN // QB, block, 0)
    dqkv_ref[:, :GROUP] = (dqt_ref[...] * HEAD_DIM**-0.5).astype(BF16).T
    dqkv = dqkv_ref[...]
    dw = dot(rowst_ref[...], dqkv)
    sums = jnp.broadcast_to(jnp.sum(dqkv.astype(F32), axis=0, keepdims=True), sums_ref.shape)

    @pl.when(s == 0)
    def _():
        acc_ref[...] = dw
        sums_ref[...] = sums

    @pl.when(s > 0)
    def _():
        acc_ref[...] += dw
        sums_ref[...] += sums

    @pl.when(s == pl.num_programs(1) - 1)
    def _():
        dw_ref[...] = acc_ref[...].astype(BF16)


def attention_backward(qkv, mixed, grad, rowst, lse, segc, segr, low, count):
    seqs, _, width = mixed.shape
    groups = width // GROUP
    return pl.pallas_call(
        backward_kernel,
        grid_spec=pltpu.PrefetchScalarGridSpec(
            num_scalar_prefetch=2,
            grid=(groups, seqs),
            in_specs=[
                pl.BlockSpec((None, LEN, TRIPLE), lambda g, s, *_: (s, 0, g)),
                pl.BlockSpec((None, LEN, GROUP), lambda g, s, *_: (s, 0, g)),
                pl.BlockSpec((None, LEN, GROUP), lambda g, s, *_: (s, 0, g)),
                pl.BlockSpec((None, width, LEN), lambda g, s, *_: (s, 0, 0)),
                pl.BlockSpec((None, None, 8, LEN), lambda g, s, *_: (s, g, 0, 0)),
                pl.BlockSpec((None, LEN, 128), lambda g, s, *_: (s, 0, 0)),
                pl.BlockSpec((None, 8, LEN), lambda g, s, *_: (s, 0, 0)),
            ],
            out_specs=[
                pl.BlockSpec((None, LEN, TRIPLE), lambda g, s, *_: (s, 0, g)),
                pl.BlockSpec((width, TRIPLE), lambda g, s, *_: (0, g)),
                pl.BlockSpec((8, TRIPLE), lambda g, s, *_: (0, g)),
            ],
            scratch_shapes=[
                pltpu.VMEM((LEN, GROUP), BF16),
                pltpu.VMEM((GROUP, LEN), BF16),
                pltpu.VMEM((GROUP, LEN), BF16),
                pltpu.VMEM((GROUP, LEN), BF16),
                pltpu.VMEM((GROUP, LEN), F32),
                pltpu.VMEM((width, TRIPLE), F32),
                pltpu.VMEM((8, LEN), F32),
            ],
        ),
        out_shape=[
            jax.ShapeDtypeStruct((seqs, LEN, 3 * width), BF16),
            jax.ShapeDtypeStruct((width, 3 * width), BF16),
            jax.ShapeDtypeStruct((8, 3 * width), F32),
        ],
        compiler_params=pltpu.CompilerParams(vmem_limit_bytes=48 * 2**20),
        name="attention_backward",
    )(low, count, qkv, mixed, grad, rowst, lse, segc, segr)


def middle_kernel(
    parts, width, tokens,
    pad_ref, mixed_ref, rows_ref, cot_ref, w_ref, vec_ref,
    out_ref, res_ref, mgrad_ref, dw_ref, sums_ref, stats_ref,
    hidden_ref, slope_ref, first_ref, normed_ref, upper_ref, wide_ref, acc_ref, stage_ref, sem,
):
    i = pl.program_id(0)
    per_seq = LEN // tokens

    @pl.when(i == 0)
    def _():
        acc_ref[...] = jnp.zeros_like(acc_ref)
        sums_ref[...] = jnp.zeros_like(sums_ref)
        stats_ref[...] = jnp.zeros_like(stats_ref)

    def weight(k):
        if isinstance(k, int):
            return w_ref[:, k * width : (k + 1) * width]
        return w_ref[:, pl.ds(pl.multiple_of(k * width, width), width)]

    def vector(row):
        return vec_ref[row : row + 1, :]

    def add_sum(row, values):
        sums_ref[row : row + 1, :] += jnp.sum(values, axis=0, keepdims=True)

    place = (i % per_seq) * tokens + lax.broadcasted_iota(jnp.int32, (tokens, 1), 0)
    valid = (place < LEN - pad_ref[i // per_seq]).astype(F32)

    def add_stat(row, values):
        stats_ref[row : row + 1, :] += jnp.sum(valid * values * values, axis=0, keepdims=True)

    def mean(values):
        return jnp.mean(values, axis=1, keepdims=True)

    def normed_of(values):
        centred = values - mean(values)
        inverse = lax.rsqrt(mean(centred * centred) + EPSILON)
        return centred * inverse, inverse

    def norm_backward(scaled, normed, inverse):
        return inverse * (scaled - mean(scaled) - normed * mean(scaled * normed))

    rows = rows_ref[...].astype(F32)
    branch = dot(mixed_ref[...], weight(0)) + vector(0)
    add_stat(0, rows)
    add_stat(1, branch)
    first_normed, first_inverse = normed_of(rows + branch)
    normed_ref[...] = first_normed
    first = first_normed * vector(1) + vector(2)
    first_ref[...] = first.astype(BF16)
    wide_ref[...] = jnp.zeros_like(wide_ref)

    def feed(j, carry):
        inner = dot(first_ref[...], weight(1 + j)) + vec_ref[pl.ds(6 + j, 1), :]
        half = 0.5 * (1.0 + lax.erf(inner * ROOT_HALF))
        hidden = (inner * half).astype(BF16)
        hidden_ref[j] = hidden
        slope_ref[j] = (half + inner * jnp.exp(-0.5 * inner * inner) * INV_ROOT_TWO_PI).astype(BF16)
        wide_ref[...] += dot(hidden, weight(1 + parts + j))
        return carry

    lax.fori_loop(0, parts, feed, 0)
    second = wide_ref[...] + vector(3)
    add_stat(2, second)
    second_normed, second_inverse = normed_of(first + second)
    result = second_normed * vector(4) + vector(5)
    add_stat(3, result)
    out_ref[...] = result.astype(BF16)
    upstream = cot_ref[...].astype(F32) * valid
    add_sum(0, upstream * second_normed)
    add_sum(1, upstream)
    upper = norm_backward(upstream * vector(4), second_normed, second_inverse)
    upper_low = upper.astype(BF16)
    upper_ref[...] = upper_low
    add_sum(2, upper_low.astype(F32))
    wide_ref[...] = upper
    upper_t = upper_low.T
    first_t = first_ref[...].T

    def back(j, carry):
        acc_ref[1 + parts + j] += dot(upper_t, hidden_ref[j])
        inner_low = (dot(upper_ref[...], weight(1 + parts + j), 1, 1) * slope_ref[j].astype(F32)).astype(BF16)
        sums_ref[pl.ds(8 + j, 1), :] += jnp.sum(inner_low.astype(F32), axis=0, keepdims=True)
        acc_ref[1 + j] += dot(first_t, inner_low)
        wide_ref[...] += dot(inner_low, weight(1 + j), 1, 1)
        return carry

    lax.fori_loop(0, parts, back, 0)
    first_grad = wide_ref[...]
    first_normed = normed_ref[...]
    add_sum(3, first_grad * first_normed)
    add_sum(4, first_grad)
    residual = norm_backward(first_grad * vector(1), first_normed, first_inverse)
    res_ref[...] = residual
    branch_low = residual.astype(BF16)
    add_sum(5, branch_low.astype(F32))
    acc_ref[0] += dot(mixed_ref[...], branch_low, 0, 0)
    mgrad_ref[...] = dot(branch_low, weight(0), 1, 1).astype(BF16)

    @pl.when(i == pl.num_programs(0) - 1)
    def _():
        def copy(k, slot):
            columns = pl.ds(pl.multiple_of(k * width, width), width)
            return pltpu.make_async_copy(stage_ref.at[slot], dw_ref.at[:, columns], sem.at[slot])

        def flush(k, carry):
            slot = lax.rem(k, 2)

            @pl.when(k >= 2)
            def _():
                copy(k - 2, slot).wait()

            @pl.when(k > parts)
            def _():
                stage_ref[slot] = acc_ref[k].astype(BF16).T

            @pl.when(k <= parts)
            def _():
                stage_ref[slot] = acc_ref[k].astype(BF16)

            copy(k, slot).start()
            return carry

        lax.fori_loop(0, 1 + 2 * parts, flush, 0)
        copy(2 * parts - 1, (2 * parts - 1) % 2).wait()
        copy(2 * parts, (2 * parts) % 2).wait()


def middle(mixed, rows, cotangent, w, vec, pad):
    count, width = mixed.shape
    tokens = 256
    parts = (w.shape[1] // width - 1) // 2
    block = pl.BlockSpec((tokens, width), lambda i, *_: (i, 0))
    return pl.pallas_call(
        functools.partial(middle_kernel, parts, width, tokens),
        grid_spec=pltpu.PrefetchScalarGridSpec(
            num_scalar_prefetch=1,
            grid=(count // tokens,),
            in_specs=[
                block,
                block,
                block,
                pl.BlockSpec(w.shape, lambda i, *_: (0, 0), pipeline_mode=pl.Buffered(1)),
                pl.BlockSpec(vec.shape, lambda i, *_: (0, 0)),
            ],
            out_specs=[
                block,
                block,
                block,
                pl.BlockSpec(memory_space=pl.ANY),
                pl.BlockSpec((16, width), lambda i, *_: (0, 0)),
                pl.BlockSpec((8, width), lambda i, *_: (0, 0)),
            ],
            scratch_shapes=[
                pltpu.VMEM((parts, tokens, width), BF16),
                pltpu.VMEM((parts, tokens, width), BF16),
                pltpu.VMEM((tokens, width), BF16),
                pltpu.VMEM((tokens, width), F32),
                pltpu.VMEM((tokens, width), BF16),
                pltpu.VMEM((tokens, width), F32),
                pltpu.VMEM((1 + 2 * parts, width, width), F32),
                pltpu.VMEM((2, width, width), BF16),
                pltpu.SemaphoreType.DMA((2,)),
            ],
        ),
        out_shape=[
            jax.ShapeDtypeStruct((count, width), BF16),
            jax.ShapeDtypeStruct((count, width), F32),
            jax.ShapeDtypeStruct((count, width), BF16),
            jax.ShapeDtypeStruct((width, (1 + 2 * parts) * width), BF16),
            jax.ShapeDtypeStruct((16, width), F32),
            jax.ShapeDtypeStruct((8, width), F32),
        ],
        compiler_params=pltpu.CompilerParams(vmem_limit_bytes=60 * 2**20),
        name="middle",
    )(pad, mixed, rows, cotangent, w, vec)


def gather(shard):
    return lax.all_gather(shard, AXES, axis=0, tiled=True)


def scatter(partial):
    partial = lax.psum_scatter(partial, "dp", scatter_dimension=0, tiled=True)
    return lax.psum_scatter(partial, "fsdp", scatter_dimension=0, tiled=True)


def total_over_devices(values):
    for axis in AXES:
        size = lax.axis_size(axis)
        step = 1
        while step < size:
            values = values + lax.ppermute(values, axis, [(d, d ^ step) for d in range(size)])
            step *= 2
    return values


def per_device(
    layer_input, cotangent, doc_lengths, pad_tail,
    query_weight, query_bias, key_weight, value_weight, value_bias,
    merge_weight, merge_bias, first_gain, first_shift,
    inner_weight, inner_bias, outer_weight, outer_bias, second_gain, second_shift,
):
    seqs, _, width = layer_input.shape
    own = query_weight.shape[0]
    devices = width // own
    parts = inner_weight.shape[1] // width
    groups = width // GROUP

    vectors = [query_bias, value_bias, merge_bias, first_gain, first_shift, outer_bias, second_gain, second_shift]
    columns = jnp.concatenate([jnp.stack(vectors), inner_bias.reshape(parts, own)]).T
    columns = jnp.pad(columns, ((0, 0), (0, VEC - columns.shape[1])))
    triples = [
        mat[:, g * GROUP : (g + 1) * GROUP]
        for g in range(groups)
        for mat in (query_weight, key_weight, value_weight)
    ]
    near = gather(jnp.concatenate(triples + [columns], axis=1))
    inner_own = inner_weight.reshape(own, devices, parts, own).transpose(0, 2, 1, 3).reshape(own, parts * width)
    outer_own = outer_weight.reshape(parts, own, width).transpose(1, 0, 2).reshape(own, parts * width)
    far = gather(jnp.concatenate([merge_weight, inner_own, outer_own], axis=1))

    segment, low, count = segments(doc_lengths, pad_tail)
    segc = jnp.broadcast_to(segment[:, :, None], (seqs, LEN, 128))
    segr = jnp.broadcast_to(segment[:, None, :], (seqs, 8, LEN))
    rowst = jnp.swapaxes(layer_input, 1, 2)

    vec_rows = near[:, 3 * width :].T.astype(F32)
    bias = jnp.stack([vec_rows[0], jnp.zeros((width,), F32), vec_rows[1]])
    bias = bias.reshape(3, groups, GROUP).transpose(1, 0, 2).reshape(1, 3 * width)
    bias = jnp.broadcast_to(bias, (8, 3 * width))
    vec = vec_rows[2:18]

    qkv, mixed, lse = attention_forward(layer_input, near, bias, segc, segr, low, count)
    tokens = seqs * LEN
    output, residual, mixed_grad, far_partial, sums, stats = middle(
        mixed.reshape(tokens, width), layer_input.reshape(tokens, width), cotangent.reshape(tokens, width), far, vec, pad_tail
    )
    far_grad = scatter(far_partial)
    dqkv, near_partial, near_sums = attention_backward(
        qkv, mixed, mixed_grad.reshape(mixed.shape), rowst, lse, segc, segr, low, count
    )
    valid_count = jnp.sum(LEN - pad_tail).astype(F32)
    stat_row = jnp.concatenate([jnp.sum(stats[:4], axis=1), valid_count[None], jnp.zeros((width - 5,), F32)])
    totals = total_over_devices(jnp.concatenate([sums[:6], sums[8 : 8 + parts], stat_row[None]]))

    near_rows = near_sums[0].reshape(groups, 3, GROUP)
    near_cols = jnp.stack([near_rows[:, 0].reshape(width), near_rows[:, 2].reshape(width)])
    near_cols = jnp.pad(near_cols.T, ((0, 0), (0, VEC - 2))).astype(BF16)
    near_grad = scatter(jnp.concatenate([near_partial, near_cols], axis=1)).astype(F32)
    input_gradient = residual + dot(dqkv.reshape(tokens, 3 * width), near[:, : 3 * width], 1, 1)

    which = lax.axis_index(AXES)
    mine = lax.dynamic_slice_in_dim(totals[: 6 + parts], which * own, own, axis=1)
    inner_bias_gradient = mine[6:].reshape(parts * own)
    triple = near_grad[:, : 3 * width].reshape(own, groups, 3, GROUP)
    query_grad, key_grad, value_grad = (triple[:, :, k].reshape(own, width) for k in range(3))
    far_grad = far_grad.astype(F32)
    inner_grad = far_grad[:, width : (1 + parts) * width]
    inner_grad = inner_grad.reshape(own, parts, devices, own).transpose(0, 2, 1, 3).reshape(own, parts * width)
    outer_grad = far_grad[:, (1 + parts) * width :].reshape(own, parts, width).transpose(1, 0, 2)
    all_tokens = tokens * devices
    valid_total = totals[6 + parts, 4]
    share = jnp.reshape(valid_total / all_tokens, (1,))
    layer_stats = jnp.concatenate([share, jnp.sqrt(totals[6 + parts, :4] / (valid_total * width))])
    return (
        output.reshape(layer_input.shape),
        input_gradient.reshape(layer_input.shape),
        query_grad,
        near_grad[:, 3 * width],
        key_grad,
        value_grad,
        near_grad[:, 3 * width + 1],
        far_grad[:, :width],
        mine[5],
        mine[3],
        mine[4],
        inner_grad,
        inner_bias_gradient,
        outer_grad.reshape(parts * own, width),
        mine[2],
        mine[0],
        mine[1],
        layer_stats,
    )


def solution(mesh):
    matrix, vector, cube = P(AXES, None), P(AXES), P(AXES, None, None)
    in_specs = (
        cube, cube, matrix, vector,
        matrix, vector, matrix, matrix, vector,
        matrix, vector, vector, vector,
        matrix, vector, matrix, vector, vector, vector,
    )
    out_specs = (
        cube, cube,
        matrix, vector, matrix, matrix, vector,
        matrix, vector, vector, vector,
        matrix, vector, matrix, vector, vector, vector,
        P(),
    )
    return jax.shard_map(per_device, mesh=mesh, in_specs=in_specs, out_specs=out_specs, check_vma=False)
```

time: 1480 us -> 576 us (0.39)
  matrix products: 521 us -> 14 us
  waiting for transfers between devices: 542 us -> 245 us
  Pallas kernels: 0 us -> 244 us
  other arithmetic: 187 us -> 8.17 us
  blocking collectives: 83.7 us -> 0 us
  local copies, waits for them, and re-layouts: 98.8 us -> 40.4 us
  loops' own time: 22.6 us -> 0 us
    dot_general x64 -> x1, matrix products: 521 us -> 14 us  [dot(): lax.dot_general(left, right, (((left_dim,), (right_dim,)), ((), ())), pre...]
    pallas_call x0 -> x3, Pallas kernels: none -> 244 us  [the longest x1 122 us: middle(): pl.pallas_call(functools.partial(middle_kernel, parts, width, tokens), gr...]
    unnamed x15 -> x7, waiting for transfers between devices: 166 us -> 6.12 us
    reduce_scatter x3, waiting for transfers between devices: 283 us -> 144 us  [the longest x2 117 us: scatter(): partial = lax.psum_scatter(partial, 'dp', scatter_dimension=0, tiled=True)]
    convert_element_type x16 -> x2, other arithmetic: 92.9 us -> 0.94 us  [the longest x1 0.92 us: per_device(): scatter(jnp.concatenate([near_partial, near_cols], axis=1)).astype(F32)]
    unnamed x2 -> x0, blocking collectives: 83.7 us -> none
    reduce_sum x17 -> x3, other arithmetic: 78 us -> 0.85 us  [the longest x1 0.63 us: per_device(): valid_count = jnp.sum(LEN - pad_tail).astype(F32)]
    unnamed x262 -> x40, local copies, waits for them, and re-layouts: 61.4 us -> 16.5 us
  transfers between devices with their start and end apart: 12 -> 11, of which waited for: 6 -> 10; matrix products, arithmetic and copies ran while one was open for 46% -> 6% of each run, Pallas kernels for 0% -> 9%
where the time goes in v1:
time: 576 us; the launch traced here: 575 us
  waiting for transfers between devices  245 us (43%)
  Pallas kernels  244 us (42%)
  local copies, waits for them, and re-layouts  40.4 us (7%)
  between operations  16.4 us (3%)
  matrix products  14 us (2%)
  other arithmetic  8.17 us (1%)
  starting transfers between devices  7.69 us (1%)
    pallas_call x1, Pallas kernels, middle(): pl.pallas_call(functools.partial(middle_kernel, parts, width, tokens), gr...  122 us
    reduce_scatter x2, waiting for transfers between devices, scatter(): partial = lax.psum_scatter(partial, 'dp', scatter_dimension=0, tiled=True)  117 us
    all_gather x2, waiting for transfers between devices, gather(): return lax.all_gather(shard, AXES, axis=0, tiled=True)  85 us
    pallas_call x1, Pallas kernels, attention_backward(): pl.pallas_call(backward_kernel, grid_spec=pltpu.PrefetchScalarGridSpec(nu...  71.9 us
    pallas_call x1, Pallas kernels, attention_forward(): pl.pallas_call(forward_kernel, grid_spec=pltpu.PrefetchScalarGridSpec(num...  50.1 us
    reduce_scatter x1, waiting for transfers between devices, scatter(): return lax.psum_scatter(partial, 'fsdp', scatter_dimension=0, tiled=True)  27.3 us
    unnamed x40, local copies, waits for them, and re-layouts  16.5 us
    dot_general x1, matrix products, dot(): lax.dot_general(left, right, (((left_dim,), (right_dim,)), ((), ())), pre...  14 us
  transfers between devices with their start and end apart: 11, of which 10 were waited for; matrix products, arithmetic and copies ran while one was open for 6% of the time, Pallas kernels for 9%

profile of v1, /device:TPU:0, one launch (start us, length us, event | category | flops | bytes accessed | tf_op | source)
XLA Modules:
  0.0 575.5 jit_solution(9513572749258454167)
XLA Ops:
  7.3 0.9 constant_dynamic-update-slice_fusion.9
  8.2 0.8 constant_dynamic-update-slice_fusion.8
  9.0 0.7 constant_dynamic-update-slice_fusion.7
  9.7 0.7 constant_dynamic-update-slice_fusion.6
  10.4 0.7 constant_dynamic-update-slice_fusion.5
  11.1 0.7 constant_dynamic-update-slice_fusion.4
  11.8 0.7 constant_dynamic-update-slice_fusion.3
  12.5 0.7 constant_dynamic-update-slice_fusion.2
  13.2 0.7 constant_dynamic-update-slice_fusion.1
  13.9 0.7 reshape.158
  14.7 0.8 concatenate.25
  15.6 0.6 copy-done.6
  16.3 3.0 reshape.163
  19.3 2.2 copy.90
  21.5 2.1 reshape.164
  23.8 0.7 pad_maximum_fusion
  24.6 0.6 fusion.10
  25.3 0.2 reduce_window_sum.11
  25.6 2.9 copy.92
  28.8 0.2 select_reduce_fusion
  29.1 50.8 %all-gather.3.cloned.1.call-done.w_ref = bf16[768,2432]{1,0:T(8,128)(2,1)} async-done(((bf16[24,2432]{1,0:T(8,128)(2,1)}), bf16[768,2432]{1,0:T(8,128)(2,1)}) %all-gather.3.cloned.1.call-update) | async-done | bytes 3735568 | tf_op jit(solution)/shard_map/all_gather | solution.py:434
  79.9 0.9 slice.158
  81.0 0.6 slice.161.vec_ref
  81.7 0.3 broadcast_in_dim.62.segc_ref
  82.1 50.1 %attention_forward.1 = (bf16[2,1024,2304]{2,1,0:T(8,128)(2,1)}, bf16[2,1024,768]{2,1,0:T(8,128)(2,1)S(1)}, f32[2,3,8,1024]{3,2,1,0:T(8,128)S(1)}) custom-call(s32[2,4]{1,0:T(2,128)S(1)} %get-tuple-element.49.low_ref, s32[2,4]{1,0:T(2,128)S(1)} %get-tuple-element.50.count_ref, bf16[2,1024,768]{2,1,0:T(8,128)(2,1)} %rows_ref.1, ...), custom_call_target="tpu_custom_call" | custom-call | tf_op jit(solution)/shard_map/attention_forward/pallas_call | solution.py:107
  132.1 1.9 copy-done
  134.1 1.0 copy-done.2
  135.0 34.2 %all-gather.5.cloned.1.call-done.w_ref = bf16[768,6912]{1,0:T(8,128)(2,1)} async-done(((bf16[24,6912]{1,0:T(8,128)(2,1)}), bf16[768,6912]{1,0:T(8,128)(2,1)}) %all-gather.5.cloned.1.call-update) | async-done | bytes 10616848 | tf_op jit(solution)/shard_map/all_gather | solution.py:434
  169.3 122.3 %middle.1 = (bf16[2048,768]{1,0:T(8,128)(2,1)}, f32[2048,768]{1,0:T(8,128)}, bf16[2048,768]{1,0:T(8,128)(2,1)}, bf16[768,6912]{1,0:T(8,128)(2,1)}, f32[16,768]{1,0:T(8,128)}, /*index=5*/f32[8,768]{1,0:T(8,128)}) custom-call(s32[2]{0:T(128)} %pad_ref.1, bf16[2048,768]{1,0:T(8,128)(2,1)} %bitcast.66, bf16[2048,768]{1,0:T(8,128)(2,1)} %bitcast.67, ...), custom_call_target="tpu_custom_call" | custom-call | tf_op jit(solution)/shard_map/middle/pallas_call | solution.py:388
  291.6 1.2 copy-done.3
  292.8 71.9 %attention_backward.1 = (bf16[2,1024,2304]{2,1,0:T(8,128)(2,1)}, bf16[768,2304]{1,0:T(8,128)(2,1)}, f32[8,2304]{1,0:T(8,128)S(1)}) custom-call(s32[2,4]{1,0:T(2,128)S(1)} %get-tuple-element.49.low_ref, s32[2,4]{1,0:T(2,128)S(1)} %get-tuple-element.50.count_ref, bf16[2,1024,2304]{2,1,0:T(8,128)(2,1)} %get-tuple-element.33.qkv_ref, ...), custom_call_target="tpu_custom_call" | custom-call | tf_op jit(solution)/shard_map/attention_backward/pallas_call | solution.py:215
  364.9 0.2 copy.95
  365.0 4.1 fusion.1
  369.3 0.5 reduce-scatter.9.cloned.1.call-update
  369.8 48.6 %reduce-scatter.7.cloned.1.call-done = bf16[96,2432]{1,0:T(8,128)(2,1)} async-done(((bf16[768,2432]{1,0:T(8,128)(2,1)}), bf16[96,2432]{1,0:T(8,128)(2,1)}) %reduce-scatter.7.cloned.1.call-update) | async-done | bytes 466960 | tf_op jit(solution)/shard_map/reduce_scatter | solution.py:438
  419.5 1.2 collective-permute-done
  420.8 1.5 collective-permute-start.1
  422.3 2.7 collective-permute-done.1
  424.9 1.5 collective-permute-start.2
  426.4 2.7 collective-permute-done.2
  429.1 1.5 collective-permute-start.3
  430.6 2.6 collective-permute-done.3
  433.3 2.9 collective-permute-start.4
  436.1 68.3 %reduce-scatter.9.cloned.1.call-done = bf16[96,6912]{1,0:T(8,128)(2,1)} async-done(((bf16[768,6912]{1,0:T(8,128)(2,1)}), bf16[96,6912]{1,0:T(8,128)(2,1)}) %reduce-scatter.9.cloned.1.call-update) | async-done | bytes 1327120 | tf_op jit(solution)/shard_map/reduce_scatter | solution.py:438
  504.5 14.0 %fusion.4 = f32[2048,768]{1,0:T(8,128)} fusion(f32[2048,768]{1,0:T(8,128)} %get-tuple-element.32, bf16[2048,2304]{1,0:T(8,128)(2,1)} %bitcast.99, bf16[768,2432]{1,0:T(8,128)(2,1)} %all-gather.3.cloned.1.call-done.w_ref), kind=kOutput, calls=%fused_computation.5 | convolution fusion | flops 7249330176 | bytes 25559040 | tf_op jit(solution)/shard_map/dot_general | solution.py:30
  518.5 0.6 slice.175
  520.4 0.6 reshape.174
  521.0 0.6 pad_maximum_fusion.5
  521.6 0.6 dynamic-slice_bitcast_fusion
  522.2 5.5 reduce-scatter.13.cloned.1.call-done
  527.8 0.9 slice.165
  528.8 0.6 slice_reduce_fusion
  529.5 0.6 copy.103
  530.1 0.6 copy.104
  530.8 0.6 copy.105
  531.4 0.9 convert_element_type.26
  532.3 0.7 slice_reduce_fusion.3
  533.0 27.3 %reduce-scatter.11.cloned.1.call-done = bf16[24,6912]{1,0:T(8,128)(2,1)} async-done(((bf16[96,6912]{1,0:T(8,128)(2,1)}), bf16[24,6912]{1,0:T(8,128)(2,1)}) %reduce-scatter.11.cloned.1.call-update) | async-done | bytes 331792 | tf_op jit(solution)/shard_map/reduce_scatter | solution.py:439
  560.3 1.0 fusion.14
  561.4 1.1 reshape.172
  562.5 1.2 copy.96
  563.8 2.6 reshape.173
  566.5 0.8 copy.97
  567.2 1.4 slice.171
  (74 shorter events, 2.2 us)
Async XLA Ops:
  7.2 16.5 %copy-start.5 = (bf16[96,768]{1,0:T(8,128)(2,1)S(1)}, bf16[96,768]{1,0:T(8,128)(2,1)}, u32[]{:S(2)}) copy-start(bf16[96,768]{1,0:T(8,128)(2,1)} %param.34) | copy-start | bytes 442372
  7.2 16.6 %copy-start.7 = (bf16[24,768]{1,0:T(8,128)(2,1)S(1)}, bf16[24,768]{1,0:T(8,128)(2,1)}, u32[]{:S(2)}) copy-start(bf16[24,768]{1,0:T(8,128)(2,1)} %param.28) | copy-start | bytes 110596
  7.2 17.4 %copy-start.10 = (s32[2]{0:T(128)S(1)}, s32[2]{0:T(128)}, u32[]{:S(2)}) copy-start(s32[2]{0:T(128)} %pad_ref.1) | copy-start | bytes 28
  7.2 18.1 %copy-start.11 = (s32[2,8]{1,0:T(2,128)S(1)}, s32[2,8]{1,0:T(2,128)}, u32[]{:S(2)}) copy-start(s32[2,8]{1,0:T(2,128)} %param.21) | copy-start | bytes 196
  7.2 18.4 %copy-start.4 = (bf16[2,1024,768]{2,1,0:T(8,128)(2,1)S(1)}, bf16[2,1024,768]{2,1,0:T(8,128)(2,1)}, u32[]{:S(2)}) copy-start(bf16[2,1024,768]{2,1,0:T(8,128)(2,1)} %rows_ref.1) | copy-start | bytes 9437188
  7.2 72.6 %all-gather.3.cloned.1.call-start = ((), (), s32[]{:S(2)}) async-start(), calls=%async_computation.4 | async-start | bytes 3852288 | tf_op jit(solution)/shard_map/all_gather | solution.py:434
  15.6 0.6 copy-start.6
  16.3 153.0 %all-gather.5.cloned.1.call-start = ((), (), s32[]{:S(2)}) async-start(), calls=%async_computation.5 | async-start | bytes 10948608 | tf_op jit(solution)/shard_map/all_gather | solution.py:434
  24.5 393.9 %reduce-scatter.7.cloned.1.call-start = ((), (), s32[]{:S(2)}) async-start(), calls=%async_computation.6 | async-start | bytes 4202496 | tf_op jit(solution)/shard_map/reduce_scatter | solution.py:438
  132.1 1.9 copy-start
  134.1 1.0 copy-start.2
  169.3 122.3 %copy-start.1 = (bf16[2,1024,768]{2,1,0:T(8,128)(2,1)S(1)}, bf16[2,1024,768]{2,1,0:T(8,128)(2,1)}, u32[]{:S(2)}) copy-start(bf16[2,1024,768]{2,1,0:T(8,128)(2,1)} %copy-done) | copy-start | bytes 9437188
  291.6 1.2 copy-start.3
  369.2 135.2 %reduce-scatter.9.cloned.1.call-start = ((), (), s32[]{:S(2)}) async-start(), calls=%async_computation.7 | async-start | bytes 11943936 | tf_op jit(solution)/shard_map/reduce_scatter | solution.py:438
  369.3 49.9 %copy-start.8 = (f32[16,768]{1,0:T(8,128)S(1)}, f32[16,768]{1,0:T(8,128)}, u32[]{:S(2)}) copy-start(f32[16,768]{1,0:T(8,128)} %get-tuple-element.40) | copy-start | bytes 147460
  369.3 50.0 %copy-start.9 = (f32[8,768]{1,0:T(8,128)S(1)}, f32[8,768]{1,0:T(8,128)}, u32[]{:S(2)}) copy-start(f32[8,768]{1,0:T(8,128)} %get-tuple-element.41) | copy-start | bytes 73732
  369.8 158.0 %reduce-scatter.13.cloned.1.call-start = ((), (), s32[]{:S(2)}) async-start(), calls=%async_computation.9 | async-start | bytes 583680
  418.5 141.8 %reduce-scatter.11.cloned.1.call-start = ((), (), s32[]{:S(2)}) async-start(), calls=%async_computation.8 | async-start | bytes 1658880 | tf_op jit(solution)/shard_map/reduce_scatter | solution.py:439
  419.5 1.3 collective-permute-start
  420.8 4.2 collective-permute-start.1
  424.9 4.2 collective-permute-start.2
  429.1 4.2 collective-permute-start.3
  433.3 85.2 %collective-permute-start.4 = (f32[11,768]{1,0:T(8,128)S(1)}, f32[11,768]{1,0:T(8,128)S(1)}, u32[]{:S(2)}, u32[]{:S(2)}) collective-permute-start(f32[11,768]{1,0:T(8,128)S(1)} %add.57), channel_id=1, source_target_pairs={{0,2},{1,3},{2,0},{3,1},{4,6},{5,7},{6,4},{7,5},{8,10},{9,11},{10,... | collective-permute-start | bytes 101384 | tf_op jit(solution)/shard_map/ppermute | solution.py:447
Sparse Core Ops, SparseCore 0:
  16.4 63.4 all-gather.2
  83.2 85.9 all-gather.4
  369.3 49.0 reduce-scatter.6
  422.2 82.1 reduce-scatter.8
  506.7 21.0 reduce-scatter.12
  529.9 30.3 reduce-scatter.10

commit v2 on v1

--- a/solution.py
+++ b/solution.py
@@ -35,6 +35,10 @@
 def head_masks():
     lane = lax.broadcasted_iota(jnp.int32, (1, GROUP), 1) // HEAD_DIM
     return [lane == h for h in range(HEADS_IN)]
+
+
+def cost(flops, moved):
+    return pl.CostEstimate(flops=int(flops), bytes_accessed=int(moved), transcendentals=0)
 
 
 def segments(doc_lengths, pad_tail):
@@ -129,17 +133,24 @@
             jax.ShapeDtypeStruct((seqs, groups, 8, LEN), F32),
         ],
         compiler_params=pltpu.CompilerParams(vmem_limit_bytes=48 * 2**20),
+        cost_estimate=cost(2 * seqs * LEN * width * (3 * width + 16 * LEN), seqs * LEN * width * 10),
         name="attention_forward",
     )(low, count, rows, w, bias, segc, segr)
 
 
 def backward_kernel(
-    low_ref, count_ref, qkv_ref, mixed_ref, grad_ref, rowst_ref, lse_ref, segc_ref, segr_ref,
-    dqkv_ref, dw_ref, sums_ref,
-    q_ref, qt_ref, gt_ref, kt_ref, dqt_ref, acc_ref, delta_ref,
+    low_ref, count_ref, qkv_ref, mixed_ref, grad_ref, rowst_ref, lse_ref, segc_ref, segr_ref, vec_ref,
+    dqkv_ref, dw_ref, columns_ref,
+    q_ref, qt_ref, gt_ref, kt_ref, dqt_ref, acc_ref, delta_ref, sums_ref,
 ):
-    s = pl.program_id(1)
+    g, s = pl.program_id(0), pl.program_id(1)
     masks = head_masks()
+
+    @pl.when((g == 0) & (s == 0))
+    def _():
+        sums_ref[...] = jnp.zeros_like(sums_ref)
+        sums_ref[:16, :] = vec_ref[...]
+
     grad = grad_ref[...]
     prod = grad.astype(F32) * mixed_ref[...].astype(F32)
     coarse = prod.astype(BF16)
@@ -192,24 +203,29 @@
     dqkv_ref[:, :GROUP] = (dqt_ref[...] * HEAD_DIM**-0.5).astype(BF16).T
     dqkv = dqkv_ref[...]
     dw = dot(rowst_ref[...], dqkv)
-    sums = jnp.broadcast_to(jnp.sum(dqkv.astype(F32), axis=0, keepdims=True), sums_ref.shape)
+    sums = jnp.sum(dqkv.astype(F32), axis=0, keepdims=True)
+    lanes = pl.ds(pl.multiple_of(g * GROUP, GROUP), GROUP)
+    sums_ref[6:7, lanes] += sums[:, :GROUP]
+    sums_ref[7:8, lanes] += sums[:, 2 * GROUP :]
 
     @pl.when(s == 0)
     def _():
         acc_ref[...] = dw
-        sums_ref[...] = sums
 
     @pl.when(s > 0)
     def _():
         acc_ref[...] += dw
-        sums_ref[...] += sums
 
     @pl.when(s == pl.num_programs(1) - 1)
     def _():
         dw_ref[...] = acc_ref[...].astype(BF16)
 
-
-def attention_backward(qkv, mixed, grad, rowst, lse, segc, segr, low, count):
+    @pl.when((g == pl.num_programs(0) - 1) & (s == pl.num_programs(1) - 1))
+    def _():
+        columns_ref[...] = sums_ref[...].T.astype(BF16)
+
+
+def attention_backward(qkv, mixed, grad, rowst, lse, segc, segr, vec, low, count):
     seqs, _, width = mixed.shape
     groups = width // GROUP
     return pl.pallas_call(
@@ -225,11 +241,12 @@
                 pl.BlockSpec((None, None, 8, LEN), lambda g, s, *_: (s, g, 0, 0)),
                 pl.BlockSpec((None, LEN, 128), lambda g, s, *_: (s, 0, 0)),
                 pl.BlockSpec((None, 8, LEN), lambda g, s, *_: (s, 0, 0)),
+                pl.BlockSpec((16, width), lambda g, s, *_: (0, 0)),
             ],
             out_specs=[
                 pl.BlockSpec((None, LEN, TRIPLE), lambda g, s, *_: (s, 0, g)),
                 pl.BlockSpec((width, TRIPLE), lambda g, s, *_: (0, g)),
-                pl.BlockSpec((8, TRIPLE), lambda g, s, *_: (0, g)),
+                pl.BlockSpec((width, VEC), lambda g, s, *_: (0, 0)),
             ],
             scratch_shapes=[
                 pltpu.VMEM((LEN, GROUP), BF16),
@@ -239,16 +256,18 @@
                 pltpu.VMEM((GROUP, LEN), F32),
                 pltpu.VMEM((width, TRIPLE), F32),
                 pltpu.VMEM((8, LEN), F32),
+                pltpu.VMEM((VEC, width), F32),
             ],
         ),
         out_shape=[
             jax.ShapeDtypeStruct((seqs, LEN, 3 * width), BF16),
             jax.ShapeDtypeStruct((width, 3 * width), BF16),
-            jax.ShapeDtypeStruct((8, 3 * width), F32),
+            jax.ShapeDtypeStruct((width, VEC), BF16),
         ],
         compiler_params=pltpu.CompilerParams(vmem_limit_bytes=48 * 2**20),
+        cost_estimate=cost(2 * seqs * LEN * width * (3 * width + 32 * LEN), seqs * LEN * width * 20),
         name="attention_backward",
-    )(low, count, qkv, mixed, grad, rowst, lse, segc, segr)
+    )(low, count, qkv, mixed, grad, rowst, lse, segc, segr, vec)
 
 
 def middle_kernel(
@@ -426,12 +445,76 @@
             jax.ShapeDtypeStruct((8, width), F32),
         ],
         compiler_params=pltpu.CompilerParams(vmem_limit_bytes=60 * 2**20),
+        cost_estimate=cost(12 * count * width * w.shape[1], count * width * 14 + 4 * w.size),
         name="middle",
     )(pad, mixed, rows, cotangent, w, vec)
 
 
 def gather(shard):
     return lax.all_gather(shard, AXES, axis=0, tiled=True)
+
+
+def swap(values, axis, flip):
+    return lax.ppermute(values, axis, [(d, d ^ flip) for d in range(lax.axis_size(axis))])
+
+
+def place_kernel(columns, lines, where_ref, *refs):
+    sources, target = refs[:lines], refs[lines]
+    plane, column = where_ref[0], where_ref[1]
+    for m, source in enumerate(sources):
+        for k in range(columns):
+            target[(plane ^ m) * columns + (column ^ k)] = source[k]
+
+
+def quick_gather(shard):
+    planes, columns = lax.axis_size("dp"), lax.axis_size("fsdp")
+    rows, width = shard.shape
+    if planes % 2 or rows % 8:
+        return gather(shard)
+    column = jnp.stack([shard] + [swap(shard, "fsdp", k) for k in range(1, columns)])
+    even = [column] + [swap(column, "dp", m) for m in range(2, planes, 2)]
+    odd = [swap(part, "dp", 1) for part in even]
+    sources = [part for pair in zip(even, odd) for part in pair]
+    where = jnp.stack([lax.axis_index("dp"), lax.axis_index("fsdp")]).astype(jnp.int32)
+    whole = pl.pallas_call(
+        functools.partial(place_kernel, columns, len(sources)),
+        grid_spec=pltpu.PrefetchScalarGridSpec(
+            num_scalar_prefetch=1,
+            grid=(1,),
+            in_specs=[pl.BlockSpec((columns, rows, width), lambda i, *_: (0, 0, 0))] * len(sources),
+            out_specs=pl.BlockSpec((planes * columns, rows, width), lambda i, *_: (0, 0, 0)),
+        ),
+        out_shape=jax.ShapeDtypeStruct((planes * columns, rows, width), shard.dtype),
+        compiler_params=pltpu.CompilerParams(vmem_limit_bytes=48 * 2**20),
+        name="place",
+    )(where, *sources)
+    return whole.reshape(planes * columns * rows, width)
+
+
+def quick_scatter(partial):
+    planes, columns = lax.axis_size("dp"), lax.axis_size("fsdp")
+    rows = partial.shape[0] // (planes * columns)
+    if planes % 2 or rows % 8:
+        return scatter(partial)
+    plane, column = lax.axis_index("dp"), lax.axis_index("fsdp")
+    core, chip = plane % 2, plane // 2
+
+    def pick(values, index, axis=0):
+        return lax.dynamic_index_in_dim(values, index, axis, keepdims=False)
+
+    halves = partial.reshape(planes // 2, 2, columns * rows, -1)
+    other = swap(pick(halves, 1 - core, 1), "dp", 1)
+    chips = (pick(halves, core, 1).astype(F32) + other.astype(F32)).astype(partial.dtype)
+    arrived = [swap(pick(chips, chip ^ m), "dp", 2 * m) for m in range(1, planes // 2)]
+    own = pick(chips, chip).astype(F32)
+    for part in arrived:
+        own = own + part.astype(F32)
+    own = own.astype(partial.dtype).reshape(columns, rows, -1)
+    arrived = [swap(pick(own, column ^ k), "fsdp", k) for k in range(1, columns)]
+    own = pick(own, column).astype(F32)
+    for part in arrived:
+        own = own + part.astype(F32)
+    return own
 
 
 def scatter(partial):
@@ -440,12 +523,11 @@
 
 
 def total_over_devices(values):
-    for axis in AXES:
-        size = lax.axis_size(axis)
-        step = 1
-        while step < size:
-            values = values + lax.ppermute(values, axis, [(d, d ^ step) for d in range(size)])
-            step *= 2
+    for axis, flips in (("dp", [1]), ("dp", range(2, lax.axis_size("dp"), 2)), ("fsdp", range(1, lax.axis_size("fsdp")))):
+        parts = [values] + [swap(values, axis, flip) for flip in flips]
+        while len(parts) > 1:
+            parts = [a + b for a, b in zip(parts[::2], parts[1::2])]
+        values = parts[0]
     return values
 
 
@@ -469,7 +551,7 @@
         for g in range(groups)
         for mat in (query_weight, key_weight, value_weight)
     ]
-    near = gather(jnp.concatenate(triples + [columns], axis=1))
+    near = quick_gather(jnp.concatenate(triples + [columns], axis=1))
     inner_own = inner_weight.reshape(own, devices, parts, own).transpose(0, 2, 1, 3).reshape(own, parts * width)
     outer_own = outer_weight.reshape(parts, own, width).transpose(1, 0, 2).reshape(own, parts * width)
     far = gather(jnp.concatenate([merge_weight, inner_own, outer_own], axis=1))
@@ -491,22 +573,17 @@
         mixed.reshape(tokens, width), layer_input.reshape(tokens, width), cotangent.reshape(tokens, width), far, vec, pad_tail
     )
     far_grad = scatter(far_partial)
-    dqkv, near_partial, near_sums = attention_backward(
-        qkv, mixed, mixed_grad.reshape(mixed.shape), rowst, lse, segc, segr, low, count
+    valid_count = jnp.sum(LEN - pad_tail).astype(F32)
+    stat_row = jnp.concatenate([jnp.sum(stats[:4], axis=1), valid_count[None], jnp.zeros((VEC - 5,), F32)])
+    totals = total_over_devices(jnp.broadcast_to(stat_row, (8, VEC)))[0]
+    dqkv, near_partial, near_columns = attention_backward(
+        qkv, mixed, mixed_grad.reshape(mixed.shape), rowst, lse, segc, segr, sums, low, count
     )
-    valid_count = jnp.sum(LEN - pad_tail).astype(F32)
-    stat_row = jnp.concatenate([jnp.sum(stats[:4], axis=1), valid_count[None], jnp.zeros((width - 5,), F32)])
-    totals = total_over_devices(jnp.concatenate([sums[:6], sums[8 : 8 + parts], stat_row[None]]))
-
-    near_rows = near_sums[0].reshape(groups, 3, GROUP)
-    near_cols = jnp.stack([near_rows[:, 0].reshape(width), near_rows[:, 2].reshape(width)])
-    near_cols = jnp.pad(near_cols.T, ((0, 0), (0, VEC - 2))).astype(BF16)
-    near_grad = scatter(jnp.concatenate([near_partial, near_cols], axis=1)).astype(F32)
+    near_grad = quick_scatter(jnp.concatenate([near_partial, near_columns], axis=1)).astype(F32)
     input_gradient = residual + dot(dqkv.reshape(tokens, 3 * width), near[:, : 3 * width], 1, 1)
 
-    which = lax.axis_index(AXES)
-    mine = lax.dynamic_slice_in_dim(totals[: 6 + parts], which * own, own, axis=1)
-    inner_bias_gradient = mine[6:].reshape(parts * own)
+    mine = near_grad[:, 3 * width :].T
+    inner_bias_gradient = mine[8 : 8 + parts].reshape(parts * own)
     triple = near_grad[:, : 3 * width].reshape(own, groups, 3, GROUP)
     query_grad, key_grad, value_grad = (triple[:, :, k].reshape(own, width) for k in range(3))
     far_grad = far_grad.astype(F32)
@@ -514,17 +591,17 @@
     inner_grad = inner_grad.reshape(own, parts, devices, own).transpose(0, 2, 1, 3).reshape(own, parts * width)
     outer_grad = far_grad[:, (1 + parts) * width :].reshape(own, parts, width).transpose(1, 0, 2)
     all_tokens = tokens * devices
-    valid_total = totals[6 + parts, 4]
+    valid_total = totals[4]
     share = jnp.reshape(valid_total / all_tokens, (1,))
-    layer_stats = jnp.concatenate([share, jnp.sqrt(totals[6 + parts, :4] / (valid_total * width))])
+    layer_stats = jnp.concatenate([share, jnp.sqrt(totals[:4] / (valid_total * width))])
     return (
         output.reshape(layer_input.shape),
         input_gradient.reshape(layer_input.shape),
         query_grad,
-        near_grad[:, 3 * width],
+        mine[6],
         key_grad,
         value_grad,
-        near_grad[:, 3 * width + 1],
+        mine[7],
         far_grad[:, :width],
         mine[5],
         mine[3],

time: 576 us -> 420 us (0.73)
  waiting for transfers between devices: 245 us -> 66.3 us
  starting transfers between devices: 7.69 us -> 32.3 us
  local copies, waits for them, and re-layouts: 40.4 us -> 33.4 us
    reduce_scatter x2 -> x1, waiting for transfers between devices: 117 us -> 0.01 us  [scatter(): partial = lax.psum_scatter(partial, 'dp', scatter_dimension=0, tiled=True)]
    all_gather x2 -> x1, waiting for transfers between devices: 85 us -> 0.01 us  [gather(): return lax.all_gather(shard, AXES, axis=0, tiled=True)]
    ppermute x5 -> x24, waiting for transfers between devices: 9.16 us -> 55.8 us  [swap(): lax.ppermute(values, axis, [(d, d ^ flip) for d in range(lax.axis_size(ax...]
    ppermute x5 -> x24, starting transfers between devices: 7.45 us -> 31.6 us  [swap(): lax.ppermute(values, axis, [(d, d ^ flip) for d in range(lax.axis_size(ax...]
    reduce_scatter x1, waiting for transfers between devices: 27.3 us -> 10.4 us  [scatter(): return lax.psum_scatter(partial, 'fsdp', scatter_dimension=0, tiled=True)]
    unnamed x7 -> x3, waiting for transfers between devices: 6.12 us -> 0.05 us
    unnamed x40 -> x57, local copies, waits for them, and re-layouts: 16.5 us -> 13.1 us
  transfers between devices with their start and end apart: 11 -> 27, of which waited for: 10 -> 13; matrix products, arithmetic and copies ran while one was open for 6% -> 8% of each run, Pallas kernels for 9% -> 30%
where the time goes in v2:
time: 420 us; the launch traced here: 418 us
  Pallas kernels  248 us (59%)
  waiting for transfers between devices  66.3 us (16%)
  local copies, waits for them, and re-layouts  33.4 us (8%)
  starting transfers between devices  32.3 us (8%)
  between operations  16.5 us (4%)
  matrix products  13 us (3%)
  other arithmetic  8.26 us (2%)
    pallas_call x1, Pallas kernels, middle(): pl.pallas_call(functools.partial(middle_kernel, parts, width, tokens), gr...  122 us
    pallas_call x1, Pallas kernels, attention_backward(): pl.pallas_call(backward_kernel, grid_spec=pltpu.PrefetchScalarGridSpec(nu...  72 us
    ppermute x24, waiting for transfers between devices, swap(): lax.ppermute(values, axis, [(d, d ^ flip) for d in range(lax.axis_size(ax...  55.8 us
    pallas_call x1, Pallas kernels, attention_forward(): pl.pallas_call(forward_kernel, grid_spec=pltpu.PrefetchScalarGridSpec(num...  50.1 us
    ppermute x24, starting transfers between devices, swap(): lax.ppermute(values, axis, [(d, d ^ flip) for d in range(lax.axis_size(ax...  31.6 us
    unnamed x57, local copies, waits for them, and re-layouts  13.1 us
    dot_general x1, matrix products, dot(): lax.dot_general(left, right, (((left_dim,), (right_dim,)), ((), ())), pre...  13 us
    reduce_scatter x1, waiting for transfers between devices, scatter(): return lax.psum_scatter(partial, 'fsdp', scatter_dimension=0, tiled=True)  10.4 us
  transfers between devices with their start and end apart: 27, of which 13 were waited for; matrix products, arithmetic and copies ran while one was open for 8% of the time, Pallas kernels for 30%

profile of v2, /device:TPU:0, one launch (start us, length us, event | category | flops | bytes accessed | tf_op | source)
XLA Modules:
  0.0 417.7 jit_solution(7478669960101403165)
XLA Ops:
  7.4 2.2 reshape.182
  9.7 1.3 reshape.183
  11.0 1.0 copy.111
  12.0 0.7 pad_maximum_fusion.2
  12.8 0.6 reduce-scatter.3.cloned.1.call-start
  14.6 3.1 collective-permute-start
  17.7 2.6 collective-permute-start.1
  20.5 0.6 fusion.12
  21.2 0.9 collective-permute-done
  22.1 9.9 %collective-permute-done.1 = bf16[24,2432]{1,0:T(8,128)(2,1)S(1)} collective-permute-done((bf16[24,2432]{1,0:T(8,128)(2,1)S(1)}, bf16[24,2432]{1,0:T(8,128)(2,1)S(1)}, u32[]{:S(2)}, u32[]{:S(2)}) %collective-permute-start.1) | collective-permute-done | bytes 116768 | tf_op jit(solution)/shard_map/ppermute | solution.py:458
  32.1 1.6 collective-permute-start.4
  33.6 1.7 collective-permute-start.6
  36.3 8.6 %collective-permute-done.4.refs_2_ = bf16[4,24,2432]{2,1,0:T(8,128)(2,1)S(1)} collective-permute-done((bf16[4,24,2432]{2,1,0:T(8,128)(2,1)S(1)}, bf16[4,24,2432]{2,1,0:T(8,128)(2,1)S(1)}, u32[]{:S(2)}, u32[]{:S(2)}) %collective-permute-start.4) | collective-permute-done | bytes 466976 | tf_op jit(solution)/shard_map/ppermute | solution.py:458
  44.9 4.9 %collective-permute-done.6.refs_4_ = bf16[4,24,2432]{2,1,0:T(8,128)(2,1)S(1)} collective-permute-done((bf16[4,24,2432]{2,1,0:T(8,128)(2,1)S(1)}, bf16[4,24,2432]{2,1,0:T(8,128)(2,1)S(1)}, u32[]{:S(2)}, u32[]{:S(2)}) %collective-permute-start.6) | collective-permute-done | bytes 466976 | tf_op jit(solution)/shard_map/ppermute | solution.py:458
  49.7 8.7 %collective-permute-done.8.refs_6_ = bf16[4,24,2432]{2,1,0:T(8,128)(2,1)S(1)} collective-permute-done((bf16[4,24,2432]{2,1,0:T(8,128)(2,1)S(1)}, bf16[4,24,2432]{2,1,0:T(8,128)(2,1)S(1)}, u32[]{:S(2)}, u32[]{:S(2)}) %collective-permute-start.8) | collective-permute-done | bytes 466976 | tf_op jit(solution)/shard_map/ppermute | solution.py:458
  58.6 4.7 %copy.112 = bf16[2,1024,768]{1,2,0:T(8,128)(2,1)} copy(bf16[2,1024,768]{2,1,0:T(8,128)(2,1)} %rows_ref.1) | data formatting | bytes 6291456 | tf_op args[0]
  63.4 3.6 place.1
  67.1 0.9 slice.141
  68.2 0.6 slice.144.vec_ref
  68.9 0.3 broadcast_in_dim.62.segc_ref
  69.3 50.1 %attention_forward.1 = (bf16[2,1024,2304]{2,1,0:T(8,128)(2,1)}, bf16[2,1024,768]{2,1,0:T(8,128)(2,1)S(1)}, f32[2,3,8,1024]{3,2,1,0:T(8,128)S(1)}) custom-call(s32[2,4]{1,0:T(2,128)S(1)} %get-tuple-element.55.low_ref, s32[2,4]{1,0:T(2,128)S(1)} %get-tuple-element.56.count_ref, bf16[2,1024,768]{2,1,0:T(8,128)(2,1)} %rows_ref.1, bf16[768,2432]{1,0:T(8,128)(2,1)} %bitcast.90, ...), custom_call_target="tpu_custom_call" | custom-call | flops 58787364864 | bytes 15728640 | tf_op jit(solution)/shard_map/attention_forward/pallas_call | solution.py:111
  119.3 1.7 copy-done
  121.1 122.2 %middle.1 = (bf16[2048,768]{1,0:T(8,128)(2,1)}, f32[2048,768]{1,0:T(8,128)}, bf16[2048,768]{1,0:T(8,128)(2,1)}, bf16[768,6912]{1,0:T(8,128)(2,1)}, f32[16,768]{1,0:T(8,128)}, /*index=5*/f32[8,768]{1,0:T(8,128)}) custom-call(s32[2]{0:T(128)} %pad_ref.1, bf16[2048,768]{1,0:T(8,128)(2,1)} %bitcast.85, bf16[2048,768]{1,0:T(8,128)(2,1)} %bitcast.92, ...), custom_call_target="tpu_custom_call" | custom-call | flops 130459631616 | bytes 43253760 | tf_op jit(solution)/shard_map/middle/pallas_call | solution.py:407
  243.4 0.7 copy-done.2
  244.1 1.9 copy-done.1
  246.0 72.0 %attention_backward.1 = (bf16[2,1024,2304]{2,1,0:T(8,128)(2,1)}, bf16[768,2304]{1,0:T(8,128)(2,1)}, bf16[768,128]{1,0:T(8,128)(2,1)S(1)}) custom-call(s32[2,4]{1,0:T(2,128)S(1)} %get-tuple-element.55.low_ref, s32[2,4]{1,0:T(2,128)S(1)} %get-tuple-element.56.count_ref, bf16[2,1024,2304]{2,1,0:T(8,128)(2,1)} %get-tuple-element.33.qkv_ref, ...), custom_call_target="tpu_custom_call" | custom-call | flops 110326972416 | bytes 31457280 | tf_op jit(solution)/shard_map/attention_backward/pallas_call | solution.py:231
  318.0 2.3 pad_maximum_fusion
  320.2 1.9 copy-done.3
  323.2 0.5 collective-permute-start.17
  323.7 2.4 collective-permute-done.17
  326.2 3.8 collective-permute-start.19
  329.9 1.6 collective-permute-done.19
  331.5 2.9 collective-permute-done.20
  334.4 6.4 %collective-permute-start.21 = (f32[8,128]{1,0:T(8,128)S(1)}, f32[8,128]{1,0:T(8,128)S(1)}, u32[]{:S(2)}, u32[]{:S(2)}) collective-permute-start(f32[8,128]{1,0:T(8,128)S(1)} %add_add_fusion.1), channel_id=1, source_target_pairs={{0,1},{1,0},{2,3},{3,2},{4,5},{5,4},{6,7},{7,6},{8,9},{9,8},{10,11... | collective-permute-start | bytes 12296 | tf_op jit(solution)/shard_map/ppermute | solution.py:458
  340.9 2.2 collective-permute-start.22
  343.1 1.4 collective-permute-start.23
  344.5 2.5 fusion
  347.0 1.2 dynamic-slice_bitcast_fusion.3
  348.1 0.6 collective-permute-start.11
  348.7 1.9 collective-permute-start.12
  350.6 1.0 collective-permute-start.13
  351.6 13.0 %fusion.3 = f32[2048,768]{1,0:T(8,128)} fusion(f32[2048,768]{1,0:T(8,128)} %get-tuple-element.32, bf16[2048,2304]{1,0:T(8,128)(2,1)} %bitcast.123, bf16[768,2432]{1,0:T(8,128)(2,1)S(1)} %bitcast.91), kind=kOutput, calls=%fused_computation.5 | convolution fusion | flops 7249330176 | bytes 25559040 | tf_op jit(solution)/shard_map/dot_general | solution.py:30
  364.7 0.6 slice.139
  365.9 3.0 collective-permute-done.12
  368.9 1.6 collective-permute-done.13
  370.8 0.6 collective-permute-start.14
  371.4 2.4 collective-permute-start.15
  373.9 1.4 collective-permute-start.16
  375.9 0.6 pad_maximum_fusion.5
  376.5 6.4 %collective-permute-done.14 = bf16[24,2432]{1,0:T(8,128)(2,1)S(1)} collective-permute-done((bf16[24,2432]{1,0:T(8,128)(2,1)S(1)}, bf16[24,2432]{1,0:T(8,128)(2,1)S(1)}, u32[]{:S(2)}, u32[]{:S(2)}) %collective-permute-start.14) | collective-permute-done | bytes 116768 | tf_op jit(solution)/shard_map/ppermute | solution.py:458
  382.9 4.9 %collective-permute-done.15 = bf16[24,2432]{1,0:T(8,128)(2,1)S(1)} collective-permute-done((bf16[24,2432]{1,0:T(8,128)(2,1)S(1)}, bf16[24,2432]{1,0:T(8,128)(2,1)S(1)}, u32[]{:S(2)}, u32[]{:S(2)}) %collective-permute-start.15) | collective-permute-done | bytes 116768 | tf_op jit(solution)/shard_map/ppermute | solution.py:458
  388.0 0.6 slice_reduce_fusion
  388.6 0.6 copy.120
  389.3 0.6 copy.121
  389.9 0.6 copy.122
  390.7 0.6 reshape.195
  391.3 0.8 slice_reduce_fusion.3
  392.1 10.4 %reduce-scatter.5.cloned.1.call-done = bf16[24,6912]{1,0:T(8,128)(2,1)} async-done(((bf16[96,6912]{1,0:T(8,128)(2,1)}), bf16[24,6912]{1,0:T(8,128)(2,1)}) %reduce-scatter.5.cloned.1.call-update) | async-done | bytes 331792 | tf_op jit(solution)/shard_map/reduce_scatter | solution.py:522
  402.6 1.0 fusion.15
  403.6 1.1 reshape.193
  404.7 1.2 copy.114
  406.0 2.6 reshape.194
  408.7 0.8 copy.116
  409.5 1.4 slice.153
  (128 shorter events, 4.6 us)
Async XLA Ops:
  7.2 4.8 %copy-start.8 = (bf16[24,768]{1,0:T(8,128)(2,1)S(1)}, bf16[24,768]{1,0:T(8,128)(2,1)}, u32[]{:S(2)}) copy-start(bf16[24,768]{1,0:T(8,128)(2,1)} %param.28) | copy-start | bytes 110596
  7.2 6.1 %copy-start.20 = (bf16[96]{0:T(256)(128)(2,1)S(1)}, bf16[96]{0:T(256)(128)(2,1)}, u32[]{:S(2)}) copy-start(bf16[96]{0:T(256)(128)(2,1)} %param.33) | copy-start | bytes 580
  7.2 6.3 %copy-start.12 = (bf16[24]{0:T(256)(128)(2,1)S(1)}, bf16[24]{0:T(256)(128)(2,1)}, u32[]{:S(2)}) copy-start(bf16[24]{0:T(256)(128)(2,1)} %param.27) | copy-start | bytes 148
  7.2 6.4 %copy-start.13 = (bf16[24]{0:T(256)(128)(2,1)S(1)}, bf16[24]{0:T(256)(128)(2,1)}, u32[]{:S(2)}) copy-start(bf16[24]{0:T(256)(128)(2,1)} %param.29) | copy-start | bytes 148
  7.2 6.5 %copy-start.14 = (bf16[24]{0:T(256)(128)(2,1)S(1)}, bf16[24]{0:T(256)(128)(2,1)}, u32[]{:S(2)}) copy-start(bf16[24]{0:T(256)(128)(2,1)} %param.30) | copy-start | bytes 148
  7.2 6.6 %copy-start.15 = (bf16[24]{0:T(256)(128)(2,1)S(1)}, bf16[24]{0:T(256)(128)(2,1)}, u32[]{:S(2)}) copy-start(bf16[24]{0:T(256)(128)(2,1)} %param.31) | copy-start | bytes 148
  7.3 6.7 %copy-start.16 = (bf16[24]{0:T(256)(128)(2,1)S(1)}, bf16[24]{0:T(256)(128)(2,1)}, u32[]{:S(2)}) copy-start(bf16[24]{0:T(256)(128)(2,1)} %param.35) | copy-start | bytes 148
  7.3 6.8 %copy-start.17 = (bf16[24]{0:T(256)(128)(2,1)S(1)}, bf16[24]{0:T(256)(128)(2,1)}, u32[]{:S(2)}) copy-start(bf16[24]{0:T(256)(128)(2,1)} %param.36) | copy-start | bytes 148
  7.3 6.9 %copy-start.18 = (bf16[24]{0:T(256)(128)(2,1)S(1)}, bf16[24]{0:T(256)(128)(2,1)}, u32[]{:S(2)}) copy-start(bf16[24]{0:T(256)(128)(2,1)} %param.37) | copy-start | bytes 148
  7.3 7.0 %copy-start.19 = (bf16[24]{0:T(256)(128)(2,1)S(1)}, bf16[24]{0:T(256)(128)(2,1)}, u32[]{:S(2)}) copy-start(bf16[24]{0:T(256)(128)(2,1)} %param.24) | copy-start | bytes 148
  7.3 7.2 %copy-start.5 = (bf16[24,768]{1,0:T(8,128)(2,1)S(1)}, bf16[24,768]{1,0:T(8,128)(2,1)}, u32[]{:S(2)}) copy-start(bf16[24,768]{1,0:T(8,128)(2,1)} %param.23) | copy-start | bytes 110596
  7.3 7.2 %copy-start.6 = (bf16[24,768]{1,0:T(8,128)(2,1)S(1)}, bf16[24,768]{1,0:T(8,128)(2,1)}, u32[]{:S(2)}) copy-start(bf16[24,768]{1,0:T(8,128)(2,1)} %param.25) | copy-start | bytes 110596
  7.3 7.2 %copy-start.7 = (bf16[24,768]{1,0:T(8,128)(2,1)S(1)}, bf16[24,768]{1,0:T(8,128)(2,1)}, u32[]{:S(2)}) copy-start(bf16[24,768]{1,0:T(8,128)(2,1)} %param.26) | copy-start | bytes 110596
  7.3 13.0 %copy-start.10 = (s32[2,8]{1,0:T(2,128)S(1)}, s32[2,8]{1,0:T(2,128)}, u32[]{:S(2)}) copy-start(s32[2,8]{1,0:T(2,128)} %param.21) | copy-start | bytes 196
  7.3 13.2 %copy-start.11 = (s32[2]{0:T(128)S(1)}, s32[2]{0:T(128)}, u32[]{:S(2)}) copy-start(s32[2]{0:T(128)} %pad_ref.1) | copy-start | bytes 28
  7.3 113.7 %all-gather.2.cloned.1.call-start = ((), (), s32[]{:S(2)}) async-start(), calls=%async_computation.2 | async-start | bytes 10948608 | tf_op jit(solution)/shard_map/all_gather | solution.py:454
  12.8 351.8 %reduce-scatter.3.cloned.1.call-start = ((), (), s32[]{:S(2)}) async-start(), calls=%async_computation.3 | async-start | bytes 11943936 | tf_op jit(solution)/shard_map/reduce_scatter | solution.py:521
  14.6 7.5 %collective-permute-start = (bf16[24,2432]{1,0:T(8,128)(2,1)S(1)}, bf16[24,2432]{1,0:T(8,128)(2,1)S(1)}, u32[]{:S(2)}, u32[]{:S(2)}) collective-permute-start(bf16[24,2432]{1,0:T(8,128)(2,1)S(1)} %constant_dynamic-update-slice_fusion), channel_id=1, source_target_pairs={{0,1},{1,0},{2,3},{3,2},{4,5},{5,4},{6,7},{7,6},{8,9},{9,8},{10,11... | collective-permute-start | bytes 350216 | tf_op jit(solution)/shard_map/ppermute | solution.py:458
  17.7 14.3 %collective-permute-start.1 = (bf16[24,2432]{1,0:T(8,128)(2,1)S(1)}, bf16[24,2432]{1,0:T(8,128)(2,1)S(1)}, u32[]{:S(2)}, u32[]{:S(2)}) collective-permute-start(bf16[24,2432]{1,0:T(8,128)(2,1)S(1)} %constant_dynamic-update-slice_fusion), channel_id=1, source_target_pairs={{0,2},{1,3},{2,0},{3,1},{4,6},{5,7},{6,4},{7,5},{8,10},{9,11},{10,... | collective-permute-start | bytes 350216 | tf_op jit(solution)/shard_map/ppermute | solution.py:458
  20.3 11.7 %collective-permute-start.2 = (bf16[24,2432]{1,0:T(8,128)(2,1)S(1)}, bf16[24,2432]{1,0:T(8,128)(2,1)S(1)}, u32[]{:S(2)}, u32[]{:S(2)}) collective-permute-start(bf16[24,2432]{1,0:T(8,128)(2,1)S(1)} %constant_dynamic-update-slice_fusion), channel_id=1, source_target_pairs={{0,3},{1,2},{2,1},{3,0},{4,7},{5,6},{6,5},{7,4},{8,11},{9,10},{10,... | collective-permute-start | bytes 350216 | tf_op jit(solution)/shard_map/ppermute | solution.py:458
  32.1 12.8 %collective-permute-start.4 = (bf16[4,24,2432]{2,1,0:T(8,128)(2,1)S(1)}, bf16[4,24,2432]{2,1,0:T(8,128)(2,1)S(1)}, u32[]{:S(2)}, u32[]{:S(2)}) collective-permute-start(bf16[4,24,2432]{2,1,0:T(8,128)(2,1)S(1)} %pad_maximum_fusion.1.refs_0_), channel_id=1, source_target_pairs={{0,8},{4,12},{8,0},{12,4},{16,24},{20,28},{24,16},{28,20},{1,9},{5... | collective-permute-start | bytes 1400840 | tf_op jit(solution)/shard_map/ppermute | solution.py:458
  33.6 16.1 %collective-permute-start.6 = (bf16[4,24,2432]{2,1,0:T(8,128)(2,1)S(1)}, bf16[4,24,2432]{2,1,0:T(8,128)(2,1)S(1)}, u32[]{:S(2)}, u32[]{:S(2)}) collective-permute-start(bf16[4,24,2432]{2,1,0:T(8,128)(2,1)S(1)} %pad_maximum_fusion.1.refs_0_), channel_id=1, source_target_pairs={{0,16},{4,20},{8,24},{12,28},{16,0},{20,4},{24,8},{28,12},{1,17},{... | collective-permute-start | bytes 1400840 | tf_op jit(solution)/shard_map/ppermute | solution.py:458
  35.3 23.2 %collective-permute-start.8 = (bf16[4,24,2432]{2,1,0:T(8,128)(2,1)S(1)}, bf16[4,24,2432]{2,1,0:T(8,128)(2,1)S(1)}, u32[]{:S(2)}, u32[]{:S(2)}) collective-permute-start(bf16[4,24,2432]{2,1,0:T(8,128)(2,1)S(1)} %pad_maximum_fusion.1.refs_0_), channel_id=1, source_target_pairs={{0,24},{4,28},{8,16},{12,20},{16,8},{20,12},{24,0},{28,4},{1,25},{... | collective-permute-start | bytes 1400840 | tf_op jit(solution)/shard_map/ppermute | solution.py:458
  36.2 27.2 %collective-permute-start.3 = (bf16[4,24,2432]{2,1,0:T(8,128)(2,1)S(1)}, bf16[4,24,2432]{2,1,0:T(8,128)(2,1)S(1)}, u32[]{:S(2)}, u32[]{:S(2)}) collective-permute-start(bf16[4,24,2432]{2,1,0:T(8,128)(2,1)S(1)} %pad_maximum_fusion.1.refs_0_), channel_id=1, source_target_pairs={{0,4},{4,0},{8,12},{12,8},{16,20},{20,16},{24,28},{28,24},{1,5},{5... | collective-permute-start | bytes 1400840 | tf_op jit(solution)/shard_map/ppermute | solution.py:458
  44.9 18.5 %collective-permute-start.5 = (bf16[4,24,2432]{2,1,0:T(8,128)(2,1)S(1)}, bf16[4,24,2432]{2,1,0:T(8,128)(2,1)S(1)}, u32[]{:S(2)}, u32[]{:S(2)}) collective-permute-start(bf16[4,24,2432]{2,1,0:T(8,128)(2,1)S(1)} %collective-permute-done.4.refs_2_), channel_id=1, source_target_pairs={{0,4},{4,0},{8,12},{12,8},{16,20},{20,16},{24,28},{28,24},{1,5},{5... | collective-permute-start | bytes 1400840 | tf_op jit(solution)/shard_map/ppermute | solution.py:458
  49.7 13.7 %collective-permute-start.7 = (bf16[4,24,2432]{2,1,0:T(8,128)(2,1)S(1)}, bf16[4,24,2432]{2,1,0:T(8,128)(2,1)S(1)}, u32[]{:S(2)}, u32[]{:S(2)}) collective-permute-start(bf16[4,24,2432]{2,1,0:T(8,128)(2,1)S(1)} %collective-permute-done.6.refs_4_), channel_id=1, source_target_pairs={{0,4},{4,0},{8,12},{12,8},{16,20},{20,16},{24,28},{28,24},{1,5},{5... | collective-permute-start | bytes 1400840 | tf_op jit(solution)/shard_map/ppermute | solution.py:458
  58.5 4.9 %collective-permute-start.9 = (bf16[4,24,2432]{2,1,0:T(8,128)(2,1)S(1)}, bf16[4,24,2432]{2,1,0:T(8,128)(2,1)}, u32[]{:S(2)}, u32[]{:S(2)}) collective-permute-start(bf16[4,24,2432]{2,1,0:T(8,128)(2,1)S(1)} %collective-permute-done.8.refs_6_), channel_id=1, source_target_pairs={{0,4},{4,0},{8,12},{12,8},{16,20},{20,16},{24,28},{28,24},{1,5},{5... | collective-permute-start | bytes 1400840 | tf_op jit(solution)/shard_map/ppermute | solution.py:458
  119.3 1.7 copy-start
  243.3 0.8 copy-start.2
  243.3 159.3 %reduce-scatter.5.cloned.1.call-start = ((), (), s32[]{:S(2)}) async-start(), calls=%async_computation.4 | async-start | bytes 1658880 | tf_op jit(solution)/shard_map/reduce_scatter | solution.py:522
  244.1 1.9 copy-start.1
  320.2 1.9 copy-start.3
  320.2 2.7 copy-start.9
  322.2 22.2 %collective-permute-start.10 = (bf16[4,96,2432]{2,1,0:T(8,128)(2,1)S(1)}, bf16[4,96,2432]{2,1,0:T(8,128)(2,1)}, u32[]{:S(2)}, u32[]{:S(2)}) collective-permute-start(bf16[4,96,2432]{2,1,0:T(8,128)(2,1)S(1)} %dynamic-slice_bitcast_fusion), channel_id=1, source_target_pairs={{0,4},{4,0},{8,12},{12,8},{16,20},{20,16},{24,28},{28,24},{1,5},{5... | collective-permute-start | bytes 5603336 | tf_op jit(solution)/shard_map/ppermute | solution.py:458
  323.2 3.0 collective-permute-start.17
  326.2 3.8 collective-permute-start.18
  326.2 5.4 %collective-permute-start.19 = (f32[8,128]{1,0:T(8,128)S(1)}, f32[8,128]{1,0:T(8,128)S(1)}, u32[]{:S(2)}, u32[]{:S(2)}) collective-permute-start(f32[8,128]{1,0:T(8,128)S(1)} %broadcast_add_fusion), channel_id=1, source_target_pairs={{0,16},{4,20},{8,24},{12,28},{16,0},{20,4},{24,8},{28,12},{1,17},{... | collective-permute-start | bytes 12296 | tf_op jit(solution)/shard_map/ppermute | solution.py:458
  329.9 4.5 %collective-permute-start.20 = (f32[8,128]{1,0:T(8,128)S(1)}, f32[8,128]{1,0:T(8,128)S(1)}, u32[]{:S(2)}, u32[]{:S(2)}) collective-permute-start(f32[8,128]{1,0:T(8,128)S(1)} %broadcast_add_fusion), channel_id=1, source_target_pairs={{0,24},{4,28},{8,16},{12,20},{16,8},{20,12},{24,0},{28,4},{1,25},{... | collective-permute-start | bytes 12296 | tf_op jit(solution)/shard_map/ppermute | solution.py:458
  334.4 17.2 %copy-start.4 = (bf16[32,24,2432]{2,1,0:T(8,128)(2,1)S(1)}, bf16[32,24,2432]{2,1,0:T(8,128)(2,1)}, u32[]{:S(2)}) copy-start(bf16[32,24,2432]{2,1,0:T(8,128)(2,1)} %place.1) | copy-start | bytes 11206660
  334.4 16.1 %collective-permute-start.21 = (f32[8,128]{1,0:T(8,128)S(1)}, f32[8,128]{1,0:T(8,128)S(1)}, u32[]{:S(2)}, u32[]{:S(2)}) collective-permute-start(f32[8,128]{1,0:T(8,128)S(1)} %add_add_fusion.1), channel_id=1, source_target_pairs={{0,1},{1,0},{2,3},{3,2},{4,5},{5,4},{6,7},{7,6},{8,9},{9,8},{10,11... | collective-permute-start | bytes 12296 | tf_op jit(solution)/shard_map/ppermute | solution.py:458
  340.9 23.8 %collective-permute-start.22 = (f32[8,128]{1,0:T(8,128)S(1)}, f32[8,128]{1,0:T(8,128)S(1)}, u32[]{:S(2)}, u32[]{:S(2)}) collective-permute-start(f32[8,128]{1,0:T(8,128)S(1)} %add_add_fusion.1), channel_id=1, source_target_pairs={{0,2},{1,3},{2,0},{3,1},{4,6},{5,7},{6,4},{7,5},{8,10},{9,11},{10,... | collective-permute-start | bytes 12296 | tf_op jit(solution)/shard_map/ppermute | solution.py:458
  343.1 21.6 %collective-permute-start.23 = (f32[8,128]{1,0:T(8,128)S(1)}, f32[8,128]{1,0:T(8,128)S(1)}, u32[]{:S(2)}, u32[]{:S(2)}) collective-permute-start(f32[8,128]{1,0:T(8,128)S(1)} %add_add_fusion.1), channel_id=1, source_target_pairs={{0,3},{1,2},{2,1},{3,0},{4,7},{5,6},{6,5},{7,4},{8,11},{9,10},{10,... | collective-permute-start | bytes 12296 | tf_op jit(solution)/shard_map/ppermute | solution.py:458
  348.1 17.8 %collective-permute-start.11 = (bf16[96,2432]{1,0:T(8,128)(2,1)}, bf16[96,2432]{1,0:T(8,128)(2,1)S(1)}, u32[]{:S(2)}, u32[]{:S(2)}) collective-permute-start(bf16[96,2432]{1,0:T(8,128)(2,1)} %get-tuple-element.57), channel_id=1, source_target_pairs={{0,8},{4,12},{8,0},{12,4},{16,24},{20,28},{24,16},{28,20},{1,9},{5... | collective-permute-start | bytes 1400840 | tf_op jit(solution)/shard_map/ppermute | solution.py:458
  348.7 20.2 %collective-permute-start.12 = (bf16[96,2432]{1,0:T(8,128)(2,1)}, bf16[96,2432]{1,0:T(8,128)(2,1)S(1)}, u32[]{:S(2)}, u32[]{:S(2)}) collective-permute-start(bf16[96,2432]{1,0:T(8,128)(2,1)} %get-tuple-element.59), channel_id=1, source_target_pairs={{0,16},{4,20},{8,24},{12,28},{16,0},{20,4},{24,8},{28,12},{1,17},{... | collective-permute-start | bytes 1400840 | tf_op jit(solution)/shard_map/ppermute | solution.py:458
  350.6 19.9 %collective-permute-start.13 = (bf16[96,2432]{1,0:T(8,128)(2,1)}, bf16[96,2432]{1,0:T(8,128)(2,1)S(1)}, u32[]{:S(2)}, u32[]{:S(2)}) collective-permute-start(bf16[96,2432]{1,0:T(8,128)(2,1)} %get-tuple-element.58), channel_id=1, source_target_pairs={{0,24},{4,28},{8,16},{12,20},{16,8},{20,12},{24,0},{28,4},{1,25},{... | collective-permute-start | bytes 1400840 | tf_op jit(solution)/shard_map/ppermute | solution.py:458
  370.8 12.1 %collective-permute-start.14 = (bf16[24,2432]{1,0:T(8,128)(2,1)S(1)}, bf16[24,2432]{1,0:T(8,128)(2,1)S(1)}, u32[]{:S(2)}, u32[]{:S(2)}) collective-permute-start(bf16[24,2432]{1,0:T(8,128)(2,1)S(1)} %get-tuple-element.60), channel_id=1, source_target_pairs={{0,1},{1,0},{2,3},{3,2},{4,5},{5,4},{6,7},{7,6},{8,9},{9,8},{10,11... | collective-permute-start | bytes 350216 | tf_op jit(solution)/shard_map/ppermute | solution.py:458
  371.4 16.4 %collective-permute-start.15 = (bf16[24,2432]{1,0:T(8,128)(2,1)S(1)}, bf16[24,2432]{1,0:T(8,128)(2,1)S(1)}, u32[]{:S(2)}, u32[]{:S(2)}) collective-permute-start(bf16[24,2432]{1,0:T(8,128)(2,1)S(1)} %get-tuple-element.62), channel_id=1, source_target_pairs={{0,2},{1,3},{2,0},{3,1},{4,6},{5,7},{6,4},{7,5},{8,10},{9,11},{10,... | collective-permute-start | bytes 350216 | tf_op jit(solution)/shard_map/ppermute | solution.py:458
  373.9 13.9 %collective-permute-start.16 = (bf16[24,2432]{1,0:T(8,128)(2,1)S(1)}, bf16[24,2432]{1,0:T(8,128)(2,1)S(1)}, u32[]{:S(2)}, u32[]{:S(2)}) collective-permute-start(bf16[24,2432]{1,0:T(8,128)(2,1)S(1)} %get-tuple-element.61), channel_id=1, source_target_pairs={{0,3},{1,2},{2,1},{3,0},{4,7},{5,6},{6,5},{7,4},{8,11},{9,10},{10,... | collective-permute-start | bytes 350216 | tf_op jit(solution)/shard_map/ppermute | solution.py:458
Sparse Core Ops, SparseCore 0:
  12.9 98.3 all-gather.1
  243.4 89.1 reduce-scatter.2
  364.7 37.8 reduce-scatter.4

commit v3 on v2

--- a/solution.py
+++ b/solution.py
@@ -24,6 +24,7 @@
 QB = 256
 CHUNK = 256
 VEC = 128
+DIGITS = 8
 
 
 def dot(left, right, left_dim=1, right_dim=0):
@@ -139,12 +140,17 @@
 
 
 def backward_kernel(
-    low_ref, count_ref, qkv_ref, mixed_ref, grad_ref, rowst_ref, lse_ref, segc_ref, segr_ref, vec_ref,
-    dqkv_ref, dw_ref, columns_ref,
-    q_ref, qt_ref, gt_ref, kt_ref, dqt_ref, acc_ref, delta_ref, sums_ref,
+    chips,
+    low_ref, count_ref, pad_ref, plane_ref, qkv_ref, mixed_ref, grad_ref, rows_ref, lse_ref, segc_ref, segr_ref, vec_ref, stats_ref,
+    dqkv_ref, keep_ref, send_ref,
+    q_ref, qt_ref, gt_ref, kt_ref, dqt_ref, acc_ref, delta_ref, sums_ref, stage_ref, columns_ref, rowst_ref, sem,
 ):
-    g, s = pl.program_id(0), pl.program_id(1)
+    s, g = pl.program_id(0), pl.program_id(1)
     masks = head_masks()
+
+    @pl.when(g == 0)
+    def _():
+        rowst_ref[...] = rows_ref[...].T
 
     @pl.when((g == 0) & (s == 0))
     def _():
@@ -210,43 +216,86 @@
 
     @pl.when(s == 0)
     def _():
-        acc_ref[...] = dw
+        acc_ref[g] = dw
 
     @pl.when(s > 0)
     def _():
-        acc_ref[...] += dw
-
-    @pl.when(s == pl.num_programs(1) - 1)
-    def _():
-        dw_ref[...] = acc_ref[...].astype(BF16)
-
-    @pl.when((g == pl.num_programs(0) - 1) & (s == pl.num_programs(1) - 1))
-    def _():
+        acc_ref[g] += dw
+
+    last_s, last_g = pl.num_programs(0) - 1, pl.num_programs(1) - 1
+
+    def copies(source, lanes, first_sem):
+        if chips == 0:
+            return [pltpu.make_async_copy(source, keep_ref.at[0, :, lanes], sem.at[first_sem])]
+        rows = source.shape[0] // (2 * chips)
+        core, chip = plane_ref[0] & 1, lax.shift_right_logical(plane_ref[0], 1)
+        moves = []
+        for m in range(chips):
+            for side, target in enumerate((keep_ref, send_ref)):
+                owner = 2 * (chip ^ m) + (core ^ side)
+                piece = source.at[pl.ds(pl.multiple_of(owner * rows, rows), rows), :]
+                moves.append(pltpu.make_async_copy(piece, target.at[m, :, lanes], sem.at[first_sem + 2 * m + side]))
+        return moves
+
+    def group_copies(group):
+        return copies(stage_ref, pl.ds(pl.multiple_of(group * TRIPLE, TRIPLE), TRIPLE), 0)
+
+    @pl.when(s == last_s)
+    def _():
+        @pl.when(g > 0)
+        def _():
+            for move in group_copies(g - 1):
+                move.wait()
+
+        stage_ref[...] = acc_ref[g].astype(BF16)
+        for move in group_copies(g):
+            move.start()
+
+    @pl.when((g == last_g) & (s == last_s))
+    def _():
+        for row in range(4):
+            value = jnp.sum(stats_ref[row : row + 1, :], axis=1, keepdims=True)
+            sums_ref[16 + row : 17 + row, :] = jnp.broadcast_to(value, (1, sums_ref.shape[1]))
+        tokens = pl.num_programs(0) * LEN
+        for seq in range(pad_ref.shape[0]):
+            tokens -= pad_ref[seq]
+        for row in range(DIGITS):
+            digit = (lax.shift_right_logical(tokens, 3 * row) & 7).astype(F32)
+            sums_ref[20 + row : 21 + row, :] = jnp.full((1, sums_ref.shape[1]), digit)
         columns_ref[...] = sums_ref[...].T.astype(BF16)
-
-
-def attention_backward(qkv, mixed, grad, rowst, lse, segc, segr, vec, low, count):
+        width = sums_ref.shape[1]
+        moves = copies(columns_ref, slice(3 * width, 3 * width + VEC), max(1, 2 * chips))
+        for move in moves:
+            move.start()
+        for move in group_copies(g) + moves:
+            move.wait()
+
+
+def attention_backward(qkv, mixed, grad, rows, lse, segc, segr, vec, stats, low, count, pad, chips):
     seqs, _, width = mixed.shape
     groups = width // GROUP
+    plane = lax.axis_index("dp").astype(jnp.int32).reshape(1)
+    packed = (max(1, chips), width // max(1, 2 * chips), 3 * width + VEC)
     return pl.pallas_call(
-        backward_kernel,
+        functools.partial(backward_kernel, chips),
         grid_spec=pltpu.PrefetchScalarGridSpec(
-            num_scalar_prefetch=2,
-            grid=(groups, seqs),
+            num_scalar_prefetch=4,
+            grid=(seqs, groups),
             in_specs=[
-                pl.BlockSpec((None, LEN, TRIPLE), lambda g, s, *_: (s, 0, g)),
-                pl.BlockSpec((None, LEN, GROUP), lambda g, s, *_: (s, 0, g)),
-                pl.BlockSpec((None, LEN, GROUP), lambda g, s, *_: (s, 0, g)),
-                pl.BlockSpec((None, width, LEN), lambda g, s, *_: (s, 0, 0)),
-                pl.BlockSpec((None, None, 8, LEN), lambda g, s, *_: (s, g, 0, 0)),
-                pl.BlockSpec((None, LEN, 128), lambda g, s, *_: (s, 0, 0)),
-                pl.BlockSpec((None, 8, LEN), lambda g, s, *_: (s, 0, 0)),
-                pl.BlockSpec((16, width), lambda g, s, *_: (0, 0)),
+                pl.BlockSpec((None, LEN, TRIPLE), lambda s, g, *_: (s, 0, g)),
+                pl.BlockSpec((None, LEN, GROUP), lambda s, g, *_: (s, 0, g)),
+                pl.BlockSpec((None, LEN, GROUP), lambda s, g, *_: (s, 0, g)),
+                pl.BlockSpec((None, LEN, width), lambda s, g, *_: (s, 0, 0)),
+                pl.BlockSpec((None, None, 8, LEN), lambda s, g, *_: (s, g, 0, 0)),
+                pl.BlockSpec((None, LEN, 128), lambda s, g, *_: (s, 0, 0)),
+                pl.BlockSpec((None, 8, LEN), lambda s, g, *_: (s, 0, 0)),
+                pl.BlockSpec((16, width), lambda s, g, *_: (0, 0)),
+                pl.BlockSpec((8, width), lambda s, g, *_: (0, 0)),
             ],
             out_specs=[
-                pl.BlockSpec((None, LEN, TRIPLE), lambda g, s, *_: (s, 0, g)),
-                pl.BlockSpec((width, TRIPLE), lambda g, s, *_: (0, g)),
-                pl.BlockSpec((width, VEC), lambda g, s, *_: (0, 0)),
+                pl.BlockSpec((None, LEN, TRIPLE), lambda s, g, *_: (s, 0, g)),
+                pl.BlockSpec(memory_space=pl.ANY),
+                pl.BlockSpec(memory_space=pl.ANY),
             ],
             scratch_shapes=[
                 pltpu.VMEM((LEN, GROUP), BF16),
@@ -254,200 +303,336 @@
                 pltpu.VMEM((GROUP, LEN), BF16),
                 pltpu.VMEM((GROUP, LEN), BF16),
                 pltpu.VMEM((GROUP, LEN), F32),
-                pltpu.VMEM((width, TRIPLE), F32),
+                pltpu.VMEM((groups, width, TRIPLE), F32),
                 pltpu.VMEM((8, LEN), F32),
                 pltpu.VMEM((VEC, width), F32),
+                pltpu.VMEM((width, TRIPLE), BF16),
+                pltpu.VMEM((width, VEC), BF16),
+                pltpu.VMEM((width, LEN), BF16),
+                pltpu.SemaphoreType.DMA((2 * max(1, 2 * chips),)),
             ],
         ),
         out_shape=[
             jax.ShapeDtypeStruct((seqs, LEN, 3 * width), BF16),
-            jax.ShapeDtypeStruct((width, 3 * width), BF16),
-            jax.ShapeDtypeStruct((width, VEC), BF16),
+            jax.ShapeDtypeStruct(packed, BF16),
+            jax.ShapeDtypeStruct(packed if chips else (8, 128), BF16),
         ],
         compiler_params=pltpu.CompilerParams(vmem_limit_bytes=48 * 2**20),
         cost_estimate=cost(2 * seqs * LEN * width * (3 * width + 32 * LEN), seqs * LEN * width * 20),
         name="attention_backward",
-    )(low, count, qkv, mixed, grad, rowst, lse, segc, segr, vec)
-
-
-def middle_kernel(
+    )(low, count, pad, plane, qkv, mixed, grad, rows, lse, segc, segr, vec, stats)
+
+
+def mean(values):
+    return jnp.mean(values, axis=1, keepdims=True)
+
+
+def normed_of(values):
+    centred = values - mean(values)
+    inverse = lax.rsqrt(mean(centred * centred) + EPSILON)
+    return centred * inverse, inverse
+
+
+def norm_backward(scaled, normed, inverse):
+    return inverse * (scaled - mean(scaled) - normed * mean(scaled * normed))
+
+
+def add_rows(sums_ref, row, values):
+    sums_ref[row] += jnp.sum(values.reshape(-1, 8, values.shape[1]), axis=0)
+
+
+class Blocks:
+    def __init__(self, wide_ref, held_ref, sem, first_step):
+        self.wide_ref, self.held_ref, self.sem, self.first_step = wide_ref, held_ref, sem, first_step
+
+    def copy(self, k):
+        width = self.held_ref.shape[2]
+        columns = pl.ds(pl.multiple_of(k * width, width), width)
+        return pltpu.make_async_copy(self.wide_ref.at[:, columns], self.held_ref.at[k], self.sem.at[k])
+
+    def start(self, order):
+        @pl.when(self.first_step)
+        def _():
+            for k in order:
+                self.copy(k).start()
+
+    def wait(self, k):
+        @pl.when(self.first_step)
+        def _():
+            self.copy(k).wait()
+
+
+def send_block(acc_ref, stage_ref, dw_ref, sem, k, first, last_step, turned):
+    width = stage_ref.shape[1]
+
+    def copy(k):
+        columns = pl.ds(pl.multiple_of(k * width, width), width)
+        slot = lax.rem(k, 2)
+        return pltpu.make_async_copy(stage_ref.at[slot], dw_ref.at[:, columns], sem.at[slot])
+
+    @pl.when(last_step)
+    def _():
+        @pl.when(k >= first + 2)
+        def _():
+            copy(k - 2).wait()
+
+        value = acc_ref[k].astype(BF16)
+        stage_ref[lax.rem(k, 2)] = value.T if turned else value
+        copy(k).start()
+
+
+def upper_kernel(
     parts, width, tokens,
     pad_ref, mixed_ref, rows_ref, cot_ref, w_ref, vec_ref,
-    out_ref, res_ref, mgrad_ref, dw_ref, sums_ref, stats_ref,
-    hidden_ref, slope_ref, first_ref, normed_ref, upper_ref, wide_ref, acc_ref, stage_ref, sem,
+    out_ref, normed_ref, inverse_ref, upper_ref, slope_ref, dw_ref, sums_ref, stats_ref,
+    held_ref, hidden_ref, low_ref, wide_ref, acc_ref, stage_ref, part_ref, w_sem, sem,
 ):
     i = pl.program_id(0)
+    last = i == pl.num_programs(0) - 1
     per_seq = LEN // tokens
+    weights = Blocks(w_ref, held_ref, w_sem, i == 0)
+    weights.start([0] + [k + j for j in range(parts) for k in (1, 1 + parts)])
 
     @pl.when(i == 0)
     def _():
         acc_ref[...] = jnp.zeros_like(acc_ref)
-        sums_ref[...] = jnp.zeros_like(sums_ref)
-        stats_ref[...] = jnp.zeros_like(stats_ref)
-
-    def weight(k):
-        if isinstance(k, int):
-            return w_ref[:, k * width : (k + 1) * width]
-        return w_ref[:, pl.ds(pl.multiple_of(k * width, width), width)]
+        part_ref[...] = jnp.zeros_like(part_ref)
 
     def vector(row):
         return vec_ref[row : row + 1, :]
 
-    def add_sum(row, values):
-        sums_ref[row : row + 1, :] += jnp.sum(values, axis=0, keepdims=True)
-
-    place = (i % per_seq) * tokens + lax.broadcasted_iota(jnp.int32, (tokens, 1), 0)
-    valid = (place < LEN - pad_ref[i // per_seq]).astype(F32)
-
-    def add_stat(row, values):
-        stats_ref[row : row + 1, :] += jnp.sum(valid * values * values, axis=0, keepdims=True)
-
-    def mean(values):
-        return jnp.mean(values, axis=1, keepdims=True)
-
-    def normed_of(values):
-        centred = values - mean(values)
-        inverse = lax.rsqrt(mean(centred * centred) + EPSILON)
-        return centred * inverse, inverse
-
-    def norm_backward(scaled, normed, inverse):
-        return inverse * (scaled - mean(scaled) - normed * mean(scaled * normed))
-
+    def valid_of():
+        place = (i % per_seq) * tokens + lax.broadcasted_iota(jnp.int32, (tokens, 1), 0)
+        return (place < LEN - pad_ref[i // per_seq]).astype(F32)
+
+    weights.wait(0)
+    wide_ref[...] = dot(mixed_ref[...], held_ref[0])
+
+    valid = valid_of()
     rows = rows_ref[...].astype(F32)
-    branch = dot(mixed_ref[...], weight(0)) + vector(0)
-    add_stat(0, rows)
-    add_stat(1, branch)
-    first_normed, first_inverse = normed_of(rows + branch)
-    normed_ref[...] = first_normed
-    first = first_normed * vector(1) + vector(2)
-    first_ref[...] = first.astype(BF16)
-    wide_ref[...] = jnp.zeros_like(wide_ref)
+    branch = wide_ref[...] + vector(0)
+    add_rows(part_ref, 3, valid * rows * rows)
+    add_rows(part_ref, 4, valid * branch * branch)
+    normed, inverse = normed_of(rows + branch)
+    normed_ref[...] = normed
+    inverse_ref[...] = jnp.broadcast_to(inverse, (tokens, 128))
+    first = normed * vector(1) + vector(2)
+    low_ref[...] = first.astype(BF16)
+    wide_ref[...] = first + vector(3)
 
     def feed(j, carry):
-        inner = dot(first_ref[...], weight(1 + j)) + vec_ref[pl.ds(6 + j, 1), :]
+        weights.wait(1 + j)
+        weights.wait(1 + parts + j)
+        inner = dot(low_ref[...], held_ref[1 + j]) + vec_ref[pl.ds(6 + j, 1), :]
         half = 0.5 * (1.0 + lax.erf(inner * ROOT_HALF))
         hidden = (inner * half).astype(BF16)
         hidden_ref[j] = hidden
-        slope_ref[j] = (half + inner * jnp.exp(-0.5 * inner * inner) * INV_ROOT_TWO_PI).astype(BF16)
-        wide_ref[...] += dot(hidden, weight(1 + parts + j))
+        slope = half + inner * jnp.exp(-0.5 * inner * inner) * INV_ROOT_TWO_PI
+        slope_ref[:, pl.ds(pl.multiple_of(j * width, width), width)] = slope.astype(BF16)
+        wide_ref[...] += dot(hidden, held_ref[1 + parts + j])
         return carry
 
     lax.fori_loop(0, parts, feed, 0)
-    second = wide_ref[...] + vector(3)
-    add_stat(2, second)
-    second_normed, second_inverse = normed_of(first + second)
-    result = second_normed * vector(4) + vector(5)
-    add_stat(3, result)
+
+    valid = valid_of()
+    total = wide_ref[...]
+    second = total - (normed_ref[...] * vector(1) + vector(2))
+    add_rows(part_ref, 5, valid * second * second)
+    normed, inverse = normed_of(total)
+    result = normed * vector(4) + vector(5)
+    add_rows(part_ref, 6, valid * result * result)
     out_ref[...] = result.astype(BF16)
     upstream = cot_ref[...].astype(F32) * valid
-    add_sum(0, upstream * second_normed)
-    add_sum(1, upstream)
-    upper = norm_backward(upstream * vector(4), second_normed, second_inverse)
+    add_rows(part_ref, 0, upstream * normed)
+    add_rows(part_ref, 1, upstream)
+    upper = norm_backward(upstream * vector(4), normed, inverse)
+    upper_ref[...] = upper
     upper_low = upper.astype(BF16)
-    upper_ref[...] = upper_low
-    add_sum(2, upper_low.astype(F32))
+    add_rows(part_ref, 2, upper_low.astype(F32))
+    low_ref[...] = upper_low
+
+    upper_t = low_ref[...].T
+
+    def back(j, carry):
+        acc_ref[j] += dot(upper_t, hidden_ref[j])
+        send_block(acc_ref, stage_ref, dw_ref, sem, j, 0, last, True)
+        return carry
+
+    lax.fori_loop(0, parts, back, 0)
+
+    @pl.when(last)
+    def _():
+        sums_ref[...] = jnp.zeros_like(sums_ref)
+        for row in range(3):
+            sums_ref[row : row + 1, :] = jnp.sum(part_ref[row], axis=0, keepdims=True)
+        for row in range(4):
+            stats_ref[row : row + 1, :] = jnp.sum(part_ref[3 + row], axis=0, keepdims=True)
+        stats_ref[4:, :] = jnp.zeros_like(stats_ref[4:, :])
+        for k in (parts - 2, parts - 1):
+            out_copy(stage_ref, dw_ref, sem, k).wait()
+
+
+def lower_kernel(
+    parts, width, tokens,
+    mixed_ref, normed_ref, inverse_ref, upper_ref, slope_ref, w_ref, vec_ref, sums_in_ref,
+    res_ref, mgrad_ref, dw_ref, sums_ref,
+    held_ref, low_ref, first_ref, wide_ref, acc_ref, stage_ref, part_ref, w_sem, sem,
+):
+    i = pl.program_id(0)
+    last = i == pl.num_programs(0) - 1
+    weights = Blocks(w_ref, held_ref, w_sem, i == 0)
+    weights.start([k + j for j in range(parts) for k in (1 + parts, 1)] + [0])
+
+    @pl.when(i == 0)
+    def _():
+        acc_ref[...] = jnp.zeros_like(acc_ref)
+        part_ref[...] = jnp.zeros_like(part_ref)
+
+    def vector(row):
+        return vec_ref[row : row + 1, :]
+
+    upper = upper_ref[...]
     wide_ref[...] = upper
-    upper_t = upper_low.T
+    low_ref[...] = upper.astype(BF16)
+    first_ref[...] = (normed_ref[...] * vector(1) + vector(2)).astype(BF16)
+
     first_t = first_ref[...].T
 
     def back(j, carry):
-        acc_ref[1 + parts + j] += dot(upper_t, hidden_ref[j])
-        inner_low = (dot(upper_ref[...], weight(1 + parts + j), 1, 1) * slope_ref[j].astype(F32)).astype(BF16)
-        sums_ref[pl.ds(8 + j, 1), :] += jnp.sum(inner_low.astype(F32), axis=0, keepdims=True)
+        weights.wait(1 + parts + j)
+        weights.wait(1 + j)
+        slope = slope_ref[:, pl.ds(pl.multiple_of(j * width, width), width)].astype(F32)
+        inner_low = (dot(low_ref[...], held_ref[1 + parts + j], 1, 1) * slope).astype(BF16)
+        add_rows(part_ref, 3 + j, inner_low.astype(F32))
         acc_ref[1 + j] += dot(first_t, inner_low)
-        wide_ref[...] += dot(inner_low, weight(1 + j), 1, 1)
+        wide_ref[...] += dot(inner_low, held_ref[1 + j], 1, 1)
+        send_block(acc_ref, stage_ref, dw_ref, sem, 1 + j, 1, last, False)
         return carry
 
     lax.fori_loop(0, parts, back, 0)
+
     first_grad = wide_ref[...]
-    first_normed = normed_ref[...]
-    add_sum(3, first_grad * first_normed)
-    add_sum(4, first_grad)
-    residual = norm_backward(first_grad * vector(1), first_normed, first_inverse)
+    normed = normed_ref[...]
+    add_rows(part_ref, 0, first_grad * normed)
+    add_rows(part_ref, 1, first_grad)
+    residual = norm_backward(first_grad * vector(1), normed, inverse_ref[:, :1])
     res_ref[...] = residual
     branch_low = residual.astype(BF16)
-    add_sum(5, branch_low.astype(F32))
-    acc_ref[0] += dot(mixed_ref[...], branch_low, 0, 0)
-    mgrad_ref[...] = dot(branch_low, weight(0), 1, 1).astype(BF16)
-
-    @pl.when(i == pl.num_programs(0) - 1)
-    def _():
-        def copy(k, slot):
-            columns = pl.ds(pl.multiple_of(k * width, width), width)
-            return pltpu.make_async_copy(stage_ref.at[slot], dw_ref.at[:, columns], sem.at[slot])
-
-        def flush(k, carry):
-            slot = lax.rem(k, 2)
-
-            @pl.when(k >= 2)
-            def _():
-                copy(k - 2, slot).wait()
-
-            @pl.when(k > parts)
-            def _():
-                stage_ref[slot] = acc_ref[k].astype(BF16).T
-
-            @pl.when(k <= parts)
-            def _():
-                stage_ref[slot] = acc_ref[k].astype(BF16)
-
-            copy(k, slot).start()
-            return carry
-
-        lax.fori_loop(0, 1 + 2 * parts, flush, 0)
-        copy(2 * parts - 1, (2 * parts - 1) % 2).wait()
-        copy(2 * parts, (2 * parts) % 2).wait()
-
-
-def middle(mixed, rows, cotangent, w, vec, pad):
+    add_rows(part_ref, 2, branch_low.astype(F32))
+    low_ref[...] = branch_low
+
+    weights.wait(0)
+    acc_ref[0] += dot(mixed_ref[...], low_ref[...], 0, 0)
+    mgrad_ref[...] = dot(low_ref[...], held_ref[0], 1, 1).astype(BF16)
+
+    @pl.when(last)
+    def _():
+        sums_ref[...] = sums_in_ref[...]
+        for row in range(3):
+            sums_ref[3 + row : 4 + row, :] = jnp.sum(part_ref[row], axis=0, keepdims=True)
+        for j in range(parts):
+            sums_ref[8 + j : 9 + j, :] = jnp.sum(part_ref[3 + j], axis=0, keepdims=True)
+        for k in (parts - 1, parts):
+            out_copy(stage_ref, dw_ref, sem, k).wait()
+        stage_ref[0] = acc_ref[0].astype(BF16)
+        out_copy(stage_ref, dw_ref, sem, 0).start()
+        out_copy(stage_ref, dw_ref, sem, 0).wait()
+
+
+def out_copy(stage_ref, dw_ref, sem, k):
+    width = stage_ref.shape[1]
+    return pltpu.make_async_copy(stage_ref.at[k % 2], dw_ref.at[:, k * width : (k + 1) * width], sem.at[k % 2])
+
+
+def upper_half(mixed, rows, cotangent, w, vec, pad, tokens=512):
     count, width = mixed.shape
-    tokens = 256
     parts = (w.shape[1] // width - 1) // 2
-    block = pl.BlockSpec((tokens, width), lambda i, *_: (i, 0))
+
+    def block(columns):
+        return pl.BlockSpec((tokens, columns), lambda i, *_: (i, 0))
+
+    def fixed(*shape):
+        return pl.BlockSpec(shape, lambda i, *_: (0, 0))
+
+    anywhere = pl.BlockSpec(memory_space=pl.ANY)
     return pl.pallas_call(
-        functools.partial(middle_kernel, parts, width, tokens),
+        functools.partial(upper_kernel, parts, width, tokens),
         grid_spec=pltpu.PrefetchScalarGridSpec(
             num_scalar_prefetch=1,
             grid=(count // tokens,),
-            in_specs=[
-                block,
-                block,
-                block,
-                pl.BlockSpec(w.shape, lambda i, *_: (0, 0), pipeline_mode=pl.Buffered(1)),
-                pl.BlockSpec(vec.shape, lambda i, *_: (0, 0)),
-            ],
+            in_specs=[block(width), block(width), block(width), anywhere, fixed(16, width)],
             out_specs=[
-                block,
-                block,
-                block,
-                pl.BlockSpec(memory_space=pl.ANY),
-                pl.BlockSpec((16, width), lambda i, *_: (0, 0)),
-                pl.BlockSpec((8, width), lambda i, *_: (0, 0)),
+                block(width), block(width), block(128), block(width), block(parts * width), anywhere,
+                fixed(16, width), fixed(8, width),
             ],
             scratch_shapes=[
-                pltpu.VMEM((parts, tokens, width), BF16),
+                pltpu.VMEM((1 + 2 * parts, width, width), BF16),
                 pltpu.VMEM((parts, tokens, width), BF16),
                 pltpu.VMEM((tokens, width), BF16),
                 pltpu.VMEM((tokens, width), F32),
-                pltpu.VMEM((tokens, width), BF16),
-                pltpu.VMEM((tokens, width), F32),
-                pltpu.VMEM((1 + 2 * parts, width, width), F32),
+                pltpu.VMEM((parts, width, width), F32),
                 pltpu.VMEM((2, width, width), BF16),
+                pltpu.VMEM((8, 8, width), F32),
+                pltpu.SemaphoreType.DMA((1 + 2 * parts,)),
                 pltpu.SemaphoreType.DMA((2,)),
             ],
         ),
         out_shape=[
             jax.ShapeDtypeStruct((count, width), BF16),
             jax.ShapeDtypeStruct((count, width), F32),
-            jax.ShapeDtypeStruct((count, width), BF16),
-            jax.ShapeDtypeStruct((width, (1 + 2 * parts) * width), BF16),
+            jax.ShapeDtypeStruct((count, 128), F32),
+            jax.ShapeDtypeStruct((count, width), F32),
+            jax.ShapeDtypeStruct((count, parts * width), BF16),
+            jax.ShapeDtypeStruct((width, parts * width), BF16),
             jax.ShapeDtypeStruct((16, width), F32),
             jax.ShapeDtypeStruct((8, width), F32),
         ],
         compiler_params=pltpu.CompilerParams(vmem_limit_bytes=60 * 2**20),
-        cost_estimate=cost(12 * count * width * w.shape[1], count * width * 14 + 4 * w.size),
-        name="middle",
+        cost_estimate=cost(2 * count * width * width * (1 + 3 * parts), count * width * 40 + 4 * w.size),
+        name="upper_half",
     )(pad, mixed, rows, cotangent, w, vec)
+
+
+def lower_half(mixed, normed, inverse, upper, slope, w, vec, sums, tokens=512):
+    count, width = mixed.shape
+    parts = (w.shape[1] // width - 1) // 2
+
+    def block(columns):
+        return pl.BlockSpec((tokens, columns), lambda i: (i, 0))
+
+    def fixed(*shape):
+        return pl.BlockSpec(shape, lambda i: (0, 0))
+
+    anywhere = pl.BlockSpec(memory_space=pl.ANY)
+    return pl.pallas_call(
+        functools.partial(lower_kernel, parts, width, tokens),
+        grid=(count // tokens,),
+        in_specs=[
+            block(width), block(width), block(128), block(width), block(parts * width), anywhere,
+            fixed(16, width), fixed(16, width),
+        ],
+        out_specs=[block(width), block(width), anywhere, fixed(16, width)],
+        scratch_shapes=[
+            pltpu.VMEM((1 + 2 * parts, width, width), BF16),
+            pltpu.VMEM((tokens, width), BF16),
+            pltpu.VMEM((tokens, width), BF16),
+            pltpu.VMEM((tokens, width), F32),
+            pltpu.VMEM((1 + parts, width, width), F32),
+            pltpu.VMEM((2, width, width), BF16),
+            pltpu.VMEM((3 + parts, 8, width), F32),
+            pltpu.SemaphoreType.DMA((1 + 2 * parts,)),
+            pltpu.SemaphoreType.DMA((2,)),
+        ],
+        out_shape=[
+            jax.ShapeDtypeStruct((count, width), F32),
+            jax.ShapeDtypeStruct((count, width), BF16),
+            jax.ShapeDtypeStruct((width, (1 + parts) * width), BF16),
+            jax.ShapeDtypeStruct((16, width), F32),
+        ],
+        compiler_params=pltpu.CompilerParams(vmem_limit_bytes=60 * 2**20),
+        cost_estimate=cost(2 * count * width * width * (2 + 3 * parts), count * width * 40 + 4 * w.size),
+        name="lower_half",
+    )(mixed, normed, inverse, upper, slope, w, vec, sums)
 
 
 def gather(shard):
@@ -469,7 +654,7 @@
 def quick_gather(shard):
     planes, columns = lax.axis_size("dp"), lax.axis_size("fsdp")
     rows, width = shard.shape
-    if planes % 2 or rows % 8:
+    if not quick(rows):
         return gather(shard)
     column = jnp.stack([shard] + [swap(shard, "fsdp", k) for k in range(1, columns)])
     even = [column] + [swap(column, "dp", m) for m in range(2, planes, 2)]
@@ -491,44 +676,43 @@
     return whole.reshape(planes * columns * rows, width)
 
 
-def quick_scatter(partial):
-    planes, columns = lax.axis_size("dp"), lax.axis_size("fsdp")
-    rows = partial.shape[0] // (planes * columns)
-    if planes % 2 or rows % 8:
-        return scatter(partial)
-    plane, column = lax.axis_index("dp"), lax.axis_index("fsdp")
-    core, chip = plane % 2, plane // 2
-
-    def pick(values, index, axis=0):
-        return lax.dynamic_index_in_dim(values, index, axis, keepdims=False)
-
-    halves = partial.reshape(planes // 2, 2, columns * rows, -1)
-    other = swap(pick(halves, 1 - core, 1), "dp", 1)
-    chips = (pick(halves, core, 1).astype(F32) + other.astype(F32)).astype(partial.dtype)
-    arrived = [swap(pick(chips, chip ^ m), "dp", 2 * m) for m in range(1, planes // 2)]
-    own = pick(chips, chip).astype(F32)
-    for part in arrived:
-        own = own + part.astype(F32)
-    own = own.astype(partial.dtype).reshape(columns, rows, -1)
-    arrived = [swap(pick(own, column ^ k), "fsdp", k) for k in range(1, columns)]
-    own = pick(own, column).astype(F32)
-    for part in arrived:
-        own = own + part.astype(F32)
-    return own
-
-
-def scatter(partial):
-    partial = lax.psum_scatter(partial, "dp", scatter_dimension=0, tiled=True)
+def tree_sum(parts):
+    parts = [part.astype(F32) for part in parts]
+    while len(parts) > 1:
+        parts = [a + b for a, b in zip(parts[::2], parts[1::2])]
+    return parts[0]
+
+
+def quick(rows):
+    return lax.axis_size("dp") % 2 == 0 and rows % 8 == 0
+
+
+def pick(values, index):
+    return lax.dynamic_index_in_dim(values, index, 0, keepdims=False)
+
+
+def over_planes(partial):
+    return lax.psum_scatter(partial, "dp", scatter_dimension=0, tiled=True)
+
+
+def over_columns(partial):
     return lax.psum_scatter(partial, "fsdp", scatter_dimension=0, tiled=True)
 
 
-def total_over_devices(values):
-    for axis, flips in (("dp", [1]), ("dp", range(2, lax.axis_size("dp"), 2)), ("fsdp", range(1, lax.axis_size("fsdp")))):
-        parts = [values] + [swap(values, axis, flip) for flip in flips]
-        while len(parts) > 1:
-            parts = [a + b for a, b in zip(parts[::2], parts[1::2])]
-        values = parts[0]
-    return values
+def join_planes(keep, send):
+    other = swap(send, "dp", 1)
+    parts = [tree_sum([keep[m], other[m]]).astype(keep.dtype) for m in range(keep.shape[0])]
+    return tree_sum(parts[:1] + [swap(parts[m], "dp", 2 * m) for m in range(1, len(parts))]).astype(keep.dtype)
+
+
+def blocks_for_columns(partial):
+    columns = lax.axis_size("fsdp")
+    blocks = partial.reshape(columns, partial.shape[0] // columns, partial.shape[1])
+    return [pick(blocks, lax.axis_index("fsdp") ^ k) for k in range(columns)]
+
+
+def join_blocks(blocks):
+    return tree_sum(blocks[:1] + [swap(block, "fsdp", k) for k, block in enumerate(blocks) if k])
 
 
 def per_device(
@@ -551,15 +735,13 @@
         for g in range(groups)
         for mat in (query_weight, key_weight, value_weight)
     ]
+    segment, low, count = segments(doc_lengths, pad_tail)
+    segc = jnp.broadcast_to(segment[:, :, None], (seqs, LEN, 128))
+    segr = jnp.broadcast_to(segment[:, None, :], (seqs, 8, LEN))
     near = quick_gather(jnp.concatenate(triples + [columns], axis=1))
     inner_own = inner_weight.reshape(own, devices, parts, own).transpose(0, 2, 1, 3).reshape(own, parts * width)
     outer_own = outer_weight.reshape(parts, own, width).transpose(1, 0, 2).reshape(own, parts * width)
     far = gather(jnp.concatenate([merge_weight, inner_own, outer_own], axis=1))
-
-    segment, low, count = segments(doc_lengths, pad_tail)
-    segc = jnp.broadcast_to(segment[:, :, None], (seqs, LEN, 128))
-    segr = jnp.broadcast_to(segment[:, None, :], (seqs, 8, LEN))
-    rowst = jnp.swapaxes(layer_input, 1, 2)
 
     vec_rows = near[:, 3 * width :].T.astype(F32)
     bias = jnp.stack([vec_rows[0], jnp.zeros((width,), F32), vec_rows[1]])
@@ -569,29 +751,43 @@
 
     qkv, mixed, lse = attention_forward(layer_input, near, bias, segc, segr, low, count)
     tokens = seqs * LEN
-    output, residual, mixed_grad, far_partial, sums, stats = middle(
-        mixed.reshape(tokens, width), layer_input.reshape(tokens, width), cotangent.reshape(tokens, width), far, vec, pad_tail
+    flat_mixed = mixed.reshape(tokens, width)
+    output, normed, inverse, upper, slope, outer_partial, sums, stats = upper_half(
+        flat_mixed, layer_input.reshape(tokens, width), cotangent.reshape(tokens, width), far, vec, pad_tail
     )
-    far_grad = scatter(far_partial)
-    valid_count = jnp.sum(LEN - pad_tail).astype(F32)
-    stat_row = jnp.concatenate([jnp.sum(stats[:4], axis=1), valid_count[None], jnp.zeros((VEC - 5,), F32)])
-    totals = total_over_devices(jnp.broadcast_to(stat_row, (8, VEC)))[0]
-    dqkv, near_partial, near_columns = attention_backward(
-        qkv, mixed, mixed_grad.reshape(mixed.shape), rowst, lse, segc, segr, sums, low, count
+    outer_grad = over_planes(outer_partial)
+    residual, mixed_grad, inner_partial, sums = lower_half(flat_mixed, normed, inverse, upper, slope, far, vec, sums)
+    inner_grad = over_planes(inner_partial)
+    chips = lax.axis_size("dp") // 2 if quick(own) else 0
+    dqkv, keep, send = attention_backward(
+        qkv, mixed, mixed_grad.reshape(mixed.shape), layer_input, lse, segc, segr, sums, stats, low, count, pad_tail, chips
     )
-    near_grad = quick_scatter(jnp.concatenate([near_partial, near_columns], axis=1)).astype(F32)
+    if chips:
+        far_blocks = blocks_for_columns(jnp.concatenate([inner_grad, outer_grad], axis=1))
+        keep, send, far_blocks = lax.optimization_barrier((keep, send, far_blocks))
+        far_grad = join_blocks(far_blocks)
+        near_grad = join_blocks(blocks_for_columns(join_planes(keep, send)))
+    else:
+        far_grad = over_columns(jnp.concatenate([inner_grad, outer_grad], axis=1)).astype(F32)
+        near_grad = over_columns(over_planes(keep[0])).astype(F32)
+    residual, far_grad = lax.optimization_barrier((residual, far_grad))
     input_gradient = residual + dot(dqkv.reshape(tokens, 3 * width), near[:, : 3 * width], 1, 1)
 
     mine = near_grad[:, 3 * width :].T
     inner_bias_gradient = mine[8 : 8 + parts].reshape(parts * own)
     triple = near_grad[:, : 3 * width].reshape(own, groups, 3, GROUP)
     query_grad, key_grad, value_grad = (triple[:, :, k].reshape(own, width) for k in range(3))
-    far_grad = far_grad.astype(F32)
     inner_grad = far_grad[:, width : (1 + parts) * width]
     inner_grad = inner_grad.reshape(own, parts, devices, own).transpose(0, 2, 1, 3).reshape(own, parts * width)
     outer_grad = far_grad[:, (1 + parts) * width :].reshape(own, parts, width).transpose(1, 0, 2)
     all_tokens = tokens * devices
-    valid_total = totals[4]
+    if quick(own):
+        totals = mine[16 : 20 + DIGITS, 0]
+        valid_total = sum(totals[4 + digit] * 8.0**digit for digit in range(DIGITS))
+    else:
+        valid_own = jnp.sum(LEN - pad_tail).astype(F32)
+        totals = lax.psum(jnp.concatenate([jnp.sum(stats[:4], axis=1), valid_own[None]]), AXES)
+        valid_total = totals[4]
     share = jnp.reshape(valid_total / all_tokens, (1,))
     layer_stats = jnp.concatenate([share, jnp.sqrt(totals[:4] / (valid_total * width))])
     return (

time: 420 us -> 411 us (0.979)
  Pallas kernels: 248 us -> 226 us
  waiting for transfers between devices: 66.3 us -> 80.8 us
  local copies, waits for them, and re-layouts: 33.4 us -> 23.9 us
    ppermute x24 -> x20, waiting for transfers between devices: 55.8 us -> 70.6 us  [swap(): lax.ppermute(values, axis, [(d, d ^ flip) for d in range(lax.axis_size(ax...]
    pallas_call x2 -> x3, Pallas kernels: 194 us -> 182 us  [the longest x1 65.7 us: upper_half(): pl.pallas_call(functools.partial(upper_kernel, parts, width, tokens), gri...]
    pallas_call x1, Pallas kernels: 50.1 us -> 42 us  [attention_forward(): pl.pallas_call(forward_kernel, grid_spec=pltpu.PrefetchScalarGridSpec(num...]
    unnamed x57 -> x60, local copies, waits for them, and re-layouts: 13.1 us -> 5.84 us
    ppermute x24 -> x20, starting transfers between devices: 31.6 us -> 34.8 us  [swap(): lax.ppermute(values, axis, [(d, d ^ flip) for d in range(lax.axis_size(ax...]
  transfers between devices with their start and end apart: 27 -> 23, of which waited for: 13 -> 13; matrix products, arithmetic and copies ran while one was open for 8% -> 6% of each run, Pallas kernels for 30% -> 40%
where the time goes in v3:
time: 411 us; the launch traced here: 405 us
  Pallas kernels  226 us (55%)
  waiting for transfers between devices  80.8 us (20%)
  starting transfers between devices  35 us (9%)
  local copies, waits for them, and re-layouts  23.9 us (6%)
  between operations  19.9 us (5%)
  matrix products  13 us (3%)
  other arithmetic  5.91 us (1%)
    ppermute x20, waiting for transfers between devices, swap(): lax.ppermute(values, axis, [(d, d ^ flip) for d in range(lax.axis_size(ax...  70.6 us
    pallas_call x1, Pallas kernels, upper_half(): pl.pallas_call(functools.partial(upper_kernel, parts, width, tokens), gri...  65.7 us
    pallas_call x1, Pallas kernels, attention_backward(): pl.pallas_call(functools.partial(backward_kernel, chips), grid_spec=pltpu...  62.2 us
    pallas_call x1, Pallas kernels, lower_half(): pl.pallas_call(functools.partial(lower_kernel, parts, width, tokens), gri...  53.8 us
    pallas_call x1, Pallas kernels, attention_forward(): pl.pallas_call(forward_kernel, grid_spec=pltpu.PrefetchScalarGridSpec(num...  42 us
    ppermute x20, starting transfers between devices, swap(): lax.ppermute(values, axis, [(d, d ^ flip) for d in range(lax.axis_size(ax...  34.8 us
    dot_general x1, matrix products, dot(): lax.dot_general(left, right, (((left_dim,), (right_dim,)), ((), ())), pre...  13 us
    reduce_scatter x2, waiting for transfers between devices, over_planes(): return lax.psum_scatter(partial, 'dp', scatter_dimension=0, tiled=True)  8.25 us
  transfers between devices with their start and end apart: 23, of which 13 were waited for; matrix products, arithmetic and copies ran while one was open for 6% of the time, Pallas kernels for 40%

profile of v3, /device:TPU:0, one launch (start us, length us, event | category | flops | bytes accessed | tf_op | source)
XLA Modules:
  0.0 404.9 jit_solution(17818746383251840250)
XLA Ops:
  7.4 1.0 copy.87
  8.4 2.1 reshape.223
  10.7 1.3 reshape.224
  12.0 0.7 pad_maximum_fusion.2
  14.1 5.1 %collective-permute-start.2 = (bf16[24,2432]{1,0:T(8,128)(2,1)S(1)}, bf16[24,2432]{1,0:T(8,128)(2,1)S(1)}, u32[]{:S(2)}, u32[]{:S(2)}) collective-permute-start(bf16[24,2432]{1,0:T(8,128)(2,1)S(1)} %constant_dynamic-update-slice_fusion), channel_id=1, source_target_pairs={{0,3},{1,2},{2,1},{3,0},{4,7},{5,6},{6,5},{7,4},{8,11},{9,10},{10,... | collective-permute-start | bytes 350216 | tf_op jit(solution)/shard_map/ppermute | solution.py:643
  19.2 0.6 collective-permute-start
  19.9 0.2 reduce_window_sum.11
  20.1 3.2 collective-permute-done.2
  23.3 8.3 %collective-permute-done.1 = bf16[24,2432]{1,0:T(8,128)(2,1)S(1)} collective-permute-done((bf16[24,2432]{1,0:T(8,128)(2,1)S(1)}, bf16[24,2432]{1,0:T(8,128)(2,1)S(1)}, u32[]{:S(2)}, u32[]{:S(2)}) %collective-permute-start.1) | collective-permute-done | bytes 116768 | tf_op jit(solution)/shard_map/ppermute | solution.py:643
  31.7 2.7 collective-permute-start.8
  34.4 0.3 collective-permute-start.6
  34.7 0.5 collective-permute-start.4
  35.6 0.2 select_reduce_fusion
  35.9 10.4 %collective-permute-done.8.refs_6_ = bf16[4,24,2432]{2,1,0:T(8,128)(2,1)S(1)} collective-permute-done((bf16[4,24,2432]{2,1,0:T(8,128)(2,1)S(1)}, bf16[4,24,2432]{2,1,0:T(8,128)(2,1)S(1)}, u32[]{:S(2)}, u32[]{:S(2)}) %collective-permute-start.8) | collective-permute-done | bytes 466976 | tf_op jit(solution)/shard_map/ppermute | solution.py:643
  46.3 8.4 %collective-permute-done.6.refs_4_ = bf16[4,24,2432]{2,1,0:T(8,128)(2,1)S(1)} collective-permute-done((bf16[4,24,2432]{2,1,0:T(8,128)(2,1)S(1)}, bf16[4,24,2432]{2,1,0:T(8,128)(2,1)S(1)}, u32[]{:S(2)}, u32[]{:S(2)}) %collective-permute-start.6) | collective-permute-done | bytes 466976 | tf_op jit(solution)/shard_map/ppermute | solution.py:643
  54.7 3.9 collective-permute-done.4.refs_2_
  58.9 1.6 collective-permute-done.5.refs_3_
  60.5 2.6 place.1
  63.1 0.9 slice.211
  64.2 0.6 slice.214.vec_ref
  65.0 0.3 broadcast_in_dim.53.segc_ref
  65.3 42.0 %attention_forward.1 = (bf16[2,1024,2304]{2,1,0:T(8,128)(2,1)}, bf16[2,1024,768]{2,1,0:T(8,128)(2,1)S(1)}, f32[2,3,8,1024]{3,2,1,0:T(8,128)S(1)}) custom-call(s32[2,4]{1,0:T(2,128)S(1)} %get-tuple-element.83.low_ref, s32[2,4]{1,0:T(2,128)S(1)} %get-tuple-element.84.count_ref, bf16[2,1024,768]{2,1,0:T(8,128)(2,1)} %rows_ref.3, bf16[768,2432]{1,0:T(8,128)(2,1)} %bitcast.96, ...), custom_call_target="tpu_custom_call" | custom-call | flops 58787364864 | bytes 15728640 | tf_op jit(solution)/shard_map/attention_forward/pallas_call | solution.py:112
  107.3 1.6 copy-done.4
  109.0 1.9 all-gather.2.cloned.1.call-done.w_ref
  110.8 65.7 %upper_half.1 = (bf16[2048,768]{1,0:T(8,128)(2,1)}, f32[2048,768]{1,0:T(8,128)}, f32[2048,128]{1,0:T(8,128)}, f32[2048,768]{1,0:T(8,128)}, bf16[2048,3072]{1,0:T...) custom-call(s32[2]{0:T(128)} %pad_ref.3, bf16[2048,768]{1,0:T(8,128)(2,1)} %bitcast.91, ...), custom_call_target="tpu_custom_call" | custom-call | flops 31406948352 | bytes 84148224 | tf_op jit(solution)/shard_map/upper_half/pallas_call | solution.py:558
  176.7 53.8 %lower_half.1 = (f32[2048,768]{1,0:T(8,128)}, bf16[2048,768]{1,0:T(8,128)(2,1)}, bf16[768,3840]{1,0:T(8,128)(2,1)}, f32[16,768]{1,0:T(8,128)}) custom-call(bf16[2048,768]{1,0:T(8,128)(2,1)} %bitcast.92, f32[2048,768]{1,0:T(8,128)} %get-tuple-element.46.normed_ref, f32[2048,128]{1,0:T(8,128)} %get-tuple-element.47.inverse_ref, ...), custom_call_target="tpu_custom_call" | custom-call | flops 33822867456 | bytes 84148224 | tf_op jit(solution)/shard_map/lower_half/pallas_call | solution.py:607
  230.6 0.6 copy-done.3
  231.2 0.2 copy-done.5
  231.3 62.2 %attention_backward.1 = (bf16[2,1024,2304]{2,1,0:T(8,128)(2,1)}, bf16[4,96,2432]{2,1,0:T(8,128)(2,1)S(1)}, bf16[4,96,2432]{2,1,0:T(8,128)(2,1)S(1)}) custom-call(s32[2,4]{1,0:T(2,128)S(1)} %get-tuple-element.83.low_ref, s32[2,4]{1,0:T(2,128)S(1)} %get-tuple-element.84.count_ref, s32[2]{0:T(128)S(1)} %copy-done.3, s32[1]{0:T(128)} %bitcast.1.plane_ref, ...), custom_call_target="tpu_custom_call" | custom-call | flops 110326972416 | bytes 31457280 | tf_op jit(solution)/shard_map/attention_backward/pallas_call | solution.py:279
  293.5 1.2 copy-done
  294.8 8.2 %reduce-scatter.3.cloned.1.call-done = bf16[96,3840]{1,0:T(8,128)(2,1)} async-done(((bf16[768,3840]{1,0:T(8,128)(2,1)}), bf16[96,3840]{1,0:T(8,128)(2,1)}) %reduce-scatter.3.cloned.1.call-update) | async-done | bytes 737296 | tf_op jit(solution)/shard_map/reduce_scatter | solution.py:695
  303.0 1.5 pad_maximum_fusion
  304.7 1.5 collective-permute-start.10
  306.2 11.9 %collective-permute-start.11 = (bf16[24,6912]{1,0:T(8,128)(2,1)S(1)}, bf16[24,6912]{1,0:T(8,128)(2,1)S(1)}, u32[]{:S(2)}, u32[]{:S(2)}) collective-permute-start(bf16[24,6912]{1,0:T(8,128)(2,1)S(1)} %get-tuple-element.63), channel_id=1, source_target_pairs={{0,2},{1,3},{2,0},{3,1},{4,6},{5,7},{6,4},{7,5},{8,10},{9,11},{10,... | collective-permute-start | bytes 995336 | tf_op jit(solution)/shard_map/ppermute | solution.py:643
  318.1 22.4 %collective-permute-done.11 = bf16[24,6912]{1,0:T(8,128)(2,1)S(1)} collective-permute-done((bf16[24,6912]{1,0:T(8,128)(2,1)S(1)}, bf16[24,6912]{1,0:T(8,128)(2,1)S(1)}, u32[]{:S(2)}, u32[]{:S(2)}) %collective-permute-start.11) | collective-permute-done | bytes 331808 | tf_op jit(solution)/shard_map/ppermute | solution.py:643
  340.5 0.2 add_add_fusion
  340.6 0.4 fusion.8
  341.0 0.3 collective-permute-start.14
  341.3 0.7 collective-permute-start.16
  342.0 2.6 collective-permute-start.15
  344.6 13.0 %fusion.2 = f32[2048,768]{1,0:T(8,128)} fusion(f32[2048,768]{1,0:T(8,128)} %get-tuple-element.65, bf16[2048,2304]{1,0:T(8,128)(2,1)} %bitcast.128, bf16[768,2432]{1,0:T(8,128)(2,1)S(1)} %bitcast.97), kind=kOutput, calls=%fused_computation.2 | convolution fusion | flops 7249330176 | bytes 25559040 | tf_op jit(solution)/shard_map/dot_general | solution.py:31
  357.5 2.9 collective-permute-done.16
  360.4 5.2 %collective-permute-done.15 = bf16[96,2432]{1,0:T(8,128)(2,1)S(1)} collective-permute-done((bf16[96,2432]{1,0:T(8,128)(2,1)S(1)}, bf16[96,2432]{1,0:T(8,128)(2,1)S(1)}, u32[]{:S(2)}, u32[]{:S(2)}) %collective-permute-start.15) | collective-permute-done | bytes 466976 | tf_op jit(solution)/shard_map/ppermute | solution.py:643
  365.7 0.3 fusion.6
  366.0 0.8 dynamic-slice_bitcast_fusion.6
  366.8 7.0 %collective-permute-start.17 = (bf16[24,2432]{1,0:T(8,128)(2,1)}, bf16[24,2432]{1,0:T(8,128)(2,1)}, u32[]{:S(2)}, u32[]{:S(2)}) collective-permute-start(bf16[24,2432]{1,0:T(8,128)(2,1)} %get-tuple-element.94), channel_id=1, source_target_pairs={{0,1},{1,0},{2,3},{3,2},{4,5},{5,4},{6,7},{7,6},{8,9},{9,8},{10,11... | collective-permute-start | bytes 350216 | tf_op jit(solution)/shard_map/ppermute | solution.py:643
  373.9 1.2 collective-permute-start.19
  375.1 0.3 collective-permute-start.18
  375.4 0.6 slice.192
  376.0 0.7 copy.98
  376.7 1.1 reshape.234
  377.9 1.2 copy.88
  379.1 2.6 reshape.235
  381.7 0.5 collective-permute-done.19
  382.2 3.7 collective-permute-done.18
  385.9 1.1 fusion.11
  387.1 0.8 slice_reduce_fusion.3
  387.9 0.7 fusion.18
  394.0 0.6 reshape.236
  394.7 0.6 slice_reduce_fusion
  395.4 0.6 copy.96
  396.0 0.6 copy.95
  396.7 0.6 copy.94
  397.3 0.6 pad_maximum_fusion.4
  (116 shorter events, 3.2 us)
Async XLA Ops:
  7.2 4.8 %copy-start.12 = (bf16[24,768]{1,0:T(8,128)(2,1)S(1)}, bf16[24,768]{1,0:T(8,128)(2,1)}, u32[]{:S(2)}) copy-start(bf16[24,768]{1,0:T(8,128)(2,1)} %param.28) | copy-start | bytes 110596
  7.2 5.6 %copy-start.22 = (bf16[96]{0:T(256)(128)(2,1)S(1)}, bf16[96]{0:T(256)(128)(2,1)}, u32[]{:S(2)}) copy-start(bf16[96]{0:T(256)(128)(2,1)} %param.33) | copy-start | bytes 580
  7.2 5.8 %copy-start.14 = (bf16[24]{0:T(256)(128)(2,1)S(1)}, bf16[24]{0:T(256)(128)(2,1)}, u32[]{:S(2)}) copy-start(bf16[24]{0:T(256)(128)(2,1)} %param.24) | copy-start | bytes 148
  7.2 5.9 %copy-start.15 = (bf16[24]{0:T(256)(128)(2,1)S(1)}, bf16[24]{0:T(256)(128)(2,1)}, u32[]{:S(2)}) copy-start(bf16[24]{0:T(256)(128)(2,1)} %param.27) | copy-start | bytes 148
  7.2 6.0 %copy-start.16 = (bf16[24]{0:T(256)(128)(2,1)S(1)}, bf16[24]{0:T(256)(128)(2,1)}, u32[]{:S(2)}) copy-start(bf16[24]{0:T(256)(128)(2,1)} %param.29) | copy-start | bytes 148
  7.2 6.1 %copy-start.17 = (bf16[24]{0:T(256)(128)(2,1)S(1)}, bf16[24]{0:T(256)(128)(2,1)}, u32[]{:S(2)}) copy-start(bf16[24]{0:T(256)(128)(2,1)} %param.30) | copy-start | bytes 148
  7.3 6.2 %copy-start.18 = (bf16[24]{0:T(256)(128)(2,1)S(1)}, bf16[24]{0:T(256)(128)(2,1)}, u32[]{:S(2)}) copy-start(bf16[24]{0:T(256)(128)(2,1)} %param.31) | copy-start | bytes 148
  7.3 6.3 %copy-start.19 = (bf16[24]{0:T(256)(128)(2,1)S(1)}, bf16[24]{0:T(256)(128)(2,1)}, u32[]{:S(2)}) copy-start(bf16[24]{0:T(256)(128)(2,1)} %param.35) | copy-start | bytes 148
  7.3 6.4 %copy-start.20 = (bf16[24]{0:T(256)(128)(2,1)S(1)}, bf16[24]{0:T(256)(128)(2,1)}, u32[]{:S(2)}) copy-start(bf16[24]{0:T(256)(128)(2,1)} %param.36) | copy-start | bytes 148
  7.3 6.4 %copy-start.21 = (bf16[24]{0:T(256)(128)(2,1)S(1)}, bf16[24]{0:T(256)(128)(2,1)}, u32[]{:S(2)}) copy-start(bf16[24]{0:T(256)(128)(2,1)} %param.37) | copy-start | bytes 148
  7.3 6.7 %copy-start.9 = (bf16[24,768]{1,0:T(8,128)(2,1)S(1)}, bf16[24,768]{1,0:T(8,128)(2,1)}, u32[]{:S(2)}) copy-start(bf16[24,768]{1,0:T(8,128)(2,1)} %param.23) | copy-start | bytes 110596
  7.3 6.7 %copy-start.10 = (bf16[24,768]{1,0:T(8,128)(2,1)S(1)}, bf16[24,768]{1,0:T(8,128)(2,1)}, u32[]{:S(2)}) copy-start(bf16[24,768]{1,0:T(8,128)(2,1)} %param.25) | copy-start | bytes 110596
  7.3 6.7 %copy-start.11 = (bf16[24,768]{1,0:T(8,128)(2,1)S(1)}, bf16[24,768]{1,0:T(8,128)(2,1)}, u32[]{:S(2)}) copy-start(bf16[24,768]{1,0:T(8,128)(2,1)} %param.26) | copy-start | bytes 110596
  7.3 12.5 %copy-start.13 = (s32[2,8]{1,0:T(2,128)S(1)}, s32[2,8]{1,0:T(2,128)}, u32[]{:S(2)}) copy-start(s32[2,8]{1,0:T(2,128)} %param.21) | copy-start | bytes 196
  7.3 12.7 %copy-start.2 = (s32[2]{0:T(128)S(1)}, s32[2]{0:T(128)}, u32[]{:S(2)}) copy-start(s32[2]{0:T(128)} %pad_ref.3) | copy-start | bytes 28
  7.3 103.5 %all-gather.2.cloned.1.call-start = ((), (), s32[]{:S(2)}) async-start(), calls=%async_computation.2 | async-start | bytes 10948608 | tf_op jit(solution)/shard_map/all_gather | solution.py:639
  12.8 282.0 %reduce-scatter.5.cloned.1.call-start = ((), (), s32[]{:S(2)}) async-start(), calls=%async_computation.4 | async-start | bytes 5308416 | tf_op jit(solution)/shard_map/reduce_scatter | solution.py:695
  14.1 9.2 %collective-permute-start.2 = (bf16[24,2432]{1,0:T(8,128)(2,1)S(1)}, bf16[24,2432]{1,0:T(8,128)(2,1)S(1)}, u32[]{:S(2)}, u32[]{:S(2)}) collective-permute-start(bf16[24,2432]{1,0:T(8,128)(2,1)S(1)} %constant_dynamic-update-slice_fusion), channel_id=1, source_target_pairs={{0,3},{1,2},{2,1},{3,0},{4,7},{5,6},{6,5},{7,4},{8,11},{9,10},{10,... | collective-permute-start | bytes 350216 | tf_op jit(solution)/shard_map/ppermute | solution.py:643
  19.2 12.4 %collective-permute-start.1 = (bf16[24,2432]{1,0:T(8,128)(2,1)S(1)}, bf16[24,2432]{1,0:T(8,128)(2,1)S(1)}, u32[]{:S(2)}, u32[]{:S(2)}) collective-permute-start(bf16[24,2432]{1,0:T(8,128)(2,1)S(1)} %constant_dynamic-update-slice_fusion), channel_id=1, source_target_pairs={{0,2},{1,3},{2,0},{3,1},{4,6},{5,7},{6,4},{7,5},{8,10},{9,11},{10,... | collective-permute-start | bytes 350216 | tf_op jit(solution)/shard_map/ppermute | solution.py:643
  19.2 12.4 %collective-permute-start = (bf16[24,2432]{1,0:T(8,128)(2,1)S(1)}, bf16[24,2432]{1,0:T(8,128)(2,1)S(1)}, u32[]{:S(2)}, u32[]{:S(2)}) collective-permute-start(bf16[24,2432]{1,0:T(8,128)(2,1)S(1)} %constant_dynamic-update-slice_fusion), channel_id=1, source_target_pairs={{0,1},{1,0},{2,3},{3,2},{4,5},{5,4},{6,7},{7,6},{8,9},{9,8},{10,11... | collective-permute-start | bytes 350216 | tf_op jit(solution)/shard_map/ppermute | solution.py:643
  31.7 14.6 %collective-permute-start.8 = (bf16[4,24,2432]{2,1,0:T(8,128)(2,1)S(1)}, bf16[4,24,2432]{2,1,0:T(8,128)(2,1)S(1)}, u32[]{:S(2)}, u32[]{:S(2)}) collective-permute-start(bf16[4,24,2432]{2,1,0:T(8,128)(2,1)S(1)} %pad_maximum_fusion.1.refs_0_), channel_id=1, source_target_pairs={{0,24},{4,28},{8,16},{12,20},{16,8},{20,12},{24,0},{28,4},{1,25},{... | collective-permute-start | bytes 1400840 | tf_op jit(solution)/shard_map/ppermute | solution.py:643
  34.4 20.3 %collective-permute-start.6 = (bf16[4,24,2432]{2,1,0:T(8,128)(2,1)S(1)}, bf16[4,24,2432]{2,1,0:T(8,128)(2,1)S(1)}, u32[]{:S(2)}, u32[]{:S(2)}) collective-permute-start(bf16[4,24,2432]{2,1,0:T(8,128)(2,1)S(1)} %pad_maximum_fusion.1.refs_0_), channel_id=1, source_target_pairs={{0,16},{4,20},{8,24},{12,28},{16,0},{20,4},{24,8},{28,12},{1,17},{... | collective-permute-start | bytes 1400840 | tf_op jit(solution)/shard_map/ppermute | solution.py:643
  34.7 23.9 %collective-permute-start.4 = (bf16[4,24,2432]{2,1,0:T(8,128)(2,1)S(1)}, bf16[4,24,2432]{2,1,0:T(8,128)(2,1)S(1)}, u32[]{:S(2)}, u32[]{:S(2)}) collective-permute-start(bf16[4,24,2432]{2,1,0:T(8,128)(2,1)S(1)} %pad_maximum_fusion.1.refs_0_), channel_id=1, source_target_pairs={{0,8},{4,12},{8,0},{12,4},{16,24},{20,28},{24,16},{28,20},{1,9},{5... | collective-permute-start | bytes 1400840 | tf_op jit(solution)/shard_map/ppermute | solution.py:643
  35.8 23.1 %collective-permute-start.3 = (bf16[4,24,2432]{2,1,0:T(8,128)(2,1)S(1)}, bf16[4,24,2432]{2,1,0:T(8,128)(2,1)S(1)}, u32[]{:S(2)}, u32[]{:S(2)}) collective-permute-start(bf16[4,24,2432]{2,1,0:T(8,128)(2,1)S(1)} %pad_maximum_fusion.1.refs_0_), channel_id=1, source_target_pairs={{0,4},{4,0},{8,12},{12,8},{16,20},{20,16},{24,28},{28,24},{1,5},{5... | collective-permute-start | bytes 1400840 | tf_op jit(solution)/shard_map/ppermute | solution.py:643
  46.3 12.6 %collective-permute-start.9 = (bf16[4,24,2432]{2,1,0:T(8,128)(2,1)S(1)}, bf16[4,24,2432]{2,1,0:T(8,128)(2,1)S(1)}, u32[]{:S(2)}, u32[]{:S(2)}) collective-permute-start(bf16[4,24,2432]{2,1,0:T(8,128)(2,1)S(1)} %collective-permute-done.8.refs_6_), channel_id=1, source_target_pairs={{0,4},{4,0},{8,12},{12,8},{16,20},{20,16},{24,28},{28,24},{1,5},{5... | collective-permute-start | bytes 1400840 | tf_op jit(solution)/shard_map/ppermute | solution.py:643
  54.7 4.2 %collective-permute-start.7 = (bf16[4,24,2432]{2,1,0:T(8,128)(2,1)S(1)}, bf16[4,24,2432]{2,1,0:T(8,128)(2,1)S(1)}, u32[]{:S(2)}, u32[]{:S(2)}) collective-permute-start(bf16[4,24,2432]{2,1,0:T(8,128)(2,1)S(1)} %collective-permute-done.6.refs_4_), channel_id=1, source_target_pairs={{0,4},{4,0},{8,12},{12,8},{16,20},{20,16},{24,28},{28,24},{1,5},{5... | collective-permute-start | bytes 1400840 | tf_op jit(solution)/shard_map/ppermute | solution.py:643
  58.6 1.8 collective-permute-start.5
  107.3 1.6 copy-start.4
  176.6 126.4 %reduce-scatter.3.cloned.1.call-start = ((), (), s32[]{:S(2)}) async-start(), calls=%async_computation.3 | async-start | bytes 6635520 | tf_op jit(solution)/shard_map/reduce_scatter | solution.py:695
  230.5 0.7 copy-start.3
  230.5 0.8 copy-start.5
  230.5 0.8 copy-start.6
  293.5 1.2 copy-start
  303.0 15.0 %copy-start.1 = (bf16[4,96,2432]{2,1,0:T(8,128)(2,1)S(1)}, bf16[4,96,2432]{2,1,0:T(8,128)(2,1)}, u32[]{:S(2)}) copy-start(bf16[4,96,2432]{2,1,0:T(8,128)(2,1)} %copy-done) | copy-start | bytes 5603332
  304.6 39.9 %copy-start.7 = (bf16[32,24,2432]{2,1,0:T(8,128)(2,1)S(1)}, bf16[32,24,2432]{2,1,0:T(8,128)(2,1)}, u32[]{:S(2)}) copy-start(bf16[32,24,2432]{2,1,0:T(8,128)(2,1)} %place.1) | copy-start | bytes 11206660
  304.7 13.4 %collective-permute-start.10 = (bf16[24,6912]{1,0:T(8,128)(2,1)S(1)}, bf16[24,6912]{1,0:T(8,128)(2,1)S(1)}, u32[]{:S(2)}, u32[]{:S(2)}) collective-permute-start(bf16[24,6912]{1,0:T(8,128)(2,1)S(1)} %get-tuple-element.62), channel_id=1, source_target_pairs={{0,1},{1,0},{2,3},{3,2},{4,5},{5,4},{6,7},{7,6},{8,9},{9,8},{10,11... | collective-permute-start | bytes 995336 | tf_op jit(solution)/shard_map/ppermute | solution.py:643
  306.2 34.3 %collective-permute-start.11 = (bf16[24,6912]{1,0:T(8,128)(2,1)S(1)}, bf16[24,6912]{1,0:T(8,128)(2,1)S(1)}, u32[]{:S(2)}, u32[]{:S(2)}) collective-permute-start(bf16[24,6912]{1,0:T(8,128)(2,1)S(1)} %get-tuple-element.63), channel_id=1, source_target_pairs={{0,2},{1,3},{2,0},{3,1},{4,6},{5,7},{6,4},{7,5},{8,10},{9,11},{10,... | collective-permute-start | bytes 995336 | tf_op jit(solution)/shard_map/ppermute | solution.py:643
  318.0 22.4 %collective-permute-start.12 = (bf16[24,6912]{1,0:T(8,128)(2,1)S(1)}, bf16[24,6912]{1,0:T(8,128)(2,1)S(1)}, u32[]{:S(2)}, u32[]{:S(2)}) collective-permute-start(bf16[24,6912]{1,0:T(8,128)(2,1)S(1)} %get-tuple-element.64), channel_id=1, source_target_pairs={{0,3},{1,2},{2,1},{3,0},{4,7},{5,6},{6,5},{7,4},{8,11},{9,10},{10,... | collective-permute-start | bytes 995336 | tf_op jit(solution)/shard_map/ppermute | solution.py:643
  318.1 22.6 %collective-permute-start.13 = (bf16[4,96,2432]{2,1,0:T(8,128)(2,1)S(1)}, bf16[4,96,2432]{2,1,0:T(8,128)(2,1)S(1)}, u32[]{:S(2)}, u32[]{:S(2)}) collective-permute-start(bf16[4,96,2432]{2,1,0:T(8,128)(2,1)S(1)} %copy-done.1), channel_id=1, source_target_pairs={{0,4},{4,0},{8,12},{12,8},{16,20},{20,16},{24,28},{28,24},{1,5},{5... | collective-permute-start | bytes 5603336 | tf_op jit(solution)/shard_map/ppermute | solution.py:643
  341.0 16.5 %collective-permute-start.14 = (bf16[96,2432]{1,0:T(8,128)(2,1)S(1)}, bf16[96,2432]{1,0:T(8,128)(2,1)S(1)}, u32[]{:S(2)}, u32[]{:S(2)}) collective-permute-start(bf16[96,2432]{1,0:T(8,128)(2,1)S(1)} %get-tuple-element.85), channel_id=1, source_target_pairs={{0,8},{4,12},{8,0},{12,4},{16,24},{20,28},{24,16},{28,20},{1,9},{5... | collective-permute-start | bytes 1400840 | tf_op jit(solution)/shard_map/ppermute | solution.py:643
  341.3 19.1 %collective-permute-start.16 = (bf16[96,2432]{1,0:T(8,128)(2,1)S(1)}, bf16[96,2432]{1,0:T(8,128)(2,1)S(1)}, u32[]{:S(2)}, u32[]{:S(2)}) collective-permute-start(bf16[96,2432]{1,0:T(8,128)(2,1)S(1)} %get-tuple-element.86), channel_id=1, source_target_pairs={{0,24},{4,28},{8,16},{12,20},{16,8},{20,12},{24,0},{28,4},{1,25},{... | collective-permute-start | bytes 1400840 | tf_op jit(solution)/shard_map/ppermute | solution.py:643
  342.0 23.7 %collective-permute-start.15 = (bf16[96,2432]{1,0:T(8,128)(2,1)S(1)}, bf16[96,2432]{1,0:T(8,128)(2,1)S(1)}, u32[]{:S(2)}, u32[]{:S(2)}) collective-permute-start(bf16[96,2432]{1,0:T(8,128)(2,1)S(1)} %get-tuple-element.87), channel_id=1, source_target_pairs={{0,16},{4,20},{8,24},{12,28},{16,0},{20,4},{24,8},{28,12},{1,17},{... | collective-permute-start | bytes 1400840 | tf_op jit(solution)/shard_map/ppermute | solution.py:643
  366.0 10.7 %copy-start.8 = (bf16[96,2432]{1,0:T(8,128)(2,1)}, bf16[96,2432]{1,0:T(8,128)(2,1)S(1)}, u32[]{:S(2)}) copy-start(bf16[96,2432]{1,0:T(8,128)(2,1)S(1)} %fusion.6) | copy-start | bytes 1400836
  366.8 14.9 %collective-permute-start.17 = (bf16[24,2432]{1,0:T(8,128)(2,1)}, bf16[24,2432]{1,0:T(8,128)(2,1)}, u32[]{:S(2)}, u32[]{:S(2)}) collective-permute-start(bf16[24,2432]{1,0:T(8,128)(2,1)} %get-tuple-element.94), channel_id=1, source_target_pairs={{0,1},{1,0},{2,3},{3,2},{4,5},{5,4},{6,7},{7,6},{8,9},{9,8},{10,11... | collective-permute-start | bytes 350216 | tf_op jit(solution)/shard_map/ppermute | solution.py:643
  373.9 8.3 %collective-permute-start.19 = (bf16[24,2432]{1,0:T(8,128)(2,1)}, bf16[24,2432]{1,0:T(8,128)(2,1)}, u32[]{:S(2)}, u32[]{:S(2)}) collective-permute-start(bf16[24,2432]{1,0:T(8,128)(2,1)} %get-tuple-element.95), channel_id=1, source_target_pairs={{0,3},{1,2},{2,1},{3,0},{4,7},{5,6},{6,5},{7,4},{8,11},{9,10},{10,... | collective-permute-start | bytes 350216 | tf_op jit(solution)/shard_map/ppermute | solution.py:643
  375.1 10.9 %collective-permute-start.18 = (bf16[24,2432]{1,0:T(8,128)(2,1)}, bf16[24,2432]{1,0:T(8,128)(2,1)}, u32[]{:S(2)}, u32[]{:S(2)}) collective-permute-start(bf16[24,2432]{1,0:T(8,128)(2,1)} %get-tuple-element.96), channel_id=1, source_target_pairs={{0,2},{1,3},{2,0},{3,1},{4,6},{5,7},{6,4},{7,5},{8,10},{9,11},{10,... | collective-permute-start | bytes 350216 | tf_op jit(solution)/shard_map/ppermute | solution.py:643
Sparse Core Ops, SparseCore 0:
  12.9 97.9 all-gather.1
  176.7 62.6 reduce-scatter.4
  243.3 59.6 reduce-scatter.2

commit v4 on v3

--- a/solution.py
+++ b/solution.py
@@ -20,6 +20,7 @@
 
 GROUP = 256
 HEADS_IN = GROUP // HEAD_DIM
+PAIR = 128
 TRIPLE = 3 * GROUP
 QB = 256
 CHUNK = 256
@@ -33,9 +34,9 @@
     )
 
 
-def head_masks():
-    lane = lax.broadcasted_iota(jnp.int32, (1, GROUP), 1) // HEAD_DIM
-    return [lane == h for h in range(HEADS_IN)]
+def head_masks(columns):
+    lane = lax.broadcasted_iota(jnp.int32, (1, columns), 1) // HEAD_DIM
+    return [lane == h for h in range(columns // HEAD_DIM)]
 
 
 def cost(flops, moved):
@@ -67,7 +68,7 @@
     s = pl.program_id(0)
     qkv_ref[...] = (dot(rows_ref[...], w_ref[...]) + bias_ref[0:1, :]).astype(BF16)
     keyt_ref[...] = qkv_ref[:, GROUP : 2 * GROUP].T
-    masks = head_masks()
+    masks = head_masks(GROUP)
 
     def block(i, carry):
         start = pl.multiple_of(i * QB, QB)
@@ -146,7 +147,7 @@
     q_ref, qt_ref, gt_ref, kt_ref, dqt_ref, acc_ref, delta_ref, sums_ref, stage_ref, columns_ref, rowst_ref, sem,
 ):
     s, g = pl.program_id(0), pl.program_id(1)
-    masks = head_masks()
+    masks = head_masks(PAIR)
 
     @pl.when(g == 0)
     def _():
@@ -176,7 +177,7 @@
         mine = pl.ds(start, QB)
         keys = qkv_ref[mine, GROUP : 2 * GROUP]
         values = qkv_ref[mine, 2 * GROUP :]
-        zero = jnp.zeros_like(keys)
+        zero = jnp.zeros((QB, PAIR), BF16)
         own = segc_ref[mine, :][:, :1]
         low = pl.multiple_of(low_ref[s, i], 128)
         count = count_ref[s, i]
@@ -186,22 +187,23 @@
             def _():
                 span = pl.ds(low, CHUNK * c)
                 allowed = own == segr_ref[0:1, span]
-                dkey = dvalue = None
                 for h in range(HEADS_IN):
-                    scores = dot(jnp.where(masks[h], keys, zero), qt_ref[:, span])
+                    mask, lanes = masks[h % 2], slice(h // 2 * PAIR, (h // 2 + 1) * PAIR)
+                    scores = dot(jnp.where(mask, keys[:, lanes], zero), qt_ref[lanes, span])
                     probs = jnp.exp(jnp.where(allowed, scores, NEGATIVE) - lse_ref[h : h + 1, span])
-                    pgrad = dot(jnp.where(masks[h], values, zero), gt_ref[:, span])
+                    pgrad = dot(jnp.where(mask, values[:, lanes], zero), gt_ref[lanes, span])
                     low_score = (probs * (pgrad - delta_ref[h : h + 1, span])).astype(BF16)
-                    v_part = dot(probs.astype(BF16), grad_ref[span, :])
-                    k_part = dot(low_score, q_ref[span, :])
+                    v_part = dot(probs.astype(BF16), grad_ref[span, lanes])
+                    k_part = dot(low_score, q_ref[span, lanes])
                     head = slice(h * HEAD_DIM, (h + 1) * HEAD_DIM)
                     dqt_ref[head, span] += dot(kt_ref[head, mine], low_score)
-                    if h == 0:
+                    if h % 2 == 0:
                         dkey, dvalue = k_part, v_part
                     else:
-                        dkey, dvalue = jnp.where(masks[h], k_part, dkey), jnp.where(masks[h], v_part, dvalue)
-                dqkv_ref[mine, GROUP : 2 * GROUP] = dkey.astype(BF16)
-                dqkv_ref[mine, 2 * GROUP :] = dvalue.astype(BF16)
+                        first = h // 2 * PAIR
+                        dkey, dvalue = jnp.where(mask, k_part, dkey), jnp.where(mask, v_part, dvalue)
+                        dqkv_ref[mine, GROUP + first : GROUP + first + PAIR] = dkey.astype(BF16)
+                        dqkv_ref[mine, 2 * GROUP + first : 2 * GROUP + first + PAIR] = dvalue.astype(BF16)
 
         return carry
 
@@ -362,30 +364,33 @@
             self.copy(k).wait()
 
 
-def send_block(acc_ref, stage_ref, dw_ref, sem, k, first, last_step, turned):
+def out_copy(stage_ref, dw_ref, sem, k):
     width = stage_ref.shape[1]
-
-    def copy(k):
-        columns = pl.ds(pl.multiple_of(k * width, width), width)
-        slot = lax.rem(k, 2)
-        return pltpu.make_async_copy(stage_ref.at[slot], dw_ref.at[:, columns], sem.at[slot])
-
-    @pl.when(last_step)
-    def _():
-        @pl.when(k >= first + 2)
+    columns = pl.ds(pl.multiple_of(k * width, width), width)
+    slot = lax.rem(k, 2)
+    return pltpu.make_async_copy(stage_ref.at[slot], dw_ref.at[:, columns], sem.at[slot])
+
+
+def send_blocks(gradient, first, amount, stage_ref, dw_ref, sem):
+    def step(j, carry):
+        k = first + j
+
+        @pl.when(j >= 2)
         def _():
-            copy(k - 2).wait()
-
-        value = acc_ref[k].astype(BF16)
-        stage_ref[lax.rem(k, 2)] = value.T if turned else value
-        copy(k).start()
+            out_copy(stage_ref, dw_ref, sem, k - 2).wait()
+
+        stage_ref[lax.rem(k, 2)] = gradient(j)
+        out_copy(stage_ref, dw_ref, sem, k).start()
+        return carry
+
+    lax.fori_loop(0, amount, step, 0)
 
 
 def upper_kernel(
     parts, width, tokens,
     pad_ref, mixed_ref, rows_ref, cot_ref, w_ref, vec_ref,
     out_ref, normed_ref, inverse_ref, upper_ref, slope_ref, dw_ref, sums_ref, stats_ref,
-    held_ref, hidden_ref, low_ref, wide_ref, acc_ref, stage_ref, part_ref, w_sem, sem,
+    held_ref, hidden_ref, low_ref, uppert_ref, stage_ref, part_ref, w_sem, sem,
 ):
     i = pl.program_id(0)
     last = i == pl.num_programs(0) - 1
@@ -395,7 +400,6 @@
 
     @pl.when(i == 0)
     def _():
-        acc_ref[...] = jnp.zeros_like(acc_ref)
         part_ref[...] = jnp.zeros_like(part_ref)
 
     def vector(row):
@@ -405,12 +409,13 @@
         place = (i % per_seq) * tokens + lax.broadcasted_iota(jnp.int32, (tokens, 1), 0)
         return (place < LEN - pad_ref[i // per_seq]).astype(F32)
 
+    mine = pl.ds(pl.multiple_of(i * tokens, tokens), tokens)
     weights.wait(0)
-    wide_ref[...] = dot(mixed_ref[...], held_ref[0])
+    upper_ref[...] = dot(mixed_ref[...], held_ref[0])
 
     valid = valid_of()
     rows = rows_ref[...].astype(F32)
-    branch = wide_ref[...] + vector(0)
+    branch = upper_ref[...] + vector(0)
     add_rows(part_ref, 3, valid * rows * rows)
     add_rows(part_ref, 4, valid * branch * branch)
     normed, inverse = normed_of(rows + branch)
@@ -418,7 +423,7 @@
     inverse_ref[...] = jnp.broadcast_to(inverse, (tokens, 128))
     first = normed * vector(1) + vector(2)
     low_ref[...] = first.astype(BF16)
-    wide_ref[...] = first + vector(3)
+    upper_ref[...] = first + vector(3)
 
     def feed(j, carry):
         weights.wait(1 + j)
@@ -426,16 +431,16 @@
         inner = dot(low_ref[...], held_ref[1 + j]) + vec_ref[pl.ds(6 + j, 1), :]
         half = 0.5 * (1.0 + lax.erf(inner * ROOT_HALF))
         hidden = (inner * half).astype(BF16)
-        hidden_ref[j] = hidden
+        hidden_ref[j, mine, :] = hidden
         slope = half + inner * jnp.exp(-0.5 * inner * inner) * INV_ROOT_TWO_PI
         slope_ref[:, pl.ds(pl.multiple_of(j * width, width), width)] = slope.astype(BF16)
-        wide_ref[...] += dot(hidden, held_ref[1 + parts + j])
+        upper_ref[...] += dot(hidden, held_ref[1 + parts + j])
         return carry
 
     lax.fori_loop(0, parts, feed, 0)
 
     valid = valid_of()
-    total = wide_ref[...]
+    total = upper_ref[...]
     second = total - (normed_ref[...] * vector(1) + vector(2))
     add_rows(part_ref, 5, valid * second * second)
     normed, inverse = normed_of(total)
@@ -449,16 +454,7 @@
     upper_ref[...] = upper
     upper_low = upper.astype(BF16)
     add_rows(part_ref, 2, upper_low.astype(F32))
-    low_ref[...] = upper_low
-
-    upper_t = low_ref[...].T
-
-    def back(j, carry):
-        acc_ref[j] += dot(upper_t, hidden_ref[j])
-        send_block(acc_ref, stage_ref, dw_ref, sem, j, 0, last, True)
-        return carry
-
-    lax.fori_loop(0, parts, back, 0)
+    uppert_ref[:, mine] = upper_low.T
 
     @pl.when(last)
     def _():
@@ -468,6 +464,9 @@
         for row in range(4):
             stats_ref[row : row + 1, :] = jnp.sum(part_ref[3 + row], axis=0, keepdims=True)
         stats_ref[4:, :] = jnp.zeros_like(stats_ref[4:, :])
+        send_blocks(
+            lambda j: dot(uppert_ref[...], hidden_ref[j]).astype(BF16).T, 0, parts, stage_ref, dw_ref, sem
+        )
         for k in (parts - 2, parts - 1):
             out_copy(stage_ref, dw_ref, sem, k).wait()
 
@@ -476,7 +475,7 @@
     parts, width, tokens,
     mixed_ref, normed_ref, inverse_ref, upper_ref, slope_ref, w_ref, vec_ref, sums_in_ref,
     res_ref, mgrad_ref, dw_ref, sums_ref,
-    held_ref, low_ref, first_ref, wide_ref, acc_ref, stage_ref, part_ref, w_sem, sem,
+    held_ref, low_ref, first_ref, acc_ref, stage_ref, part_ref, w_sem, sem,
 ):
     i = pl.program_id(0)
     last = i == pl.num_programs(0) - 1
@@ -492,7 +491,7 @@
         return vec_ref[row : row + 1, :]
 
     upper = upper_ref[...]
-    wide_ref[...] = upper
+    res_ref[...] = upper
     low_ref[...] = upper.astype(BF16)
     first_ref[...] = (normed_ref[...] * vector(1) + vector(2)).astype(BF16)
 
@@ -505,13 +504,22 @@
         inner_low = (dot(low_ref[...], held_ref[1 + parts + j], 1, 1) * slope).astype(BF16)
         add_rows(part_ref, 3 + j, inner_low.astype(F32))
         acc_ref[1 + j] += dot(first_t, inner_low)
-        wide_ref[...] += dot(inner_low, held_ref[1 + j], 1, 1)
-        send_block(acc_ref, stage_ref, dw_ref, sem, 1 + j, 1, last, False)
+        res_ref[...] += dot(inner_low, held_ref[1 + j], 1, 1)
+
+        @pl.when(last)
+        def _():
+            @pl.when(j >= 2)
+            def _():
+                out_copy(stage_ref, dw_ref, sem, j - 1).wait()
+
+            stage_ref[lax.rem(1 + j, 2)] = acc_ref[1 + j].astype(BF16)
+            out_copy(stage_ref, dw_ref, sem, 1 + j).start()
+
         return carry
 
     lax.fori_loop(0, parts, back, 0)
 
-    first_grad = wide_ref[...]
+    first_grad = res_ref[...]
     normed = normed_ref[...]
     add_rows(part_ref, 0, first_grad * normed)
     add_rows(part_ref, 1, first_grad)
@@ -537,11 +545,6 @@
         stage_ref[0] = acc_ref[0].astype(BF16)
         out_copy(stage_ref, dw_ref, sem, 0).start()
         out_copy(stage_ref, dw_ref, sem, 0).wait()
-
-
-def out_copy(stage_ref, dw_ref, sem, k):
-    width = stage_ref.shape[1]
-    return pltpu.make_async_copy(stage_ref.at[k % 2], dw_ref.at[:, k * width : (k + 1) * width], sem.at[k % 2])
 
 
 def upper_half(mixed, rows, cotangent, w, vec, pad, tokens=512):
@@ -567,10 +570,9 @@
             ],
             scratch_shapes=[
                 pltpu.VMEM((1 + 2 * parts, width, width), BF16),
-                pltpu.VMEM((parts, tokens, width), BF16),
+                pltpu.VMEM((parts, count, width), BF16),
                 pltpu.VMEM((tokens, width), BF16),
-                pltpu.VMEM((tokens, width), F32),
-                pltpu.VMEM((parts, width, width), F32),
+                pltpu.VMEM((width, count), BF16),
                 pltpu.VMEM((2, width, width), BF16),
                 pltpu.VMEM((8, 8, width), F32),
                 pltpu.SemaphoreType.DMA((1 + 2 * parts,)),
@@ -616,7 +618,6 @@
             pltpu.VMEM((1 + 2 * parts, width, width), BF16),
             pltpu.VMEM((tokens, width), BF16),
             pltpu.VMEM((tokens, width), BF16),
-            pltpu.VMEM((tokens, width), F32),
             pltpu.VMEM((1 + parts, width, width), F32),
             pltpu.VMEM((2, width, width), BF16),
             pltpu.VMEM((3 + parts, 8, width), F32),
@@ -670,7 +671,7 @@
             out_specs=pl.BlockSpec((planes * columns, rows, width), lambda i, *_: (0, 0, 0)),
         ),
         out_shape=jax.ShapeDtypeStruct((planes * columns, rows, width), shard.dtype),
-        compiler_params=pltpu.CompilerParams(vmem_limit_bytes=48 * 2**20),
+        compiler_params=pltpu.CompilerParams(vmem_limit_bytes=24 * 2**20),
         name="place",
     )(where, *sources)
     return whole.reshape(planes * columns * rows, width)
@@ -699,10 +700,13 @@
     return lax.psum_scatter(partial, "fsdp", scatter_dimension=0, tiled=True)
 
 
-def join_planes(keep, send):
+def join_cores(keep, send):
     other = swap(send, "dp", 1)
-    parts = [tree_sum([keep[m], other[m]]).astype(keep.dtype) for m in range(keep.shape[0])]
-    return tree_sum(parts[:1] + [swap(parts[m], "dp", 2 * m) for m in range(1, len(parts))]).astype(keep.dtype)
+    return [tree_sum([keep[m], other[m]]).astype(keep.dtype) for m in range(keep.shape[0])]
+
+
+def join_chips(parts):
+    return tree_sum(parts[:1] + [swap(part, "dp", 2 * m) for m, part in enumerate(parts) if m]).astype(parts[0].dtype)
 
 
 def blocks_for_columns(partial):
@@ -711,8 +715,142 @@
     return [pick(blocks, lax.axis_index("fsdp") ^ k) for k in range(columns)]
 
 
-def join_blocks(blocks):
-    return tree_sum(blocks[:1] + [swap(block, "fsdp", k) for k, block in enumerate(blocks) if k])
+def swap_blocks(blocks):
+    return blocks[:1] + [swap(block, "fsdp", k) for k, block in enumerate(blocks) if k]
+
+
+def small_call(kernel, shapes, name, room=6, **options):
+    params = pltpu.CompilerParams(vmem_limit_bytes=room * 2**20)
+    return pl.pallas_call(kernel, out_shape=shapes, compiler_params=params, name=name, **options)
+
+
+def fetching_call(kernel, shape, name, arrays, fetched, scratch=()):
+    held = [pltpu.VMEM(array.shape, array.dtype) for array in arrays[:fetched]]
+    return small_call(
+        kernel,
+        shape,
+        name,
+        room=60,
+        in_specs=[pl.BlockSpec(memory_space=pltpu.MemorySpace.HBM)] * len(arrays),
+        scratch_shapes=held + list(scratch) + [pltpu.SemaphoreType.DMA((fetched,))],
+    )(*arrays)
+
+
+def fetch(sources, targets, sem):
+    copies = [pltpu.make_async_copy(s, t, sem.at[k]) for k, (s, t) in enumerate(zip(sources, targets))]
+    for copy in copies:
+        copy.start()
+    return copies
+
+
+def pack_far_kernel(merge_hbm, inner_hbm, outer_hbm, after_ref, far_ref, merge_ref, inner_ref, outer_ref, sem):
+    for copy in fetch((merge_hbm, inner_hbm, outer_hbm), (merge_ref, inner_ref, outer_ref), sem):
+        copy.wait()
+    own, width = merge_ref.shape
+    parts = inner_ref.shape[1] // width
+    far_ref[:, :width] = merge_ref[...]
+    for j in range(parts):
+        for d in range(width // own):
+            first, source = (1 + j) * width + d * own, (d * parts + j) * own
+            far_ref[:, first : first + own] = inner_ref[:, source : source + own]
+        first = (1 + parts + j) * width
+        far_ref[:, first : first + width] = outer_ref[j * own : (j + 1) * own, :]
+
+
+def pack_near_kernel(vectors, *refs):
+    sources, near_ref, held = refs[: 3 + vectors], refs[3 + vectors], refs[4 + vectors : 7 + 2 * vectors]
+    rows_ref, sem = refs[-2:]
+    for copy in fetch(sources, held, sem):
+        copy.wait()
+    lines = held[3:]
+    own, width = held[0].shape
+    for g in range(width // GROUP):
+        for k, source in enumerate(held[:3]):
+            first = (3 * g + k) * GROUP
+            near_ref[:, first : first + GROUP] = source[:, g * GROUP : (g + 1) * GROUP]
+    rows_ref[...] = jnp.zeros_like(rows_ref)
+    row = 0
+    for line in lines:
+        values = line[...].astype(F32)
+        for j in range(line.shape[0] // own):
+            rows_ref[row : row + 1, :own] = values[j * own : (j + 1) * own].reshape(1, own)
+            row += 1
+    near_ref[:, 3 * width :] = rows_ref[...].T[:own].astype(BF16)
+
+
+def unpack_kernel(far_ref, merge_ref, inner_ref, outer_ref):
+    own, width = merge_ref.shape
+    parts = inner_ref.shape[1] // width
+    merge_ref[...] = far_ref[:, :width].astype(F32)
+    for j in range(parts):
+        block = far_ref[:, (1 + j) * width : (2 + j) * width].astype(F32)
+        for d in range(width // own):
+            target = (d * parts + j) * own
+            inner_ref[:, target : target + own] = block[:, d * own : (d + 1) * own]
+        outer_ref[j * own : (j + 1) * own, :] = far_ref[:, (1 + parts + j) * width : (2 + parts + j) * width].astype(F32)
+
+
+def finish_kernel(*refs):
+    blocks, (query_ref, key_ref, value_ref, vectors_ref) = refs[:-4], refs[-4:]
+    total = tree_sum([block[...] for block in blocks])
+    width = query_ref.shape[1]
+    for g in range(width // GROUP):
+        for k, target in enumerate((query_ref, key_ref, value_ref)):
+            first = (3 * g + k) * GROUP
+            target[:, g * GROUP : (g + 1) * GROUP] = total[:, first : first + GROUP]
+    vectors_ref[...] = total[:, 3 * width :].T
+
+
+def pack_near(query, key, value, vectors):
+    own, width = query.shape
+    if quick(own):
+        shape = jax.ShapeDtypeStruct((own, 3 * width + VEC), query.dtype)
+        kernel = functools.partial(pack_near_kernel, len(vectors))
+        arrays = (query, key, value, *vectors)
+        return fetching_call(kernel, shape, "pack_near", arrays, len(arrays), [pltpu.VMEM((VEC, VEC), F32)])
+    columns = jnp.concatenate([vector.reshape(-1, own) for vector in vectors]).T
+    columns = jnp.pad(columns, ((0, 0), (0, VEC - columns.shape[1])))
+    groups = range(0, width, GROUP)
+    triples = [mat[:, first : first + GROUP] for first in groups for mat in (query, key, value)]
+    return jnp.concatenate(triples + [columns], axis=1)
+
+
+def pack_far(merge, inner, outer, after):
+    own, width = merge.shape
+    parts = inner.shape[1] // width
+    if quick(own):
+        shape = jax.ShapeDtypeStruct((own, (1 + 2 * parts) * width), merge.dtype)
+        return fetching_call(pack_far_kernel, shape, "pack_far", (merge, inner, outer, after), 3)
+    inner = inner.reshape(own, width // own, parts, own).transpose(0, 2, 1, 3).reshape(own, parts * width)
+    outer = outer.reshape(parts, own, width).transpose(1, 0, 2).reshape(own, parts * width)
+    return jnp.concatenate([merge, inner, outer], axis=1)
+
+
+def unpack_far(far, parts):
+    own, width = far.shape[0], far.shape[1] // (1 + 2 * parts)
+    if quick(own):
+        shapes = [(own, width), (own, parts * width), (parts * own, width)]
+        shapes = [jax.ShapeDtypeStruct(shape, F32) for shape in shapes]
+        return small_call(unpack_kernel, shapes, "unpack_far")(far)
+    far = far.astype(F32)
+    inner = far[:, width : (1 + parts) * width].reshape(own, parts, width // own, own)
+    outer = far[:, (1 + parts) * width :].reshape(own, parts, width)
+    return (
+        far[:, :width],
+        inner.transpose(0, 2, 1, 3).reshape(own, parts * width),
+        outer.transpose(1, 0, 2).reshape(parts * own, width),
+    )
+
+
+def finish_near(blocks):
+    own = blocks[0].shape[0]
+    width = (blocks[0].shape[1] - VEC) // 3
+    if quick(own):
+        shapes = [jax.ShapeDtypeStruct(shape, F32) for shape in [(own, width)] * 3 + [(VEC, own)]]
+        return small_call(finish_kernel, shapes, "finish_near")(*blocks)
+    total = tree_sum(blocks)
+    triple = total[:, : 3 * width].reshape(own, width // GROUP, 3, GROUP)
+    return [triple[:, :, k].reshape(own, width) for k in range(3)] + [total[:, 3 * width :].T]
 
 
 def per_device(
@@ -727,21 +865,13 @@
     parts = inner_weight.shape[1] // width
     groups = width // GROUP
 
-    vectors = [query_bias, value_bias, merge_bias, first_gain, first_shift, outer_bias, second_gain, second_shift]
-    columns = jnp.concatenate([jnp.stack(vectors), inner_bias.reshape(parts, own)]).T
-    columns = jnp.pad(columns, ((0, 0), (0, VEC - columns.shape[1])))
-    triples = [
-        mat[:, g * GROUP : (g + 1) * GROUP]
-        for g in range(groups)
-        for mat in (query_weight, key_weight, value_weight)
-    ]
+    vectors = (query_bias, value_bias, merge_bias, first_gain, first_shift, outer_bias, second_gain, second_shift, inner_bias)
+    near_own = pack_near(query_weight, key_weight, value_weight, vectors)
+    near = quick_gather(near_own)
+    far = gather(pack_far(merge_weight, inner_weight, outer_weight, near_own))
     segment, low, count = segments(doc_lengths, pad_tail)
     segc = jnp.broadcast_to(segment[:, :, None], (seqs, LEN, 128))
     segr = jnp.broadcast_to(segment[:, None, :], (seqs, 8, LEN))
-    near = quick_gather(jnp.concatenate(triples + [columns], axis=1))
-    inner_own = inner_weight.reshape(own, devices, parts, own).transpose(0, 2, 1, 3).reshape(own, parts * width)
-    outer_own = outer_weight.reshape(parts, own, width).transpose(1, 0, 2).reshape(own, parts * width)
-    far = gather(jnp.concatenate([merge_weight, inner_own, outer_own], axis=1))
 
     vec_rows = near[:, 3 * width :].T.astype(F32)
     bias = jnp.stack([vec_rows[0], jnp.zeros((width,), F32), vec_rows[1]])
@@ -762,24 +892,25 @@
     dqkv, keep, send = attention_backward(
         qkv, mixed, mixed_grad.reshape(mixed.shape), layer_input, lse, segc, segr, sums, stats, low, count, pad_tail, chips
     )
+    far_planes = jnp.concatenate([inner_grad, outer_grad], axis=1)
     if chips:
-        far_blocks = blocks_for_columns(jnp.concatenate([inner_grad, outer_grad], axis=1))
-        keep, send, far_blocks = lax.optimization_barrier((keep, send, far_blocks))
-        far_grad = join_blocks(far_blocks)
-        near_grad = join_blocks(blocks_for_columns(join_planes(keep, send)))
+        keep, far_planes = lax.optimization_barrier((keep, far_planes))
+        far_grad = over_columns(far_planes)
+        parts_own = join_cores(keep, send)
+        parts_own, residual = lax.optimization_barrier((parts_own, residual))
+        near_planes = join_chips(parts_own)
     else:
-        far_grad = over_columns(jnp.concatenate([inner_grad, outer_grad], axis=1)).astype(F32)
-        near_grad = over_columns(over_planes(keep[0])).astype(F32)
-    residual, far_grad = lax.optimization_barrier((residual, far_grad))
+        far_grad = over_columns(far_planes)
+        near_planes = over_planes(keep[0])
     input_gradient = residual + dot(dqkv.reshape(tokens, 3 * width), near[:, : 3 * width], 1, 1)
-
-    mine = near_grad[:, 3 * width :].T
+    if chips:
+        near_planes, input_gradient, far_grad = lax.optimization_barrier((near_planes, input_gradient, far_grad))
+        near_blocks = swap_blocks(blocks_for_columns(near_planes))
+    else:
+        near_blocks = [over_columns(near_planes)]
+    query_grad, key_grad, value_grad, mine = finish_near(near_blocks)
+    merge_grad, inner_grad, outer_grad = unpack_far(far_grad, parts)
     inner_bias_gradient = mine[8 : 8 + parts].reshape(parts * own)
-    triple = near_grad[:, : 3 * width].reshape(own, groups, 3, GROUP)
-    query_grad, key_grad, value_grad = (triple[:, :, k].reshape(own, width) for k in range(3))
-    inner_grad = far_grad[:, width : (1 + parts) * width]
-    inner_grad = inner_grad.reshape(own, parts, devices, own).transpose(0, 2, 1, 3).reshape(own, parts * width)
-    outer_grad = far_grad[:, (1 + parts) * width :].reshape(own, parts, width).transpose(1, 0, 2)
     all_tokens = tokens * devices
     if quick(own):
         totals = mine[16 : 20 + DIGITS, 0]
@@ -798,13 +929,13 @@
         key_grad,
         value_grad,
         mine[7],
-        far_grad[:, :width],
+        merge_grad,
         mine[5],
         mine[3],
         mine[4],
         inner_grad,
         inner_bias_gradient,
-        outer_grad.reshape(parts * own, width),
+        outer_grad,
         mine[2],
         mine[0],
         mine[1],

time: 411 us -> 361 us (0.88); the launches traced: 405 us -> 361 us
  waiting for transfers between devices: 80.8 us -> 46.2 us
  Pallas kernels: 226 us -> 244 us
  local copies, waits for them, and re-layouts: 23.9 us -> 8.32 us
  starting transfers between devices: 35 us -> 22.6 us
    ppermute x20 -> x17, waiting for transfers between devices: 70.6 us -> 44.7 us  [swap(): lax.ppermute(values, axis, [(d, d ^ flip) for d in range(lax.axis_size(ax...]
    ppermute x20 -> x17, starting transfers between devices: 34.8 us -> 22.4 us  [swap(): lax.ppermute(values, axis, [(d, d ^ flip) for d in range(lax.axis_size(ax...]
    reshape x9 -> x0, local copies, waits for them, and re-layouts: 9.11 us -> none  [the longest x2 3.67 us: per_device(): inner_grad.reshape(own, parts, devices, own).transpose(0, 2, 1, 3)]
    pallas_call x1, Pallas kernels: 62.2 us -> 70.8 us  [attention_backward(): pl.pallas_call(functools.partial(backward_kernel, chips), grid_spec=pltpu...]
    reduce_scatter x2, waiting for transfers between devices: 8.25 us -> 0.01 us  [over_planes(): return lax.psum_scatter(partial, 'dp', scatter_dimension=0, tiled=True)]
    pallas_call x1, Pallas kernels: 42 us -> 50 us  [attention_forward(): pl.pallas_call(forward_kernel, grid_spec=pltpu.PrefetchScalarGridSpec(num...]
    pallas_call x0 -> x4, Pallas kernels: none -> 5.74 us  [the longest x2 3.93 us: fetching_call(): small_call(kernel, shape, name, room=60, in_specs=[pl.BlockSpec(memory_sp...]
  transfers between devices with their start and end apart: 23 -> 21, of which waited for: 13 -> 12; matrix products, arithmetic and copies ran while one was open for 6% -> 6% of each run, Pallas kernels for 40% -> 49%
where the time goes in v4:
time: 361 us
  Pallas kernels  244 us (68%)
  waiting for transfers between devices  46.2 us (13%)
  starting transfers between devices  22.6 us (6%)
  between operations  19.1 us (5%)
  matrix products  12.8 us (4%)
  other arithmetic  8.64 us (2%)
  local copies, waits for them, and re-layouts  8.32 us (2%)
    pallas_call x1, Pallas kernels, attention_backward(): pl.pallas_call(functools.partial(backward_kernel, chips), grid_spec=pltpu...  70.8 us
    pallas_call x1, Pallas kernels, upper_half(): pl.pallas_call(functools.partial(upper_kernel, parts, width, tokens), gri...  62.1 us
    pallas_call x1, Pallas kernels, lower_half(): pl.pallas_call(functools.partial(lower_kernel, parts, width, tokens), gri...  54.2 us
    pallas_call x1, Pallas kernels, attention_forward(): pl.pallas_call(forward_kernel, grid_spec=pltpu.PrefetchScalarGridSpec(num...  50 us
    ppermute x17, waiting for transfers between devices, swap(): lax.ppermute(values, axis, [(d, d ^ flip) for d in range(lax.axis_size(ax...  44.7 us
    ppermute x17, starting transfers between devices, swap(): lax.ppermute(values, axis, [(d, d ^ flip) for d in range(lax.axis_size(ax...  22.4 us
    dot_general x1, matrix products, dot(): lax.dot_general(left, right, (((left_dim,), (right_dim,)), ((), ())), pre...  12.8 us
  transfers between devices with their start and end apart: 21, of which 12 were waited for; matrix products, arithmetic and copies ran while one was open for 6% of the time, Pallas kernels for 49%

profile of v4, /device:TPU:0, one launch (start us, length us, event | category | flops | bytes accessed | tf_op | source)
XLA Modules:
  0.0 361.3 jit_solution(12216569664956086719)
XLA Ops:
  7.2 1.7 pack_near.1.after_ref
  9.0 2.2 pack_far.1
  11.3 5.1 %collective-permute-start.2 = (bf16[24,2432]{1,0:T(8,128)(2,1)}, bf16[24,2432]{1,0:T(8,128)(2,1)S(1)}, u32[]{:S(2)}, u32[]{:S(2)}) collective-permute-start(bf16[24,2432]{1,0:T(8,128)(2,1)} %pack_near.1.after_ref), channel_id=1, source_target_pairs={{0,3},{1,2},{2,1},{3,0},{4,7},{5,6},{6,5},{7,4},{8,11},{9,10},{10,... | collective-permute-start | bytes 350216 | tf_op jit(solution)/shard_map/ppermute | solution.py:644
  16.4 0.6 collective-permute-start
  17.0 0.9 reduce_window_sum.11
  17.9 0.7 broadcast_subtract_fusion
  18.5 0.1 broadcast_minimum_fusion
  18.6 2.1 collective-permute-done.2
  20.7 5.8 %collective-permute-done.1 = bf16[24,2432]{1,0:T(8,128)(2,1)S(1)} collective-permute-done((bf16[24,2432]{1,0:T(8,128)(2,1)}, bf16[24,2432]{1,0:T(8,128)(2,1)S(1)}, u32[]{:S(2)}, u32[]{:S(2)}) %collective-permute-start.1) | collective-permute-done | bytes 116768 | tf_op jit(solution)/shard_map/ppermute | solution.py:644
  26.5 1.0 pad_maximum_fusion.1.refs_0_
  27.5 2.5 collective-permute-start.8
  30.0 0.5 collective-permute-start.6
  30.5 0.5 collective-permute-start.4
  31.1 0.1 pad.16.clone
  31.1 0.1 copy.43
  31.2 0.1 convert_reduce_fusion
  31.3 0.1 add_add_fusion
  31.4 0.2 select_reduce_fusion
  31.6 0.1 collective-permute-start.3
  31.7 10.4 %collective-permute-done.8.refs_6_ = bf16[4,24,2432]{2,1,0:T(8,128)(2,1)S(1)} collective-permute-done((bf16[4,24,2432]{2,1,0:T(8,128)(2,1)S(1)}, bf16[4,24,2432]{2,1,0:T(8,128)(2,1)S(1)}, u32[]{:S(2)}, u32[]{:S(2)}) %collective-permute-start.8) | collective-permute-done | bytes 466976 | tf_op jit(solution)/shard_map/ppermute | solution.py:644
  42.1 8.3 %collective-permute-done.6.refs_4_ = bf16[4,24,2432]{2,1,0:T(8,128)(2,1)S(1)} collective-permute-done((bf16[4,24,2432]{2,1,0:T(8,128)(2,1)S(1)}, bf16[4,24,2432]{2,1,0:T(8,128)(2,1)S(1)}, u32[]{:S(2)}, u32[]{:S(2)}) %collective-permute-start.6) | collective-permute-done | bytes 466976 | tf_op jit(solution)/shard_map/ppermute | solution.py:644
  50.4 1.3 collective-permute-done.4.refs_2_
  51.7 0.1 pad_add_fusion.where_ref
  51.8 0.1 pad.5.clone
  51.9 0.1 compare_select_fusion
  52.0 0.3 collective-permute-done.7.refs_5_
  52.2 1.3 collective-permute-done.5.refs_3_
  53.5 0.8 place.1
  54.4 1.8 copy-done
  56.2 0.1 copy.46
  56.4 0.6 slice.146.vec_ref
  57.0 0.1 pad_maximum_fusion.2
  57.1 0.3 broadcast_in_dim.53.segc_ref
  57.5 50.0 %attention_forward.1 = (bf16[2,1024,2304]{2,1,0:T(8,128)(2,1)}, bf16[2,1024,768]{2,1,0:T(8,128)(2,1)S(1)}, f32[2,3,8,1024]{3,2,1,0:T(8,128)S(1)}) custom-call(s32[2,4]{1,0:T(2,128)S(1)} %get-tuple-element.90.low_ref, s32[2,4]{1,0:T(2,128)S(1)} %get-tuple-element.91.count_ref, bf16[2,1024,768]{2,1,0:T(8,128)(2,1)} %rows_ref.3, bf16[768,2432]{1,0:T(8,128)(2,1)} %bitcast.61, ...), custom_call_target="tpu_custom_call" | custom-call | flops 58787364864 | bytes 15728640 | tf_op jit(solution)/shard_map/attention_forward/pallas_call | solution.py:113
  107.5 1.6 copy-done.4
  109.1 62.1 %upper_half.1 = (bf16[2048,768]{1,0:T(8,128)(2,1)}, f32[2048,768]{1,0:T(8,128)}, f32[2048,128]{1,0:T(8,128)}, f32[2048,768]{1,0:T(8,128)}, bf16[2048,3072]{1,0:T...) custom-call(s32[2]{0:T(128)} %pad_ref.3, bf16[2048,768]{1,0:T(8,128)(2,1)} %bitcast.63, ...), custom_call_target="tpu_custom_call" | custom-call | flops 31406948352 | bytes 84148224 | tf_op jit(solution)/shard_map/upper_half/pallas_call | solution.py:561
  171.3 54.2 %lower_half.1 = (f32[2048,768]{1,0:T(8,128)}, bf16[2048,768]{1,0:T(8,128)(2,1)}, bf16[768,3840]{1,0:T(8,128)(2,1)}, f32[16,768]{1,0:T(8,128)}) custom-call(bf16[2048,768]{1,0:T(8,128)(2,1)} %bitcast.64, f32[2048,768]{1,0:T(8,128)} %get-tuple-element.56.normed_ref, f32[2048,128]{1,0:T(8,128)} %get-tuple-element.57.inverse_ref, ...), custom_call_target="tpu_custom_call" | custom-call | flops 33822867456 | bytes 84148224 | tf_op jit(solution)/shard_map/lower_half/pallas_call | solution.py:609
  225.6 0.0 reduce-scatter.8.cloned.1.call-start
  225.7 0.5 copy-done.3
  226.2 0.2 copy-done.5
  226.4 70.8 %attention_backward.1 = (bf16[2,1024,2304]{2,1,0:T(8,128)(2,1)}, bf16[4,96,2432]{2,1,0:T(8,128)(2,1)S(1)}, bf16[4,96,2432]{2,1,0:T(8,128)(2,1)}) custom-call(s32[2,4]{1,0:T(2,128)S(1)} %get-tuple-element.90.low_ref, s32[2,4]{1,0:T(2,128)S(1)} %get-tuple-element.91.count_ref, s32[2]{0:T(128)S(1)} %copy-done.3, s32[1]{0:T(128)} %bitcast.1.plane_ref, ...), custom_call_target="tpu_custom_call" | custom-call | flops 110326972416 | bytes 31457280 | tf_op jit(solution)/shard_map/attention_backward/pallas_call | solution.py:281
  297.2 0.1 collective-permute-start.10
  297.3 2.5 pad_maximum_fusion
  299.9 1.5 collective-permute-done.10
  301.4 1.9 fusion.8
  303.3 6.9 %collective-permute-start.11 = (bf16[96,2432]{1,0:T(8,128)(2,1)S(1)}, bf16[96,2432]{1,0:T(8,128)(2,1)S(1)}, u32[]{:S(2)}, u32[]{:S(2)}) collective-permute-start(bf16[96,2432]{1,0:T(8,128)(2,1)S(1)} %get-tuple-element.72), channel_id=1, source_target_pairs={{0,8},{4,12},{8,0},{12,4},{16,24},{20,28},{24,16},{28,20},{1,9},{5... | collective-permute-start | bytes 1400840 | tf_op jit(solution)/shard_map/ppermute | solution.py:644
  310.2 1.5 collective-permute-start.13
  311.7 12.8 %fusion.2 = f32[2048,768]{1,0:T(8,128)} fusion(f32[2048,768]{1,0:T(8,128)} %get-tuple-element.75, bf16[2048,2304]{1,0:T(8,128)(2,1)} %bitcast.73, bf16[768,2432]{1,0:T(8,128)(2,1)S(1)} %bitcast.62), kind=kOutput, calls=%fused_computation.2 | convolution fusion | flops 7249330176 | bytes 25559040 | tf_op jit(solution)/shard_map/dot_general | solution.py:32
  324.5 8.2 %collective-permute-done.12 = bf16[96,2432]{1,0:T(8,128)(2,1)S(1)} collective-permute-done((bf16[96,2432]{1,0:T(8,128)(2,1)S(1)}, bf16[96,2432]{1,0:T(8,128)(2,1)S(1)}, u32[]{:S(2)}, u32[]{:S(2)}) %collective-permute-start.12) | collective-permute-done | bytes 466976 | tf_op jit(solution)/shard_map/ppermute | solution.py:644
  332.7 0.2 add_convert_fusion
  332.9 1.4 reduce-scatter.8.cloned.1.call-done.far_ref
  334.3 1.3 collective-permute-start.16
  335.6 0.1 collective-permute-start.15
  335.7 3.1 collective-permute-start.14
  338.8 1.0 copy-done.2
  339.8 1.1 unpack_far.1
  340.9 1.5 collective-permute-done.16.refs_3_
  342.3 4.1 %collective-permute-done.15.refs_2_ = bf16[24,2432]{1,0:T(8,128)(2,1)S(1)} collective-permute-done((bf16[24,2432]{1,0:T(8,128)(2,1)S(1)}, bf16[24,2432]{1,0:T(8,128)(2,1)S(1)}, u32[]{:S(2)}, u32[]{:S(2)}) %collective-permute-start.15) | collective-permute-done | bytes 116768 | tf_op jit(solution)/shard_map/ppermute | solution.py:644
  346.4 0.7 finish_near.1
  347.1 0.5 slice_bitcast_fusion
  347.7 0.6 fusion.12
  348.3 0.6 reshape.190
  354.0 0.1 sqrt_reduce_fusion
  354.2 0.6 pad_maximum_fusion.3
  (41 shorter events, 0.4 us)
Async XLA Ops:
  7.2 101.9 %all-gather.2.cloned.1.call-start = ((), (), s32[]{:S(2)}) async-start(), calls=%async_computation.3 | async-start | bytes 10948608 | tf_op jit(solution)/shard_map/all_gather | solution.py:640
  11.2 286.1 %reduce-scatter.6.cloned.1.call-start = ((), (), s32[]{:S(2)}) async-start(), calls=%async_computation.5 | async-start | bytes 5308416 | tf_op jit(solution)/shard_map/reduce_scatter | solution.py:696
  11.3 9.4 %collective-permute-start.2 = (bf16[24,2432]{1,0:T(8,128)(2,1)}, bf16[24,2432]{1,0:T(8,128)(2,1)S(1)}, u32[]{:S(2)}, u32[]{:S(2)}) collective-permute-start(bf16[24,2432]{1,0:T(8,128)(2,1)} %pack_near.1.after_ref), channel_id=1, source_target_pairs={{0,3},{1,2},{2,1},{3,0},{4,7},{5,6},{6,5},{7,4},{8,11},{9,10},{10,... | collective-permute-start | bytes 350216 | tf_op jit(solution)/shard_map/ppermute | solution.py:644
  16.4 10.1 %collective-permute-start.1 = (bf16[24,2432]{1,0:T(8,128)(2,1)}, bf16[24,2432]{1,0:T(8,128)(2,1)S(1)}, u32[]{:S(2)}, u32[]{:S(2)}) collective-permute-start(bf16[24,2432]{1,0:T(8,128)(2,1)} %pack_near.1.after_ref), channel_id=1, source_target_pairs={{0,2},{1,3},{2,0},{3,1},{4,6},{5,7},{6,4},{7,5},{8,10},{9,11},{10,... | collective-permute-start | bytes 350216 | tf_op jit(solution)/shard_map/ppermute | solution.py:644
  16.4 10.1 %collective-permute-start = (bf16[24,2432]{1,0:T(8,128)(2,1)}, bf16[24,2432]{1,0:T(8,128)(2,1)S(1)}, u32[]{:S(2)}, u32[]{:S(2)}) collective-permute-start(bf16[24,2432]{1,0:T(8,128)(2,1)} %pack_near.1.after_ref), channel_id=1, source_target_pairs={{0,1},{1,0},{2,3},{3,2},{4,5},{5,4},{6,7},{7,6},{8,9},{9,8},{10,11... | collective-permute-start | bytes 350216 | tf_op jit(solution)/shard_map/ppermute | solution.py:644
  27.5 14.6 %collective-permute-start.8 = (bf16[4,24,2432]{2,1,0:T(8,128)(2,1)S(1)}, bf16[4,24,2432]{2,1,0:T(8,128)(2,1)S(1)}, u32[]{:S(2)}, u32[]{:S(2)}) collective-permute-start(bf16[4,24,2432]{2,1,0:T(8,128)(2,1)S(1)} %pad_maximum_fusion.1.refs_0_), channel_id=1, source_target_pairs={{0,24},{4,28},{8,16},{12,20},{16,8},{20,12},{24,0},{28,4},{1,25},{... | collective-permute-start | bytes 1400840 | tf_op jit(solution)/shard_map/ppermute | solution.py:644
  30.0 20.4 %collective-permute-start.6 = (bf16[4,24,2432]{2,1,0:T(8,128)(2,1)S(1)}, bf16[4,24,2432]{2,1,0:T(8,128)(2,1)S(1)}, u32[]{:S(2)}, u32[]{:S(2)}) collective-permute-start(bf16[4,24,2432]{2,1,0:T(8,128)(2,1)S(1)} %pad_maximum_fusion.1.refs_0_), channel_id=1, source_target_pairs={{0,16},{4,20},{8,24},{12,28},{16,0},{20,4},{24,8},{28,12},{1,17},{... | collective-permute-start | bytes 1400840 | tf_op jit(solution)/shard_map/ppermute | solution.py:644
  30.5 21.2 %collective-permute-start.4 = (bf16[4,24,2432]{2,1,0:T(8,128)(2,1)S(1)}, bf16[4,24,2432]{2,1,0:T(8,128)(2,1)S(1)}, u32[]{:S(2)}, u32[]{:S(2)}) collective-permute-start(bf16[4,24,2432]{2,1,0:T(8,128)(2,1)S(1)} %pad_maximum_fusion.1.refs_0_), channel_id=1, source_target_pairs={{0,8},{4,12},{8,0},{12,4},{16,24},{20,28},{24,16},{28,20},{1,9},{5... | collective-permute-start | bytes 1400840 | tf_op jit(solution)/shard_map/ppermute | solution.py:644
  31.6 20.3 %collective-permute-start.3 = (bf16[4,24,2432]{2,1,0:T(8,128)(2,1)S(1)}, bf16[4,24,2432]{2,1,0:T(8,128)(2,1)S(1)}, u32[]{:S(2)}, u32[]{:S(2)}) collective-permute-start(bf16[4,24,2432]{2,1,0:T(8,128)(2,1)S(1)} %pad_maximum_fusion.1.refs_0_), channel_id=1, source_target_pairs={{0,4},{4,0},{8,12},{12,8},{16,20},{20,16},{24,28},{28,24},{1,5},{5... | collective-permute-start | bytes 1400840 | tf_op jit(solution)/shard_map/ppermute | solution.py:644
  42.1 9.8 %collective-permute-start.9 = (bf16[4,24,2432]{2,1,0:T(8,128)(2,1)S(1)}, bf16[4,24,2432]{2,1,0:T(8,128)(2,1)S(1)}, u32[]{:S(2)}, u32[]{:S(2)}) collective-permute-start(bf16[4,24,2432]{2,1,0:T(8,128)(2,1)S(1)} %collective-permute-done.8.refs_6_), channel_id=1, source_target_pairs={{0,4},{4,0},{8,12},{12,8},{16,20},{20,16},{24,28},{28,24},{1,5},{5... | collective-permute-start | bytes 1400840 | tf_op jit(solution)/shard_map/ppermute | solution.py:644
  50.4 1.8 collective-permute-start.7
  51.7 1.8 collective-permute-start.5
  54.3 1.8 copy-start
  107.5 1.6 copy-start.4
  171.3 126.0 %reduce-scatter.4.cloned.1.call-start = ((), (), s32[]{:S(2)}) async-start(), calls=%async_computation.4 | async-start | bytes 6635520 | tf_op jit(solution)/shard_map/reduce_scatter | solution.py:696
  225.5 0.7 copy-start.3
  225.6 0.8 copy-start.5
  225.6 0.8 copy-start.6
  225.6 108.7 %reduce-scatter.8.cloned.1.call-start = ((), (), s32[]{:S(2)}) async-start(), calls=%async_computation.6 | async-start | bytes 1658880 | tf_op jit(solution)/shard_map/reduce_scatter | solution.py:700
  297.2 4.2 %collective-permute-start.10 = (bf16[4,96,2432]{2,1,0:T(8,128)(2,1)}, bf16[4,96,2432]{2,1,0:T(8,128)(2,1)}, u32[]{:S(2)}, u32[]{:S(2)}) collective-permute-start(bf16[4,96,2432]{2,1,0:T(8,128)(2,1)} %get-tuple-element.69), channel_id=1, source_target_pairs={{0,4},{4,0},{8,12},{12,8},{16,20},{20,16},{24,28},{28,24},{1,5},{5... | collective-permute-start | bytes 5603336 | tf_op jit(solution)/shard_map/ppermute | solution.py:644
  299.9 11.9 %copy-start.1 = (bf16[32,24,2432]{2,1,0:T(8,128)(2,1)S(1)}, bf16[32,24,2432]{2,1,0:T(8,128)(2,1)}, u32[]{:S(2)}) copy-start(bf16[32,24,2432]{2,1,0:T(8,128)(2,1)} %copy-done) | copy-start | bytes 11206660
  303.3 21.2 %collective-permute-start.11 = (bf16[96,2432]{1,0:T(8,128)(2,1)S(1)}, bf16[96,2432]{1,0:T(8,128)(2,1)S(1)}, u32[]{:S(2)}, u32[]{:S(2)}) collective-permute-start(bf16[96,2432]{1,0:T(8,128)(2,1)S(1)} %get-tuple-element.72), channel_id=1, source_target_pairs={{0,8},{4,12},{8,0},{12,4},{16,24},{20,28},{24,16},{28,20},{1,9},{5... | collective-permute-start | bytes 1400840 | tf_op jit(solution)/shard_map/ppermute | solution.py:644
  310.2 22.5 %collective-permute-start.12 = (bf16[96,2432]{1,0:T(8,128)(2,1)S(1)}, bf16[96,2432]{1,0:T(8,128)(2,1)S(1)}, u32[]{:S(2)}, u32[]{:S(2)}) collective-permute-start(bf16[96,2432]{1,0:T(8,128)(2,1)S(1)} %get-tuple-element.73), channel_id=1, source_target_pairs={{0,16},{4,20},{8,24},{12,28},{16,0},{20,4},{24,8},{28,12},{1,17},{... | collective-permute-start | bytes 1400840 | tf_op jit(solution)/shard_map/ppermute | solution.py:644
  310.2 22.5 %collective-permute-start.13 = (bf16[96,2432]{1,0:T(8,128)(2,1)S(1)}, bf16[96,2432]{1,0:T(8,128)(2,1)S(1)}, u32[]{:S(2)}, u32[]{:S(2)}) collective-permute-start(bf16[96,2432]{1,0:T(8,128)(2,1)S(1)} %get-tuple-element.74), channel_id=1, source_target_pairs={{0,24},{4,28},{8,16},{12,20},{16,8},{20,12},{24,0},{28,4},{1,25},{... | collective-permute-start | bytes 1400840 | tf_op jit(solution)/shard_map/ppermute | solution.py:644
  334.3 8.0 %collective-permute-start.16 = (bf16[24,2432]{1,0:T(8,128)(2,1)S(1)}, bf16[24,2432]{1,0:T(8,128)(2,1)S(1)}, u32[]{:S(2)}, u32[]{:S(2)}) collective-permute-start(bf16[24,2432]{1,0:T(8,128)(2,1)S(1)} %get-tuple-element.96), channel_id=1, source_target_pairs={{0,3},{1,2},{2,1},{3,0},{4,7},{5,6},{6,5},{7,4},{8,11},{9,10},{10,... | collective-permute-start | bytes 350216 | tf_op jit(solution)/shard_map/ppermute | solution.py:644
  335.6 10.8 %collective-permute-start.15 = (bf16[24,2432]{1,0:T(8,128)(2,1)S(1)}, bf16[24,2432]{1,0:T(8,128)(2,1)S(1)}, u32[]{:S(2)}, u32[]{:S(2)}) collective-permute-start(bf16[24,2432]{1,0:T(8,128)(2,1)S(1)} %get-tuple-element.97), channel_id=1, source_target_pairs={{0,2},{1,3},{2,0},{3,1},{4,6},{5,7},{6,4},{7,5},{8,10},{9,11},{10,... | collective-permute-start | bytes 350216 | tf_op jit(solution)/shard_map/ppermute | solution.py:644
  335.7 10.7 %collective-permute-start.14 = (bf16[24,2432]{1,0:T(8,128)(2,1)S(1)}, bf16[24,2432]{1,0:T(8,128)(2,1)S(1)}, u32[]{:S(2)}, u32[]{:S(2)}) collective-permute-start(bf16[24,2432]{1,0:T(8,128)(2,1)S(1)} %get-tuple-element.98), channel_id=1, source_target_pairs={{0,1},{1,0},{2,3},{3,2},{4,5},{5,4},{6,7},{7,6},{8,9},{9,8},{10,11... | collective-permute-start | bytes 350216 | tf_op jit(solution)/shard_map/ppermute | solution.py:644
  338.8 1.0 copy-start.2
Sparse Core Ops, SparseCore 0:
  11.4 96.6 all-gather.1
  171.4 53.5 reduce-scatter.5
  228.9 59.6 reduce-scatter.3
  300.0 34.2 reduce-scatter.7

commit v5 on v4

--- a/solution.py
+++ b/solution.py
@@ -62,12 +62,17 @@
 
 
 def forward_kernel(
-    low_ref, count_ref, rows_ref, w_ref, bias_ref, segc_ref, segr_ref,
-    qkv_ref, mixed_ref, lse_ref, keyt_ref,
+    low_ref, count_ref, rows_ref, w_ref, bias_ref, segr_ref,
+    qkv_ref, mixed_ref, lse_ref, keyt_ref, segc_ref,
 ):
     s = pl.program_id(0)
     qkv_ref[...] = (dot(rows_ref[...], w_ref[...]) + bias_ref[0:1, :]).astype(BF16)
     keyt_ref[...] = qkv_ref[:, GROUP : 2 * GROUP].T
+
+    @pl.when(pl.program_id(1) == 0)
+    def _():
+        segc_ref[...] = jnp.broadcast_to(segr_ref[...], (128, LEN)).T
+
     masks = head_masks(GROUP)
 
     def block(i, carry):
@@ -107,7 +112,7 @@
     lax.fori_loop(0, LEN // QB, block, 0)
 
 
-def attention_forward(rows, w, bias, segc, segr, low, count):
+def attention_forward(rows, w, bias, segment, low, count):
     seqs, _, width = rows.shape
     groups = width // GROUP
     return pl.pallas_call(
@@ -118,33 +123,32 @@
             in_specs=[
                 pl.BlockSpec((None, LEN, width), lambda s, g, *_: (s, 0, 0)),
                 pl.BlockSpec((width, TRIPLE), lambda s, g, *_: (0, g)),
-                pl.BlockSpec((8, TRIPLE), lambda s, g, *_: (0, g)),
-                pl.BlockSpec((None, LEN, 128), lambda s, g, *_: (s, 0, 0)),
-                pl.BlockSpec((None, 8, LEN), lambda s, g, *_: (s, 0, 0)),
+                pl.BlockSpec((1, TRIPLE), lambda s, g, *_: (0, g)),
+                pl.BlockSpec((None, 1, LEN), lambda s, g, *_: (s, 0, 0)),
             ],
             out_specs=[
                 pl.BlockSpec((None, LEN, TRIPLE), lambda s, g, *_: (s, 0, g)),
                 pl.BlockSpec((None, LEN, GROUP), lambda s, g, *_: (s, 0, g)),
                 pl.BlockSpec((None, None, 8, LEN), lambda s, g, *_: (s, g, 0, 0)),
             ],
-            scratch_shapes=[pltpu.VMEM((GROUP, LEN), BF16)],
+            scratch_shapes=[pltpu.VMEM((GROUP, LEN), BF16), pltpu.VMEM((LEN, 128), jnp.int32)],
         ),
         out_shape=[
             jax.ShapeDtypeStruct((seqs, LEN, 3 * width), BF16),
             jax.ShapeDtypeStruct((seqs, LEN, width), BF16),
             jax.ShapeDtypeStruct((seqs, groups, 8, LEN), F32),
         ],
-        compiler_params=pltpu.CompilerParams(vmem_limit_bytes=48 * 2**20),
+        compiler_params=pltpu.CompilerParams(vmem_limit_bytes=60 * 2**20),
         cost_estimate=cost(2 * seqs * LEN * width * (3 * width + 16 * LEN), seqs * LEN * width * 10),
         name="attention_forward",
-    )(low, count, rows, w, bias, segc, segr)
+    )(low, count, rows, w, bias, segment)
 
 
 def backward_kernel(
     chips,
-    low_ref, count_ref, pad_ref, plane_ref, qkv_ref, mixed_ref, grad_ref, rows_ref, lse_ref, segc_ref, segr_ref, vec_ref, stats_ref,
+    low_ref, count_ref, pad_ref, plane_ref, qkv_ref, mixed_ref, grad_ref, rows_ref, lse_ref, segr_ref, vec_ref, stats_ref,
     dqkv_ref, keep_ref, send_ref,
-    q_ref, qt_ref, gt_ref, kt_ref, dqt_ref, acc_ref, delta_ref, sums_ref, stage_ref, columns_ref, rowst_ref, sem,
+    q_ref, qt_ref, gt_ref, kt_ref, dqt_ref, acc_ref, delta_ref, sums_ref, stage_ref, columns_ref, rowst_ref, segc_ref, sem,
 ):
     s, g = pl.program_id(0), pl.program_id(1)
     masks = head_masks(PAIR)
@@ -152,6 +156,7 @@
     @pl.when(g == 0)
     def _():
         rowst_ref[...] = rows_ref[...].T
+        segc_ref[...] = jnp.broadcast_to(segr_ref[...], (128, LEN)).T
 
     @pl.when((g == 0) & (s == 0))
     def _():
@@ -273,7 +278,7 @@
             move.wait()
 
 
-def attention_backward(qkv, mixed, grad, rows, lse, segc, segr, vec, stats, low, count, pad, chips):
+def attention_backward(qkv, mixed, grad, rows, lse, segment, vec, stats, low, count, pad, chips):
     seqs, _, width = mixed.shape
     groups = width // GROUP
     plane = lax.axis_index("dp").astype(jnp.int32).reshape(1)
@@ -289,8 +294,7 @@
                 pl.BlockSpec((None, LEN, GROUP), lambda s, g, *_: (s, 0, g)),
                 pl.BlockSpec((None, LEN, width), lambda s, g, *_: (s, 0, 0)),
                 pl.BlockSpec((None, None, 8, LEN), lambda s, g, *_: (s, g, 0, 0)),
-                pl.BlockSpec((None, LEN, 128), lambda s, g, *_: (s, 0, 0)),
-                pl.BlockSpec((None, 8, LEN), lambda s, g, *_: (s, 0, 0)),
+                pl.BlockSpec((None, 1, LEN), lambda s, g, *_: (s, 0, 0)),
                 pl.BlockSpec((16, width), lambda s, g, *_: (0, 0)),
                 pl.BlockSpec((8, width), lambda s, g, *_: (0, 0)),
             ],
@@ -311,6 +315,7 @@
                 pltpu.VMEM((width, TRIPLE), BF16),
                 pltpu.VMEM((width, VEC), BF16),
                 pltpu.VMEM((width, LEN), BF16),
+                pltpu.VMEM((LEN, 128), jnp.int32),
                 pltpu.SemaphoreType.DMA((2 * max(1, 2 * chips),)),
             ],
         ),
@@ -319,10 +324,10 @@
             jax.ShapeDtypeStruct(packed, BF16),
             jax.ShapeDtypeStruct(packed if chips else (8, 128), BF16),
         ],
-        compiler_params=pltpu.CompilerParams(vmem_limit_bytes=48 * 2**20),
+        compiler_params=pltpu.CompilerParams(vmem_limit_bytes=60 * 2**20),
         cost_estimate=cost(2 * seqs * LEN * width * (3 * width + 32 * LEN), seqs * LEN * width * 20),
         name="attention_backward",
-    )(low, count, pad, plane, qkv, mixed, grad, rows, lse, segc, segr, vec, stats)
+    )(low, count, pad, plane, qkv, mixed, grad, rows, lse, segment, vec, stats)
 
 
 def mean(values):
@@ -403,7 +408,7 @@
         part_ref[...] = jnp.zeros_like(part_ref)
 
     def vector(row):
-        return vec_ref[row : row + 1, :]
+        return vec_ref[row + 2 : row + 3, :]
 
     def valid_of():
         place = (i % per_seq) * tokens + lax.broadcasted_iota(jnp.int32, (tokens, 1), 0)
@@ -428,7 +433,7 @@
     def feed(j, carry):
         weights.wait(1 + j)
         weights.wait(1 + parts + j)
-        inner = dot(low_ref[...], held_ref[1 + j]) + vec_ref[pl.ds(6 + j, 1), :]
+        inner = dot(low_ref[...], held_ref[1 + j]) + vec_ref[pl.ds(8 + j, 1), :]
         half = 0.5 * (1.0 + lax.erf(inner * ROOT_HALF))
         hidden = (inner * half).astype(BF16)
         hidden_ref[j, mine, :] = hidden
@@ -488,7 +493,7 @@
         part_ref[...] = jnp.zeros_like(part_ref)
 
     def vector(row):
-        return vec_ref[row : row + 1, :]
+        return vec_ref[row + 2 : row + 3, :]
 
     upper = upper_ref[...]
     res_ref[...] = upper
@@ -563,7 +568,7 @@
         grid_spec=pltpu.PrefetchScalarGridSpec(
             num_scalar_prefetch=1,
             grid=(count // tokens,),
-            in_specs=[block(width), block(width), block(width), anywhere, fixed(16, width)],
+            in_specs=[block(width), block(width), block(width), anywhere, fixed(24, width)],
             out_specs=[
                 block(width), block(width), block(128), block(width), block(parts * width), anywhere,
                 fixed(16, width), fixed(8, width),
@@ -611,7 +616,7 @@
         grid=(count // tokens,),
         in_specs=[
             block(width), block(width), block(128), block(width), block(parts * width), anywhere,
-            fixed(16, width), fixed(16, width),
+            fixed(24, width), fixed(16, width),
         ],
         out_specs=[block(width), block(width), anywhere, fixed(16, width)],
         scratch_shapes=[
@@ -790,15 +795,29 @@
         outer_ref[j * own : (j + 1) * own, :] = far_ref[:, (1 + parts + j) * width : (2 + parts + j) * width].astype(F32)
 
 
-def finish_kernel(*refs):
-    blocks, (query_ref, key_ref, value_ref, vectors_ref) = refs[:-4], refs[-4:]
+def finish_kernel(all_tokens, lines, *refs):
+    blocks, (query_ref, key_ref, value_ref), rest = refs[: -(lines + 5)], refs[-(lines + 5) : -(lines + 2)], refs[-(lines + 2) :]
+    vector_refs, stats_ref, long_ref = rest[:lines], rest[lines], rest[lines + 1]
     total = tree_sum([block[...] for block in blocks])
-    width = query_ref.shape[1]
+    own, width = query_ref.shape
     for g in range(width // GROUP):
         for k, target in enumerate((query_ref, key_ref, value_ref)):
             first = (3 * g + k) * GROUP
             target[:, g * GROUP : (g + 1) * GROUP] = total[:, first : first + GROUP]
-    vectors_ref[...] = total[:, 3 * width :].T
+    vectors = total[:, 3 * width :].T
+    for row, target in enumerate(vector_refs):
+        for j in range(target.shape[0] // own):
+            long_ref[0:1, j * own : (j + 1) * own] = vectors[row + j : row + j + 1, :]
+        target[...] = long_ref[0:1, : target.shape[0]].reshape(target.shape[0])
+    line = total[0:1, 3 * width :]
+    lane = lax.broadcasted_iota(jnp.int32, line.shape, 1)
+    scale = jnp.zeros_like(line)
+    for digit in range(DIGITS):
+        scale = jnp.where(lane == 20 + digit, 8.0**digit, scale)
+    valid = jnp.sum(line * scale, axis=1, keepdims=True)
+    roots = jnp.sqrt(jnp.where((lane >= 16) & (lane < 20), line, 0.0) / (valid * width))
+    roots = jnp.where(lane == 15, valid / all_tokens, roots)
+    stats_ref[...] = roots[:, 15:20].reshape(5)
 
 
 def pack_near(query, key, value, vectors):
@@ -842,15 +861,24 @@
     )
 
 
-def finish_near(blocks):
+def finish_near(blocks, parts, all_tokens, stats, valid_own):
     own = blocks[0].shape[0]
     width = (blocks[0].shape[1] - VEC) // 3
+    sizes = [own] * 8 + [parts * own]
     if quick(own):
-        shapes = [jax.ShapeDtypeStruct(shape, F32) for shape in [(own, width)] * 3 + [(VEC, own)]]
-        return small_call(finish_kernel, shapes, "finish_near")(*blocks)
+        shapes = [(own, width)] * 3 + [(size,) for size in sizes] + [(5,)]
+        shapes = [jax.ShapeDtypeStruct(shape, F32) for shape in shapes]
+        kernel = functools.partial(finish_kernel, all_tokens, len(sizes))
+        scratch = [pltpu.VMEM((8, max(sizes)), F32)]
+        query, key, value, *rest = small_call(kernel, shapes, "finish_near", scratch_shapes=scratch)(*blocks)
+        return query, key, value, rest[:-1], rest[-1]
     total = tree_sum(blocks)
     triple = total[:, : 3 * width].reshape(own, width // GROUP, 3, GROUP)
-    return [triple[:, :, k].reshape(own, width) for k in range(3)] + [total[:, 3 * width :].T]
+    mine = total[:, 3 * width :].T
+    sums = lax.psum(jnp.concatenate([jnp.sum(stats[:4], axis=1), valid_own[None]]), AXES)
+    layer_stats = jnp.concatenate([sums[4:] / all_tokens, jnp.sqrt(sums[:4] / (sums[4] * width))])
+    vectors = [mine[row] for row in range(8)] + [mine[8 : 8 + parts].reshape(parts * own)]
+    return *(triple[:, :, k].reshape(own, width) for k in range(3)), vectors, layer_stats
 
 
 def per_device(
@@ -870,16 +898,14 @@
     near = quick_gather(near_own)
     far = gather(pack_far(merge_weight, inner_weight, outer_weight, near_own))
     segment, low, count = segments(doc_lengths, pad_tail)
-    segc = jnp.broadcast_to(segment[:, :, None], (seqs, LEN, 128))
-    segr = jnp.broadcast_to(segment[:, None, :], (seqs, 8, LEN))
+    segment = segment[:, None, :]
 
     vec_rows = near[:, 3 * width :].T.astype(F32)
     bias = jnp.stack([vec_rows[0], jnp.zeros((width,), F32), vec_rows[1]])
     bias = bias.reshape(3, groups, GROUP).transpose(1, 0, 2).reshape(1, 3 * width)
-    bias = jnp.broadcast_to(bias, (8, 3 * width))
-    vec = vec_rows[2:18]
-
-    qkv, mixed, lse = attention_forward(layer_input, near, bias, segc, segr, low, count)
+    vec = vec_rows[:24]
+
+    qkv, mixed, lse = attention_forward(layer_input, near, bias, segment, low, count)
     tokens = seqs * LEN
     flat_mixed = mixed.reshape(tokens, width)
     output, normed, inverse, upper, slope, outer_partial, sums, stats = upper_half(
@@ -890,7 +916,7 @@
     inner_grad = over_planes(inner_partial)
     chips = lax.axis_size("dp") // 2 if quick(own) else 0
     dqkv, keep, send = attention_backward(
-        qkv, mixed, mixed_grad.reshape(mixed.shape), layer_input, lse, segc, segr, sums, stats, low, count, pad_tail, chips
+        qkv, mixed, mixed_grad.reshape(mixed.shape), layer_input, lse, segment, sums, stats, low, count, pad_tail, chips
     )
     far_planes = jnp.concatenate([inner_grad, outer_grad], axis=1)
     if chips:
@@ -908,19 +934,11 @@
         near_blocks = swap_blocks(blocks_for_columns(near_planes))
     else:
         near_blocks = [over_columns(near_planes)]
-    query_grad, key_grad, value_grad, mine = finish_near(near_blocks)
+    valid_own = jnp.sum(LEN - pad_tail).astype(F32)
+    query_grad, key_grad, value_grad, mine, layer_stats = finish_near(
+        near_blocks, parts, tokens * devices, stats, valid_own
+    )
     merge_grad, inner_grad, outer_grad = unpack_far(far_grad, parts)
-    inner_bias_gradient = mine[8 : 8 + parts].reshape(parts * own)
-    all_tokens = tokens * devices
-    if quick(own):
-        totals = mine[16 : 20 + DIGITS, 0]
-        valid_total = sum(totals[4 + digit] * 8.0**digit for digit in range(DIGITS))
-    else:
-        valid_own = jnp.sum(LEN - pad_tail).astype(F32)
-        totals = lax.psum(jnp.concatenate([jnp.sum(stats[:4], axis=1), valid_own[None]]), AXES)
-        valid_total = totals[4]
-    share = jnp.reshape(valid_total / all_tokens, (1,))
-    layer_stats = jnp.concatenate([share, jnp.sqrt(totals[:4] / (valid_total * width))])
     return (
         output.reshape(layer_input.shape),
         input_gradient.reshape(layer_input.shape),
@@ -934,7 +952,7 @@
         mine[3],
         mine[4],
         inner_grad,
-        inner_bias_gradient,
+        mine[8],
         outer_grad,
         mine[2],
         mine[0],

time: 361 us -> 354 us (0.981)
  Pallas kernels: 244 us -> 235 us
  between operations: 19.1 us -> 14 us
  waiting for transfers between devices: 46.2 us -> 51.3 us
  local copies, waits for them, and re-layouts: 8.32 us -> 4.54 us
    pallas_call x1, Pallas kernels: 70.8 us -> 65.2 us  [attention_backward(): pl.pallas_call(functools.partial(backward_kernel, chips), grid_spec=pltpu...]
    ppermute x17, starting transfers between devices: 22.4 us -> 26 us  [swap(): lax.ppermute(values, axis, [(d, d ^ flip) for d in range(lax.axis_size(ax...]
  transfers between devices with their start and end apart: 21 -> 21, of which waited for: 12 -> 12; matrix products, arithmetic and copies ran while one was open for 6% -> 7% of each run, Pallas kernels for 49% -> 48%
where the time goes in v5:
time: 354 us; the launch traced here: 353 us
  Pallas kernels  235 us (66%)
  waiting for transfers between devices  51.3 us (14%)
  starting transfers between devices  26.2 us (7%)
  between operations  14 us (4%)
  matrix products  12.8 us (4%)
  other arithmetic  9.03 us (3%)
  local copies, waits for them, and re-layouts  4.54 us (1%)
    pallas_call x1, Pallas kernels, attention_backward(): pl.pallas_call(functools.partial(backward_kernel, chips), grid_spec=pltpu...  65.2 us
    pallas_call x1, Pallas kernels, upper_half(): pl.pallas_call(functools.partial(upper_kernel, parts, width, tokens), gri...  62.3 us
    pallas_call x1, Pallas kernels, lower_half(): pl.pallas_call(functools.partial(lower_kernel, parts, width, tokens), gri...  53.7 us
    pallas_call x1, Pallas kernels, attention_forward(): pl.pallas_call(forward_kernel, grid_spec=pltpu.PrefetchScalarGridSpec(num...  47.3 us
    ppermute x17, waiting for transfers between devices, swap(): lax.ppermute(values, axis, [(d, d ^ flip) for d in range(lax.axis_size(ax...  43.4 us
    ppermute x17, starting transfers between devices, swap(): lax.ppermute(values, axis, [(d, d ^ flip) for d in range(lax.axis_size(ax...  26 us
    dot_general x1, matrix products, dot(): lax.dot_general(left, right, (((left_dim,), (right_dim,)), ((), ())), pre...  12.8 us
  transfers between devices with their start and end apart: 21, of which 12 were waited for; matrix products, arithmetic and copies ran while one was open for 7% of the time, Pallas kernels for 48%

profile of v5, /device:TPU:0, one launch (start us, length us, event | category | flops | bytes accessed | tf_op | source)
XLA Modules:
  0.0 353.0 jit_solution(1316328887595363803)
XLA Ops:
  7.2 0.0 all-gather.2.cloned.1.call-start
  7.2 1.7 pack_near.1.after_ref
  9.0 2.2 pack_far.1
  11.2 0.0 all-gather.2.cloned.1.call-update
  11.2 0.0 reduce-scatter.6.cloned.1.call-start
  11.3 5.1 %collective-permute-start.2 = (bf16[24,2432]{1,0:T(8,128)(2,1)}, bf16[24,2432]{1,0:T(8,128)(2,1)S(1)}, u32[]{:S(2)}, u32[]{:S(2)}) collective-permute-start(bf16[24,2432]{1,0:T(8,128)(2,1)} %pack_near.1.after_ref), channel_id=1, source_target_pairs={{0,3},{1,2},{2,1},{3,0},{4,7},{5,6},{6,5},{7,4},{8,11},{9,10},{10,... | collective-permute-start | bytes 350216 | tf_op jit(solution)/shard_map/ppermute | solution.py:649
  16.4 0.6 collective-permute-start
  17.0 0.9 reduce_window_sum.11
  17.9 0.7 broadcast_subtract_fusion
  18.5 0.1 broadcast_minimum_fusion
  18.6 2.1 collective-permute-done.2
  20.7 5.8 %collective-permute-done.1 = bf16[24,2432]{1,0:T(8,128)(2,1)S(1)} collective-permute-done((bf16[24,2432]{1,0:T(8,128)(2,1)}, bf16[24,2432]{1,0:T(8,128)(2,1)S(1)}, u32[]{:S(2)}, u32[]{:S(2)}) %collective-permute-start.1) | collective-permute-done | bytes 116768 | tf_op jit(solution)/shard_map/ppermute | solution.py:649
  26.5 1.0 pad_maximum_fusion.1.refs_0_
  27.5 2.5 collective-permute-start.8
  30.0 0.5 collective-permute-start.6
  30.5 0.5 collective-permute-start.4
  31.1 0.1 pad.14.clone
  31.1 0.1 copy.44
  31.2 0.1 convert_reduce_fusion
  31.3 0.1 add_add_fusion
  31.4 0.2 select_reduce_fusion
  31.6 0.1 collective-permute-start.3
  31.7 10.4 %collective-permute-done.8.refs_6_ = bf16[4,24,2432]{2,1,0:T(8,128)(2,1)S(1)} collective-permute-done((bf16[4,24,2432]{2,1,0:T(8,128)(2,1)S(1)}, bf16[4,24,2432]{2,1,0:T(8,128)(2,1)S(1)}, u32[]{:S(2)}, u32[]{:S(2)}) %collective-permute-start.8) | collective-permute-done | bytes 466976 | tf_op jit(solution)/shard_map/ppermute | solution.py:649
  42.1 8.3 %collective-permute-done.6.refs_4_ = bf16[4,24,2432]{2,1,0:T(8,128)(2,1)S(1)} collective-permute-done((bf16[4,24,2432]{2,1,0:T(8,128)(2,1)S(1)}, bf16[4,24,2432]{2,1,0:T(8,128)(2,1)S(1)}, u32[]{:S(2)}, u32[]{:S(2)}) %collective-permute-start.6) | collective-permute-done | bytes 466976 | tf_op jit(solution)/shard_map/ppermute | solution.py:649
  50.4 1.3 collective-permute-done.4.refs_2_
  51.7 0.1 pad_add_fusion.where_ref
  51.8 0.1 pad.3.clone
  51.9 0.6 subtract_minimum_fusion
  52.5 0.7 compare_select_fusion.segr_ref
  53.1 0.4 collective-permute-done.5.refs_3_
  53.5 0.8 place.1
  54.4 1.8 copy-done
  56.2 0.1 copy.47
  56.4 0.6 slice.55.vec_ref
  57.0 0.1 pad_maximum_fusion.2
  57.1 0.6 reshape.132.bias_ref
  57.8 47.3 %attention_forward.1 = (bf16[2,1024,2304]{2,1,0:T(8,128)(2,1)}, bf16[2,1024,768]{2,1,0:T(8,128)(2,1)}, f32[2,3,8,1024]{3,2,1,0:T(8,128)}) custom-call(s32[2,4]{1,0:T(2,128)} %get-tuple-element.108.low_ref, s32[2,4]{1,0:T(2,128)} %get-tuple-element.109.count_ref, bf16[2,1024,768]{2,1,0:T(8,128)(2,1)} %rows_ref.3, bf16[768,2432]{1,0:T(8,128)(2,1)} %bitcast.41, ...), custom_call_target="tpu_custom_call" | custom-call | flops 58787364864 | bytes 15728640 | tf_op jit(solution)/shard_map/attention_forward/pallas_call | solution.py:118
  105.1 3.0 all-gather.2.cloned.1.call-done.w_ref
  108.1 62.3 %upper_half.1 = (bf16[2048,768]{1,0:T(8,128)(2,1)}, f32[2048,768]{1,0:T(8,128)}, f32[2048,128]{1,0:T(8,128)}, f32[2048,768]{1,0:T(8,128)}, bf16[2048,3072]{1,0:T...) custom-call(s32[2]{0:T(128)} %pad_ref.3, bf16[2048,768]{1,0:T(8,128)(2,1)} %bitcast.54, ...), custom_call_target="tpu_custom_call" | custom-call | flops 31406948352 | bytes 84148224 | tf_op jit(solution)/shard_map/upper_half/pallas_call | solution.py:566
  170.4 0.0 reduce-scatter.6.cloned.1.call-update
  170.4 0.0 reduce-scatter.4.cloned.1.call-start
  170.4 53.7 %lower_half.1 = (f32[2048,768]{1,0:T(8,128)}, bf16[2048,768]{1,0:T(8,128)(2,1)}, bf16[768,3840]{1,0:T(8,128)(2,1)}, f32[16,768]{1,0:T(8,128)}) custom-call(bf16[2048,768]{1,0:T(8,128)(2,1)} %bitcast.55, f32[2048,768]{1,0:T(8,128)} %get-tuple-element.65.normed_ref, f32[2048,128]{1,0:T(8,128)} %get-tuple-element.66.inverse_ref, ...), custom_call_target="tpu_custom_call" | custom-call | flops 33822867456 | bytes 84148224 | tf_op jit(solution)/shard_map/lower_half/pallas_call | solution.py:614
  224.2 0.0 reduce-scatter.4.cloned.1.call-update
  224.2 0.0 reduce-scatter.8.cloned.1.call-start
  224.2 65.2 %attention_backward.1 = (bf16[2,1024,2304]{2,1,0:T(8,128)(2,1)}, bf16[4,96,2432]{2,1,0:T(8,128)(2,1)}, bf16[4,96,2432]{2,1,0:T(8,128)(2,1)}) custom-call(s32[2,4]{1,0:T(2,128)} %get-tuple-element.108.low_ref, s32[2,4]{1,0:T(2,128)} %get-tuple-element.109.count_ref, s32[2]{0:T(128)} %pad_ref.3, s32[1]{0:T(128)} %bitcast.1.plane_ref, ...), custom_call_target="tpu_custom_call" | custom-call | flops 110326972416 | bytes 31457280 | tf_op jit(solution)/shard_map/attention_backward/pallas_call | solution.py:286
  289.4 2.3 collective-permute-start.10
  291.7 2.5 pad_maximum_fusion
  294.2 0.0 reduce-scatter.8.cloned.1.call-update
  294.3 1.3 collective-permute-done.10
  295.5 1.9 fusion.8
  297.4 8.3 %collective-permute-start.11 = (bf16[96,2432]{1,0:T(8,128)(2,1)S(1)}, bf16[96,2432]{1,0:T(8,128)(2,1)S(1)}, u32[]{:S(2)}, u32[]{:S(2)}) collective-permute-start(bf16[96,2432]{1,0:T(8,128)(2,1)S(1)} %get-tuple-element.81), channel_id=1, source_target_pairs={{0,8},{4,12},{8,0},{12,4},{16,24},{20,28},{24,16},{28,20},{1,9},{5... | collective-permute-start | bytes 1400840 | tf_op jit(solution)/shard_map/ppermute | solution.py:649
  305.7 1.5 collective-permute-start.13
  307.3 12.8 %fusion.2 = f32[2048,768]{1,0:T(8,128)} fusion(f32[2048,768]{1,0:T(8,128)} %get-tuple-element.84, bf16[2048,2304]{1,0:T(8,128)(2,1)} %bitcast.51, bf16[768,2432]{1,0:T(8,128)(2,1)S(1)} %bitcast.42), kind=kOutput, calls=%fused_computation.2 | convolution fusion | flops 7249330176 | bytes 25559040 | tf_op jit(solution)/shard_map/dot_general | solution.py:32
  320.1 8.3 %collective-permute-done.12 = bf16[96,2432]{1,0:T(8,128)(2,1)S(1)} collective-permute-done((bf16[96,2432]{1,0:T(8,128)(2,1)S(1)}, bf16[96,2432]{1,0:T(8,128)(2,1)S(1)}, u32[]{:S(2)}, u32[]{:S(2)}) %collective-permute-start.12) | collective-permute-done | bytes 466976 | tf_op jit(solution)/shard_map/ppermute | solution.py:649
  328.4 0.2 add_convert_fusion
  328.7 4.8 %reduce-scatter.8.cloned.1.call-done.far_ref = bf16[24,6912]{1,0:T(8,128)(2,1)} async-done(((bf16[96,6912]{1,0:T(8,128)(2,1)}), bf16[24,6912]{1,0:T(8,128)(2,1)}) %reduce-scatter.8.cloned.1.call-update) | async-done | bytes 331792 | tf_op jit(solution)/shard_map/reduce_scatter | solution.py:705
  333.5 1.3 collective-permute-start.16
  334.8 0.1 collective-permute-start.15
  334.9 3.1 collective-permute-start.14
  338.0 1.0 copy-done.2
  338.9 1.1 unpack_far.1
  340.0 1.5 collective-permute-done.16.refs_3_
  341.5 4.1 %collective-permute-done.15.refs_2_ = bf16[24,2432]{1,0:T(8,128)(2,1)S(1)} collective-permute-done((bf16[24,2432]{1,0:T(8,128)(2,1)S(1)}, bf16[24,2432]{1,0:T(8,128)(2,1)S(1)}, u32[]{:S(2)}, u32[]{:S(2)}) %collective-permute-start.15) | collective-permute-done | bytes 116768 | tf_op jit(solution)/shard_map/ppermute | solution.py:649
  345.6 0.8 finish_near.1
  (28 shorter events, 0.2 us)
Async XLA Ops:
  7.2 100.9 %all-gather.2.cloned.1.call-start = ((), (), s32[]{:S(2)}) async-start(), calls=%async_computation.3 | async-start | bytes 10948608 | tf_op jit(solution)/shard_map/all_gather | solution.py:645
  11.2 280.5 %reduce-scatter.6.cloned.1.call-start = ((), (), s32[]{:S(2)}) async-start(), calls=%async_computation.5 | async-start | bytes 5308416 | tf_op jit(solution)/shard_map/reduce_scatter | solution.py:701
  11.3 9.4 %collective-permute-start.2 = (bf16[24,2432]{1,0:T(8,128)(2,1)}, bf16[24,2432]{1,0:T(8,128)(2,1)S(1)}, u32[]{:S(2)}, u32[]{:S(2)}) collective-permute-start(bf16[24,2432]{1,0:T(8,128)(2,1)} %pack_near.1.after_ref), channel_id=1, source_target_pairs={{0,3},{1,2},{2,1},{3,0},{4,7},{5,6},{6,5},{7,4},{8,11},{9,10},{10,... | collective-permute-start | bytes 350216 | tf_op jit(solution)/shard_map/ppermute | solution.py:649
  16.4 10.1 %collective-permute-start.1 = (bf16[24,2432]{1,0:T(8,128)(2,1)}, bf16[24,2432]{1,0:T(8,128)(2,1)S(1)}, u32[]{:S(2)}, u32[]{:S(2)}) collective-permute-start(bf16[24,2432]{1,0:T(8,128)(2,1)} %pack_near.1.after_ref), channel_id=1, source_target_pairs={{0,2},{1,3},{2,0},{3,1},{4,6},{5,7},{6,4},{7,5},{8,10},{9,11},{10,... | collective-permute-start | bytes 350216 | tf_op jit(solution)/shard_map/ppermute | solution.py:649
  16.4 10.1 %collective-permute-start = (bf16[24,2432]{1,0:T(8,128)(2,1)}, bf16[24,2432]{1,0:T(8,128)(2,1)S(1)}, u32[]{:S(2)}, u32[]{:S(2)}) collective-permute-start(bf16[24,2432]{1,0:T(8,128)(2,1)} %pack_near.1.after_ref), channel_id=1, source_target_pairs={{0,1},{1,0},{2,3},{3,2},{4,5},{5,4},{6,7},{7,6},{8,9},{9,8},{10,11... | collective-permute-start | bytes 350216 | tf_op jit(solution)/shard_map/ppermute | solution.py:649
  27.5 14.6 %collective-permute-start.8 = (bf16[4,24,2432]{2,1,0:T(8,128)(2,1)S(1)}, bf16[4,24,2432]{2,1,0:T(8,128)(2,1)S(1)}, u32[]{:S(2)}, u32[]{:S(2)}) collective-permute-start(bf16[4,24,2432]{2,1,0:T(8,128)(2,1)S(1)} %pad_maximum_fusion.1.refs_0_), channel_id=1, source_target_pairs={{0,24},{4,28},{8,16},{12,20},{16,8},{20,12},{24,0},{28,4},{1,25},{... | collective-permute-start | bytes 1400840 | tf_op jit(solution)/shard_map/ppermute | solution.py:649
  30.0 20.4 %collective-permute-start.6 = (bf16[4,24,2432]{2,1,0:T(8,128)(2,1)S(1)}, bf16[4,24,2432]{2,1,0:T(8,128)(2,1)S(1)}, u32[]{:S(2)}, u32[]{:S(2)}) collective-permute-start(bf16[4,24,2432]{2,1,0:T(8,128)(2,1)S(1)} %pad_maximum_fusion.1.refs_0_), channel_id=1, source_target_pairs={{0,16},{4,20},{8,24},{12,28},{16,0},{20,4},{24,8},{28,12},{1,17},{... | collective-permute-start | bytes 1400840 | tf_op jit(solution)/shard_map/ppermute | solution.py:649
  30.5 21.2 %collective-permute-start.4 = (bf16[4,24,2432]{2,1,0:T(8,128)(2,1)S(1)}, bf16[4,24,2432]{2,1,0:T(8,128)(2,1)S(1)}, u32[]{:S(2)}, u32[]{:S(2)}) collective-permute-start(bf16[4,24,2432]{2,1,0:T(8,128)(2,1)S(1)} %pad_maximum_fusion.1.refs_0_), channel_id=1, source_target_pairs={{0,8},{4,12},{8,0},{12,4},{16,24},{20,28},{24,16},{28,20},{1,9},{5... | collective-permute-start | bytes 1400840 | tf_op jit(solution)/shard_map/ppermute | solution.py:649
  31.6 21.5 %collective-permute-start.3 = (bf16[4,24,2432]{2,1,0:T(8,128)(2,1)S(1)}, bf16[4,24,2432]{2,1,0:T(8,128)(2,1)S(1)}, u32[]{:S(2)}, u32[]{:S(2)}) collective-permute-start(bf16[4,24,2432]{2,1,0:T(8,128)(2,1)S(1)} %pad_maximum_fusion.1.refs_0_), channel_id=1, source_target_pairs={{0,4},{4,0},{8,12},{12,8},{16,20},{20,16},{24,28},{28,24},{1,5},{5... | collective-permute-start | bytes 1400840 | tf_op jit(solution)/shard_map/ppermute | solution.py:649
  42.1 11.0 %collective-permute-start.9 = (bf16[4,24,2432]{2,1,0:T(8,128)(2,1)S(1)}, bf16[4,24,2432]{2,1,0:T(8,128)(2,1)S(1)}, u32[]{:S(2)}, u32[]{:S(2)}) collective-permute-start(bf16[4,24,2432]{2,1,0:T(8,128)(2,1)S(1)} %collective-permute-done.8.refs_6_), channel_id=1, source_target_pairs={{0,4},{4,0},{8,12},{12,8},{16,20},{20,16},{24,28},{28,24},{1,5},{5... | collective-permute-start | bytes 1400840 | tf_op jit(solution)/shard_map/ppermute | solution.py:649
  50.4 2.7 collective-permute-start.7
  51.7 1.8 collective-permute-start.5
  54.3 1.8 copy-start
  170.4 121.3 %reduce-scatter.4.cloned.1.call-start = ((), (), s32[]{:S(2)}) async-start(), calls=%async_computation.4 | async-start | bytes 6635520 | tf_op jit(solution)/shard_map/reduce_scatter | solution.py:701
  224.2 109.3 %reduce-scatter.8.cloned.1.call-start = ((), (), s32[]{:S(2)}) async-start(), calls=%async_computation.6 | async-start | bytes 1658880 | tf_op jit(solution)/shard_map/reduce_scatter | solution.py:705
  289.4 6.1 %copy-start.3 = (bf16[4,96,2432]{2,1,0:T(8,128)(2,1)S(1)}, bf16[4,96,2432]{2,1,0:T(8,128)(2,1)}, u32[]{:S(2)}) copy-start(bf16[4,96,2432]{2,1,0:T(8,128)(2,1)} %get-tuple-element.77) | copy-start | bytes 5603332
  289.4 6.1 %collective-permute-start.10 = (bf16[4,96,2432]{2,1,0:T(8,128)(2,1)}, bf16[4,96,2432]{2,1,0:T(8,128)(2,1)}, u32[]{:S(2)}, u32[]{:S(2)}) collective-permute-start(bf16[4,96,2432]{2,1,0:T(8,128)(2,1)} %get-tuple-element.78), channel_id=1, source_target_pairs={{0,4},{4,0},{8,12},{12,8},{16,20},{20,16},{24,28},{28,24},{1,5},{5... | collective-permute-start | bytes 5603336 | tf_op jit(solution)/shard_map/ppermute | solution.py:649
  294.3 13.0 %copy-start.1 = (bf16[32,24,2432]{2,1,0:T(8,128)(2,1)S(1)}, bf16[32,24,2432]{2,1,0:T(8,128)(2,1)}, u32[]{:S(2)}) copy-start(bf16[32,24,2432]{2,1,0:T(8,128)(2,1)} %copy-done) | copy-start | bytes 11206660
  297.4 22.7 %collective-permute-start.11 = (bf16[96,2432]{1,0:T(8,128)(2,1)S(1)}, bf16[96,2432]{1,0:T(8,128)(2,1)S(1)}, u32[]{:S(2)}, u32[]{:S(2)}) collective-permute-start(bf16[96,2432]{1,0:T(8,128)(2,1)S(1)} %get-tuple-element.81), channel_id=1, source_target_pairs={{0,8},{4,12},{8,0},{12,4},{16,24},{20,28},{24,16},{28,20},{1,9},{5... | collective-permute-start | bytes 1400840 | tf_op jit(solution)/shard_map/ppermute | solution.py:649
  305.7 22.7 %collective-permute-start.12 = (bf16[96,2432]{1,0:T(8,128)(2,1)S(1)}, bf16[96,2432]{1,0:T(8,128)(2,1)S(1)}, u32[]{:S(2)}, u32[]{:S(2)}) collective-permute-start(bf16[96,2432]{1,0:T(8,128)(2,1)S(1)} %get-tuple-element.82), channel_id=1, source_target_pairs={{0,16},{4,20},{8,24},{12,28},{16,0},{20,4},{24,8},{28,12},{1,17},{... | collective-permute-start | bytes 1400840 | tf_op jit(solution)/shard_map/ppermute | solution.py:649
  305.7 22.7 %collective-permute-start.13 = (bf16[96,2432]{1,0:T(8,128)(2,1)S(1)}, bf16[96,2432]{1,0:T(8,128)(2,1)S(1)}, u32[]{:S(2)}, u32[]{:S(2)}) collective-permute-start(bf16[96,2432]{1,0:T(8,128)(2,1)S(1)} %get-tuple-element.83), channel_id=1, source_target_pairs={{0,24},{4,28},{8,16},{12,20},{16,8},{20,12},{24,0},{28,4},{1,25},{... | collective-permute-start | bytes 1400840 | tf_op jit(solution)/shard_map/ppermute | solution.py:649
  333.5 8.0 %collective-permute-start.16 = (bf16[24,2432]{1,0:T(8,128)(2,1)S(1)}, bf16[24,2432]{1,0:T(8,128)(2,1)S(1)}, u32[]{:S(2)}, u32[]{:S(2)}) collective-permute-start(bf16[24,2432]{1,0:T(8,128)(2,1)S(1)} %get-tuple-element.114), channel_id=1, source_target_pairs={{0,3},{1,2},{2,1},{3,0},{4,7},{5,6},{6,5},{7,4},{8,11},{9,10},{10,... | collective-permute-start | bytes 350216 | tf_op jit(solution)/shard_map/ppermute | solution.py:649
  334.8 10.8 %collective-permute-start.15 = (bf16[24,2432]{1,0:T(8,128)(2,1)S(1)}, bf16[24,2432]{1,0:T(8,128)(2,1)S(1)}, u32[]{:S(2)}, u32[]{:S(2)}) collective-permute-start(bf16[24,2432]{1,0:T(8,128)(2,1)S(1)} %get-tuple-element.115), channel_id=1, source_target_pairs={{0,2},{1,3},{2,0},{3,1},{4,6},{5,7},{6,4},{7,5},{8,10},{9,11},{10,... | collective-permute-start | bytes 350216 | tf_op jit(solution)/shard_map/ppermute | solution.py:649
  334.9 10.7 %collective-permute-start.14 = (bf16[24,2432]{1,0:T(8,128)(2,1)S(1)}, bf16[24,2432]{1,0:T(8,128)(2,1)S(1)}, u32[]{:S(2)}, u32[]{:S(2)}) collective-permute-start(bf16[24,2432]{1,0:T(8,128)(2,1)S(1)} %get-tuple-element.116), channel_id=1, source_target_pairs={{0,1},{1,0},{2,3},{3,2},{4,5},{5,4},{6,7},{7,6},{8,9},{9,8},{10,11... | collective-permute-start | bytes 350216 | tf_op jit(solution)/shard_map/ppermute | solution.py:649
  338.0 1.0 copy-start.2
Sparse Core Ops, SparseCore 0:
  11.4 96.6 all-gather.1
  170.5 54.5 reduce-scatter.5
  229.0 59.6 reduce-scatter.3
  294.4 39.0 reduce-scatter.7

commit v6 on v5

--- a/solution.py
+++ b/solution.py
@@ -930,15 +930,16 @@
         near_planes = over_planes(keep[0])
     input_gradient = residual + dot(dqkv.reshape(tokens, 3 * width), near[:, : 3 * width], 1, 1)
     if chips:
-        near_planes, input_gradient, far_grad = lax.optimization_barrier((near_planes, input_gradient, far_grad))
+        near_planes, input_gradient = lax.optimization_barrier((near_planes, input_gradient))
         near_blocks = swap_blocks(blocks_for_columns(near_planes))
     else:
         near_blocks = [over_columns(near_planes)]
+    merge_grad, inner_grad, outer_grad = unpack_far(far_grad, parts)
+    near_blocks[0], merge_grad = lax.optimization_barrier((near_blocks[0], merge_grad))
     valid_own = jnp.sum(LEN - pad_tail).astype(F32)
     query_grad, key_grad, value_grad, mine, layer_stats = finish_near(
         near_blocks, parts, tokens * devices, stats, valid_own
     )
-    merge_grad, inner_grad, outer_grad = unpack_far(far_grad, parts)
     return (
         output.reshape(layer_input.shape),
         input_gradient.reshape(layer_input.shape),

time: 354 us -> 350 us (0.989)
  Pallas kernels: 235 us -> 246 us
  starting transfers between devices: 26.2 us -> 18.6 us
  waiting for transfers between devices: 51.3 us -> 44.3 us
    ppermute x17, starting transfers between devices: 26 us -> 18.4 us  [swap(): lax.ppermute(values, axis, [(d, d ^ flip) for d in range(lax.axis_size(ax...]
    pallas_call x1, Pallas kernels: 65.2 us -> 71.6 us  [attention_backward(): pl.pallas_call(functools.partial(backward_kernel, chips), grid_spec=pltpu...]
    reduce_scatter x1, waiting for transfers between devices: 4.83 us -> 0.36 us  [over_columns(): return lax.psum_scatter(partial, 'fsdp', scatter_dimension=0, tiled=True)]
    pallas_call x1, Pallas kernels: 47.3 us -> 51.6 us  [attention_forward(): pl.pallas_call(forward_kernel, grid_spec=pltpu.PrefetchScalarGridSpec(num...]
  transfers between devices with their start and end apart: 21 -> 21, of which waited for: 12 -> 11; matrix products, arithmetic and copies ran while one was open for 7% -> 7% of each run, Pallas kernels for 48% -> 51%
where the time goes in v6:
time: 350 us
  Pallas kernels  246 us (70%)
  waiting for transfers between devices  44.3 us (13%)
  starting transfers between devices  18.6 us (5%)
  between operations  14 us (4%)
  matrix products  12.9 us (4%)
  other arithmetic  9.14 us (3%)
  local copies, waits for them, and re-layouts  4.55 us (1%)
    pallas_call x1, Pallas kernels, attention_backward(): pl.pallas_call(functools.partial(backward_kernel, chips), grid_spec=pltpu...  71.6 us
    pallas_call x1, Pallas kernels, upper_half(): pl.pallas_call(functools.partial(upper_kernel, parts, width, tokens), gri...  62.3 us
    pallas_call x1, Pallas kernels, lower_half(): pl.pallas_call(functools.partial(lower_kernel, parts, width, tokens), gri...  54 us
    pallas_call x1, Pallas kernels, attention_forward(): pl.pallas_call(forward_kernel, grid_spec=pltpu.PrefetchScalarGridSpec(num...  51.6 us
    ppermute x17, waiting for transfers between devices, swap(): lax.ppermute(values, axis, [(d, d ^ flip) for d in range(lax.axis_size(ax...  43.8 us
    ppermute x17, starting transfers between devices, swap(): lax.ppermute(values, axis, [(d, d ^ flip) for d in range(lax.axis_size(ax...  18.4 us
    dot_general x1, matrix products, dot(): lax.dot_general(left, right, (((left_dim,), (right_dim,)), ((), ())), pre...  12.9 us
  transfers between devices with their start and end apart: 21, of which 11 were waited for; matrix products, arithmetic and copies ran while one was open for 7% of the time, Pallas kernels for 51%

profile of v6, /device:TPU:0, one launch (start us, length us, event | category | flops | bytes accessed | tf_op | source)
XLA Modules:
  0.0 349.7 jit_solution(4239345104531273029)
XLA Ops:
  7.2 0.0 all-gather.2.cloned.1.call-start
  7.2 1.7 pack_near.1.after_ref
  9.0 2.2 pack_far.1
  11.2 0.0 all-gather.2.cloned.1.call-update
  11.2 0.0 reduce-scatter.6.cloned.1.call-start
  11.3 5.1 %collective-permute-start.2 = (bf16[24,2432]{1,0:T(8,128)(2,1)}, bf16[24,2432]{1,0:T(8,128)(2,1)S(1)}, u32[]{:S(2)}, u32[]{:S(2)}) collective-permute-start(bf16[24,2432]{1,0:T(8,128)(2,1)} %pack_near.1.after_ref), channel_id=1, source_target_pairs={{0,3},{1,2},{2,1},{3,0},{4,7},{5,6},{6,5},{7,4},{8,11},{9,10},{10,... | collective-permute-start | bytes 350216 | tf_op jit(solution)/shard_map/ppermute | solution.py:649
  16.4 0.6 collective-permute-start
  17.0 0.9 reduce_window_sum.11
  17.9 0.7 broadcast_subtract_fusion
  18.5 0.1 broadcast_minimum_fusion
  18.6 2.1 collective-permute-done.2
  20.7 5.8 %collective-permute-done.1 = bf16[24,2432]{1,0:T(8,128)(2,1)S(1)} collective-permute-done((bf16[24,2432]{1,0:T(8,128)(2,1)}, bf16[24,2432]{1,0:T(8,128)(2,1)S(1)}, u32[]{:S(2)}, u32[]{:S(2)}) %collective-permute-start.1) | collective-permute-done | bytes 116768 | tf_op jit(solution)/shard_map/ppermute | solution.py:649
  26.5 1.0 pad_maximum_fusion.1.refs_0_
  27.5 2.5 collective-permute-start.8
  30.0 0.5 collective-permute-start.6
  30.5 0.5 collective-permute-start.4
  31.1 0.1 pad.14.clone
  31.1 0.1 copy.44
  31.2 0.1 convert_reduce_fusion
  31.3 0.1 add_add_fusion
  31.4 0.2 select_reduce_fusion
  31.6 0.1 collective-permute-start.3
  31.7 10.4 %collective-permute-done.8.refs_6_ = bf16[4,24,2432]{2,1,0:T(8,128)(2,1)S(1)} collective-permute-done((bf16[4,24,2432]{2,1,0:T(8,128)(2,1)S(1)}, bf16[4,24,2432]{2,1,0:T(8,128)(2,1)S(1)}, u32[]{:S(2)}, u32[]{:S(2)}) %collective-permute-start.8) | collective-permute-done | bytes 466976 | tf_op jit(solution)/shard_map/ppermute | solution.py:649
  42.1 8.3 %collective-permute-done.6.refs_4_ = bf16[4,24,2432]{2,1,0:T(8,128)(2,1)S(1)} collective-permute-done((bf16[4,24,2432]{2,1,0:T(8,128)(2,1)S(1)}, bf16[4,24,2432]{2,1,0:T(8,128)(2,1)S(1)}, u32[]{:S(2)}, u32[]{:S(2)}) %collective-permute-start.6) | collective-permute-done | bytes 466976 | tf_op jit(solution)/shard_map/ppermute | solution.py:649
  50.4 1.3 collective-permute-done.4.refs_2_
  51.7 0.1 pad_add_fusion.where_ref
  51.8 0.1 pad.3.clone
  51.9 0.6 subtract_minimum_fusion
  52.5 0.7 compare_select_fusion.segr_ref
  53.1 0.4 collective-permute-done.5.refs_3_
  53.5 0.8 place.1
  54.4 1.8 copy-done
  56.2 0.1 copy.47
  56.4 0.6 slice.55.vec_ref
  57.0 0.1 pad_maximum_fusion.2
  57.1 0.6 reshape.132.bias_ref
  57.8 51.6 %attention_forward.1 = (bf16[2,1024,2304]{2,1,0:T(8,128)(2,1)}, bf16[2,1024,768]{2,1,0:T(8,128)(2,1)}, f32[2,3,8,1024]{3,2,1,0:T(8,128)}) custom-call(s32[2,4]{1,0:T(2,128)} %get-tuple-element.110.low_ref, s32[2,4]{1,0:T(2,128)} %get-tuple-element.111.count_ref, bf16[2,1024,768]{2,1,0:T(8,128)(2,1)} %rows_ref.3, bf16[768,2432]{1,0:T(8,128)(2,1)} %bitcast.41, ...), custom_call_target="tpu_custom_call" | custom-call | flops 58787364864 | bytes 15728640 | tf_op jit(solution)/shard_map/attention_forward/pallas_call | solution.py:118
  109.4 62.3 %upper_half.1 = (bf16[2048,768]{1,0:T(8,128)(2,1)}, f32[2048,768]{1,0:T(8,128)}, f32[2048,128]{1,0:T(8,128)}, f32[2048,768]{1,0:T(8,128)}, bf16[2048,3072]{1,0:T...) custom-call(s32[2]{0:T(128)} %pad_ref.3, bf16[2048,768]{1,0:T(8,128)(2,1)} %bitcast.54, ...), custom_call_target="tpu_custom_call" | custom-call | flops 31406948352 | bytes 84148224 | tf_op jit(solution)/shard_map/upper_half/pallas_call | solution.py:566
  171.7 0.0 reduce-scatter.6.cloned.1.call-update
  171.7 0.0 reduce-scatter.4.cloned.1.call-start
  171.7 54.0 %lower_half.1 = (f32[2048,768]{1,0:T(8,128)}, bf16[2048,768]{1,0:T(8,128)(2,1)}, bf16[768,3840]{1,0:T(8,128)(2,1)}, f32[16,768]{1,0:T(8,128)}) custom-call(bf16[2048,768]{1,0:T(8,128)(2,1)} %bitcast.55, f32[2048,768]{1,0:T(8,128)} %get-tuple-element.66.normed_ref, f32[2048,128]{1,0:T(8,128)} %get-tuple-element.67.inverse_ref, ...), custom_call_target="tpu_custom_call" | custom-call | flops 33822867456 | bytes 84148224 | tf_op jit(solution)/shard_map/lower_half/pallas_call | solution.py:614
  225.8 0.0 reduce-scatter.4.cloned.1.call-update
  225.8 0.0 reduce-scatter.8.cloned.1.call-start
  225.8 71.6 %attention_backward.1 = (bf16[2,1024,2304]{2,1,0:T(8,128)(2,1)}, bf16[4,96,2432]{2,1,0:T(8,128)(2,1)}, bf16[4,96,2432]{2,1,0:T(8,128)(2,1)}) custom-call(s32[2,4]{1,0:T(2,128)} %get-tuple-element.110.low_ref, s32[2,4]{1,0:T(2,128)} %get-tuple-element.111.count_ref, s32[2]{0:T(128)} %pad_ref.3, s32[1]{0:T(128)} %bitcast.1.plane_ref, ...), custom_call_target="tpu_custom_call" | custom-call | flops 110326972416 | bytes 31457280 | tf_op jit(solution)/shard_map/attention_backward/pallas_call | solution.py:286
  297.5 0.1 collective-permute-start.10
  297.6 0.0 reduce-scatter.6.cloned.1.call-done
  297.6 0.0 reduce-scatter.4.cloned.1.call-done
  297.6 2.6 pad_maximum_fusion
  300.3 1.4 collective-permute-done.10
  301.7 1.9 fusion.8
  303.6 0.1 collective-permute-start.11
  303.7 1.6 collective-permute-start.12
  305.3 1.8 collective-permute-start.13
  307.1 12.9 %fusion.2 = f32[2048,768]{1,0:T(8,128)} fusion(f32[2048,768]{1,0:T(8,128)} %get-tuple-element.85, bf16[2048,2304]{1,0:T(8,128)(2,1)} %bitcast.51, bf16[768,2432]{1,0:T(8,128)(2,1)S(1)} %bitcast.42), kind=kOutput, calls=%fused_computation.2 | convolution fusion | flops 7249330176 | bytes 25559040 | tf_op jit(solution)/shard_map/dot_general | solution.py:32
  320.0 7.4 %collective-permute-done.13 = bf16[96,2432]{1,0:T(8,128)(2,1)S(1)} collective-permute-done((bf16[96,2432]{1,0:T(8,128)(2,1)S(1)}, bf16[96,2432]{1,0:T(8,128)(2,1)S(1)}, u32[]{:S(2)}, u32[]{:S(2)}) %collective-permute-start.13) | collective-permute-done | bytes 466976 | tf_op jit(solution)/shard_map/ppermute | solution.py:649
  327.4 0.2 add_convert_fusion
  327.7 4.8 %collective-permute-start.16 = (bf16[24,2432]{1,0:T(8,128)(2,1)S(1)}, bf16[24,2432]{1,0:T(8,128)(2,1)S(1)}, u32[]{:S(2)}, u32[]{:S(2)}) collective-permute-start(bf16[24,2432]{1,0:T(8,128)(2,1)S(1)} %get-tuple-element.116), channel_id=1, source_target_pairs={{0,3},{1,2},{2,1},{3,0},{4,7},{5,6},{6,5},{7,4},{8,11},{9,10},{10,... | collective-permute-start | bytes 350216 | tf_op jit(solution)/shard_map/ppermute | solution.py:649
  332.5 0.6 collective-permute-start.14
  333.1 0.4 reduce-scatter.8.cloned.1.call-done.far_ref
  333.5 1.0 copy-done.2
  334.5 1.1 unpack_far.1
  335.6 1.1 collective-permute-done.16.refs_3_
  336.6 5.6 %collective-permute-done.15.refs_2_ = bf16[24,2432]{1,0:T(8,128)(2,1)S(1)} collective-permute-done((bf16[24,2432]{1,0:T(8,128)(2,1)S(1)}, bf16[24,2432]{1,0:T(8,128)(2,1)S(1)}, u32[]{:S(2)}, u32[]{:S(2)}) %collective-permute-start.15) | collective-permute-done | bytes 116768 | tf_op jit(solution)/shard_map/ppermute | solution.py:649
  342.3 0.8 finish_near.1
  (28 shorter events, 0.2 us)
Async XLA Ops:
  7.2 102.2 %all-gather.2.cloned.1.call-start = ((), (), s32[]{:S(2)}) async-start(), calls=%async_computation.3 | async-start | bytes 10948608 | tf_op jit(solution)/shard_map/all_gather | solution.py:645
  11.2 286.4 %reduce-scatter.6.cloned.1.call-start = ((), (), s32[]{:S(2)}) async-start(), calls=%async_computation.5 | async-start | bytes 5308416 | tf_op jit(solution)/shard_map/reduce_scatter | solution.py:701
  11.3 9.4 %collective-permute-start.2 = (bf16[24,2432]{1,0:T(8,128)(2,1)}, bf16[24,2432]{1,0:T(8,128)(2,1)S(1)}, u32[]{:S(2)}, u32[]{:S(2)}) collective-permute-start(bf16[24,2432]{1,0:T(8,128)(2,1)} %pack_near.1.after_ref), channel_id=1, source_target_pairs={{0,3},{1,2},{2,1},{3,0},{4,7},{5,6},{6,5},{7,4},{8,11},{9,10},{10,... | collective-permute-start | bytes 350216 | tf_op jit(solution)/shard_map/ppermute | solution.py:649
  16.4 10.1 %collective-permute-start.1 = (bf16[24,2432]{1,0:T(8,128)(2,1)}, bf16[24,2432]{1,0:T(8,128)(2,1)S(1)}, u32[]{:S(2)}, u32[]{:S(2)}) collective-permute-start(bf16[24,2432]{1,0:T(8,128)(2,1)} %pack_near.1.after_ref), channel_id=1, source_target_pairs={{0,2},{1,3},{2,0},{3,1},{4,6},{5,7},{6,4},{7,5},{8,10},{9,11},{10,... | collective-permute-start | bytes 350216 | tf_op jit(solution)/shard_map/ppermute | solution.py:649
  16.4 10.1 %collective-permute-start = (bf16[24,2432]{1,0:T(8,128)(2,1)}, bf16[24,2432]{1,0:T(8,128)(2,1)S(1)}, u32[]{:S(2)}, u32[]{:S(2)}) collective-permute-start(bf16[24,2432]{1,0:T(8,128)(2,1)} %pack_near.1.after_ref), channel_id=1, source_target_pairs={{0,1},{1,0},{2,3},{3,2},{4,5},{5,4},{6,7},{7,6},{8,9},{9,8},{10,11... | collective-permute-start | bytes 350216 | tf_op jit(solution)/shard_map/ppermute | solution.py:649
  27.5 14.6 %collective-permute-start.8 = (bf16[4,24,2432]{2,1,0:T(8,128)(2,1)S(1)}, bf16[4,24,2432]{2,1,0:T(8,128)(2,1)S(1)}, u32[]{:S(2)}, u32[]{:S(2)}) collective-permute-start(bf16[4,24,2432]{2,1,0:T(8,128)(2,1)S(1)} %pad_maximum_fusion.1.refs_0_), channel_id=1, source_target_pairs={{0,24},{4,28},{8,16},{12,20},{16,8},{20,12},{24,0},{28,4},{1,25},{... | collective-permute-start | bytes 1400840 | tf_op jit(solution)/shard_map/ppermute | solution.py:649
  30.0 20.4 %collective-permute-start.6 = (bf16[4,24,2432]{2,1,0:T(8,128)(2,1)S(1)}, bf16[4,24,2432]{2,1,0:T(8,128)(2,1)S(1)}, u32[]{:S(2)}, u32[]{:S(2)}) collective-permute-start(bf16[4,24,2432]{2,1,0:T(8,128)(2,1)S(1)} %pad_maximum_fusion.1.refs_0_), channel_id=1, source_target_pairs={{0,16},{4,20},{8,24},{12,28},{16,0},{20,4},{24,8},{28,12},{1,17},{... | collective-permute-start | bytes 1400840 | tf_op jit(solution)/shard_map/ppermute | solution.py:649
  30.5 21.2 %collective-permute-start.4 = (bf16[4,24,2432]{2,1,0:T(8,128)(2,1)S(1)}, bf16[4,24,2432]{2,1,0:T(8,128)(2,1)S(1)}, u32[]{:S(2)}, u32[]{:S(2)}) collective-permute-start(bf16[4,24,2432]{2,1,0:T(8,128)(2,1)S(1)} %pad_maximum_fusion.1.refs_0_), channel_id=1, source_target_pairs={{0,8},{4,12},{8,0},{12,4},{16,24},{20,28},{24,16},{28,20},{1,9},{5... | collective-permute-start | bytes 1400840 | tf_op jit(solution)/shard_map/ppermute | solution.py:649
  31.6 21.5 %collective-permute-start.3 = (bf16[4,24,2432]{2,1,0:T(8,128)(2,1)S(1)}, bf16[4,24,2432]{2,1,0:T(8,128)(2,1)S(1)}, u32[]{:S(2)}, u32[]{:S(2)}) collective-permute-start(bf16[4,24,2432]{2,1,0:T(8,128)(2,1)S(1)} %pad_maximum_fusion.1.refs_0_), channel_id=1, source_target_pairs={{0,4},{4,0},{8,12},{12,8},{16,20},{20,16},{24,28},{28,24},{1,5},{5... | collective-permute-start | bytes 1400840 | tf_op jit(solution)/shard_map/ppermute | solution.py:649
  42.1 11.0 %collective-permute-start.9 = (bf16[4,24,2432]{2,1,0:T(8,128)(2,1)S(1)}, bf16[4,24,2432]{2,1,0:T(8,128)(2,1)S(1)}, u32[]{:S(2)}, u32[]{:S(2)}) collective-permute-start(bf16[4,24,2432]{2,1,0:T(8,128)(2,1)S(1)} %collective-permute-done.8.refs_6_), channel_id=1, source_target_pairs={{0,4},{4,0},{8,12},{12,8},{16,20},{20,16},{24,28},{28,24},{1,5},{5... | collective-permute-start | bytes 1400840 | tf_op jit(solution)/shard_map/ppermute | solution.py:649
  50.4 2.7 collective-permute-start.7
  51.7 1.8 collective-permute-start.5
  54.3 1.8 copy-start
  171.7 125.9 %reduce-scatter.4.cloned.1.call-start = ((), (), s32[]{:S(2)}) async-start(), calls=%async_computation.4 | async-start | bytes 6635520 | tf_op jit(solution)/shard_map/reduce_scatter | solution.py:701
  225.8 107.7 %reduce-scatter.8.cloned.1.call-start = ((), (), s32[]{:S(2)}) async-start(), calls=%async_computation.6 | async-start | bytes 1658880 | tf_op jit(solution)/shard_map/reduce_scatter | solution.py:705
  297.5 4.3 %copy-start.3 = (bf16[4,96,2432]{2,1,0:T(8,128)(2,1)S(1)}, bf16[4,96,2432]{2,1,0:T(8,128)(2,1)}, u32[]{:S(2)}) copy-start(bf16[4,96,2432]{2,1,0:T(8,128)(2,1)} %get-tuple-element.78) | copy-start | bytes 5603332
  297.5 4.2 %collective-permute-start.10 = (bf16[4,96,2432]{2,1,0:T(8,128)(2,1)}, bf16[4,96,2432]{2,1,0:T(8,128)(2,1)}, u32[]{:S(2)}, u32[]{:S(2)}) collective-permute-start(bf16[4,96,2432]{2,1,0:T(8,128)(2,1)} %get-tuple-element.79), channel_id=1, source_target_pairs={{0,4},{4,0},{8,12},{12,8},{16,20},{20,16},{24,28},{28,24},{1,5},{5... | collective-permute-start | bytes 5603336 | tf_op jit(solution)/shard_map/ppermute | solution.py:649
  300.3 6.9 %copy-start.1 = (bf16[32,24,2432]{2,1,0:T(8,128)(2,1)S(1)}, bf16[32,24,2432]{2,1,0:T(8,128)(2,1)}, u32[]{:S(2)}) copy-start(bf16[32,24,2432]{2,1,0:T(8,128)(2,1)} %copy-done) | copy-start | bytes 11206660
  303.6 16.5 %collective-permute-start.11 = (bf16[96,2432]{1,0:T(8,128)(2,1)S(1)}, bf16[96,2432]{1,0:T(8,128)(2,1)S(1)}, u32[]{:S(2)}, u32[]{:S(2)}) collective-permute-start(bf16[96,2432]{1,0:T(8,128)(2,1)S(1)} %get-tuple-element.82), channel_id=1, source_target_pairs={{0,8},{4,12},{8,0},{12,4},{16,24},{20,28},{24,16},{28,20},{1,9},{5... | collective-permute-start | bytes 1400840 | tf_op jit(solution)/shard_map/ppermute | solution.py:649
  303.7 16.4 %collective-permute-start.12 = (bf16[96,2432]{1,0:T(8,128)(2,1)S(1)}, bf16[96,2432]{1,0:T(8,128)(2,1)S(1)}, u32[]{:S(2)}, u32[]{:S(2)}) collective-permute-start(bf16[96,2432]{1,0:T(8,128)(2,1)S(1)} %get-tuple-element.83), channel_id=1, source_target_pairs={{0,16},{4,20},{8,24},{12,28},{16,0},{20,4},{24,8},{28,12},{1,17},{... | collective-permute-start | bytes 1400840 | tf_op jit(solution)/shard_map/ppermute | solution.py:649
  305.3 22.1 %collective-permute-start.13 = (bf16[96,2432]{1,0:T(8,128)(2,1)S(1)}, bf16[96,2432]{1,0:T(8,128)(2,1)S(1)}, u32[]{:S(2)}, u32[]{:S(2)}) collective-permute-start(bf16[96,2432]{1,0:T(8,128)(2,1)S(1)} %get-tuple-element.84), channel_id=1, source_target_pairs={{0,24},{4,28},{8,16},{12,20},{16,8},{20,12},{24,0},{28,4},{1,25},{... | collective-permute-start | bytes 1400840 | tf_op jit(solution)/shard_map/ppermute | solution.py:649
  327.7 8.9 %collective-permute-start.16 = (bf16[24,2432]{1,0:T(8,128)(2,1)S(1)}, bf16[24,2432]{1,0:T(8,128)(2,1)S(1)}, u32[]{:S(2)}, u32[]{:S(2)}) collective-permute-start(bf16[24,2432]{1,0:T(8,128)(2,1)S(1)} %get-tuple-element.116), channel_id=1, source_target_pairs={{0,3},{1,2},{2,1},{3,0},{4,7},{5,6},{6,5},{7,4},{8,11},{9,10},{10,... | collective-permute-start | bytes 350216 | tf_op jit(solution)/shard_map/ppermute | solution.py:649
  332.5 9.8 %collective-permute-start.15 = (bf16[24,2432]{1,0:T(8,128)(2,1)S(1)}, bf16[24,2432]{1,0:T(8,128)(2,1)S(1)}, u32[]{:S(2)}, u32[]{:S(2)}) collective-permute-start(bf16[24,2432]{1,0:T(8,128)(2,1)S(1)} %get-tuple-element.117), channel_id=1, source_target_pairs={{0,2},{1,3},{2,0},{3,1},{4,6},{5,7},{6,4},{7,5},{8,10},{9,11},{10,... | collective-permute-start | bytes 350216 | tf_op jit(solution)/shard_map/ppermute | solution.py:649
  332.5 9.8 %collective-permute-start.14 = (bf16[24,2432]{1,0:T(8,128)(2,1)S(1)}, bf16[24,2432]{1,0:T(8,128)(2,1)S(1)}, u32[]{:S(2)}, u32[]{:S(2)}) collective-permute-start(bf16[24,2432]{1,0:T(8,128)(2,1)S(1)} %get-tuple-element.118), channel_id=1, source_target_pairs={{0,1},{1,0},{2,3},{3,2},{4,5},{5,4},{6,7},{7,6},{8,9},{9,8},{10,11... | collective-permute-start | bytes 350216 | tf_op jit(solution)/shard_map/ppermute | solution.py:649
  333.5 1.0 copy-start.2
Sparse Core Ops, SparseCore 0:
  11.4 96.6 all-gather.1
  171.8 53.2 reduce-scatter.5
  229.0 59.6 reduce-scatter.3
  300.4 33.0 reduce-scatter.7
